TPU v7x, 32 devices: a whole 2x2x4 slice. The times are simulated.
32 devices in a mesh: row: 16 (over z, x, core), chan: 2 (over y).
Axes of the slice: x: 2, y: 2, z: 4, core: 2. Of those that a mesh axis runs over, the one named last changes fastest.
Arguments:
- sky_image: float32 [2, 4096, 4096], P('chan', 'row'), may hold values from -6 to 6
- fourier_dual: float32 [2, 2, 4096, 4096], P(None, 'chan', 'row'), may hold values from -6 to 6
- visibilities: float32 [2, 2, 4096, 4096], P(None, 'chan', 'row'), may hold values from -18 to 18
- weights: float32 [2, 4096, 4096], P('chan', 'row'), may hold values from 0.1 to 1
- radius: float32 [2], P('chan'), may hold values from 0.2 to 0.6
- wavelet_dual: float32 [2, 4096, 4096], P(None, ('row', 'chan')), may hold values from -6 to 6
- reweight: float32 [4096, 4096], P(('row', 'chan')), may hold values from 0.3 to 3
Outputs:
- image_new: float32 [2, 4096, 4096], P('chan', 'row')
- fourier_new: float32 [2, 2, 4096, 4096], P(None, 'chan', 'row')
- wavelet_new: float32 [2, 4096, 4096], P(None, ('row', 'chan'))
All inputs are finite; a program needn't handle non-finite values.
Results may differ from a plain program's by a relative error of at most 0.000084.
Values sent between devices are 32-bit elements; how exact they have to be, the bound alone decides.
No kernel may reach another device: no remote copies, remote signals or barrier semaphores. Data moves between devices by JAX's collectives and lax.ppermute only.
A program may use at most 192 MiB of HBM per device.

v0:
```python
from functools import partial
import math

import jax
import jax.numpy as jnp
from jax import lax
from jax.sharding import PartitionSpec as P

data_step = 0.8
primal_step = 0.5
low_taps = (0.0625, 0.25, 0.375, 0.25, 0.0625)
high_taps = (-0.1, -0.3, 0.7, -0.2, -0.1)
low_reverse = (0.0625, 0.25, 0.375, 0.25, 0.0625)
high_reverse = (-0.1, -0.2, 0.7, -0.3, -0.1)


def padded_2(array, sides, width):
    for axis, dim in sides:
        count, length = (lax.axis_size(axis), array.shape[dim])
        up = [(i, (i + 1) % count) for i in range(count - 1)]
        down = [(j, i) for i, j in up]
        last = lax.slice_in_dim(array, length - width, length, axis=dim)
        first = lax.slice_in_dim(array, 0, width, axis=dim)
        before = lax.ppermute(last, axis, up)
        after = lax.ppermute(first, axis, down)
        array = jnp.concatenate([before, array, after], axis=dim)
    return array


def filter_rows(extended, filter_taps):
    count_rows = extended.shape[1] - 4
    total = filter_taps[0] * extended[:, 0:count_rows]
    for offset in range(1, 5):
        total = total + filter_taps[offset] * extended[:, offset : offset + count_rows]
    return total


def filter_columns(values, filter_taps):
    count_cols = values.shape[2]
    padded = jnp.pad(values, ((0, 0), (0, 0), (2, 2)))
    total = filter_taps[0] * padded[:, :, 0:count_cols]
    for offset in range(1, 5):
        total = total + filter_taps[offset] * padded[:, :, offset : offset + count_cols]
    return total


def analysis(extended, low_set, high_set):
    return filter_columns(filter_rows(extended, high_set), low_set) + filter_columns(
        filter_rows(extended, low_set), high_set
    )


def soft_dual(combined, threshold):
    magnitude = jnp.sqrt(jnp.sum(combined * combined, axis=0))
    return combined * (threshold / jnp.maximum(magnitude, threshold))


def factor_pair(length):
    outer_count = 1
    for divisor in range(1, math.isqrt(length) + 1):
        if length % divisor == 0:
            outer_count = divisor
    return (outer_count, length // outer_count)


def phase_table(rows_count, cols_count, modulus, orient):
    products = (
        jnp.arange(rows_count, dtype=jnp.int32)[:, None]
        * jnp.arange(cols_count, dtype=jnp.int32)[None, :]
        % modulus
    )
    angle = 2.0 * math.pi / modulus * products.astype(jnp.float32)
    return (jnp.cos(angle), orient * jnp.sin(angle))


def complex_mix(form, left_re, left_im, right_re, right_im):
    product = partial(jnp.einsum, form, precision=lax.Precision.HIGHEST)
    if left_im is None:
        return (product(left_re, right_re), product(left_re, right_im))
    return (
        product(left_re, right_re) - product(left_im, right_im),
        product(left_re, right_im) + product(left_im, right_re),
    )


def transform(real_in, imag_in, orient):
    length = real_in.shape[-1]
    outer_count, inner_count = factor_pair(length)
    leading = real_in.shape[:-1]
    real_in = real_in.reshape(leading + (outer_count, inner_count))
    if imag_in is not None:
        imag_in = imag_in.reshape(leading + (outer_count, inner_count))
    outer_re, outer_im = phase_table(outer_count, outer_count, outer_count, orient)
    section_re, section_im = complex_mix("...pq,pk->...kq", real_in, imag_in, outer_re, outer_im)
    twiddle_re, twiddle_im = phase_table(outer_count, inner_count, length, orient)
    section_re, section_im = (
        section_re * twiddle_re - section_im * twiddle_im,
        section_re * twiddle_im + section_im * twiddle_re,
    )
    inner_re, inner_im = phase_table(inner_count, inner_count, inner_count, orient)
    result_re, result_im = complex_mix(
        "...kq,qj->...jk", section_re, section_im, inner_re, inner_im
    )
    norm_scale = 1.0 / math.sqrt(length)
    return (
        result_re.reshape(leading + (length,)) * norm_scale,
        result_im.reshape(leading + (length,)) * norm_scale,
    )


def per_device(sky_image, fourier_dual, visibilities, weights, radius, wavelet_dual, reweight):
    stacked = jnp.stack(transform(sky_image, None, -1.0))
    arrived = jnp.swapaxes(
        lax.all_to_all(stacked, "row", split_axis=3, concat_axis=2, tiled=True), 2, 3
    )
    freq_re, freq_im = transform(arrived[0], arrived[1], -1.0)
    resid_re = fourier_dual[0] / data_step + weights * freq_re - visibilities[0]
    resid_im = fourier_dual[1] / data_step + weights * freq_im - visibilities[1]
    partials = (
        jnp.sum(resid_re * resid_re + resid_im * resid_im, axis=(1, 2)),
        jnp.sum(visibilities[0] * visibilities[0] + visibilities[1] * visibilities[1], axis=(1, 2)),
    )
    resid_norm, data_norm = lax.psum((partials[0], partials[1]), "row")
    shrink = data_step * (1.0 - radius * jnp.sqrt(data_norm) / jnp.sqrt(resid_norm))
    new_re = resid_re * shrink[:, None, None]
    new_im = resid_im * shrink[:, None, None]
    fourier_new = jnp.stack([new_re, new_im])
    outgoing = jnp.stack(transform(weights * new_re, weights * new_im, 1.0))
    facet_image = lax.all_to_all(sky_image, "chan", split_axis=1, concat_axis=0, tiled=True)
    extended = padded_2(facet_image, ((("row", "chan"), 1),), 2)
    combined = wavelet_dual + analysis(extended, low_taps, high_taps)
    wavelet_new = soft_dual(combined, reweight)
    extended_dual = padded_2(wavelet_new, ((("row", "chan"), 1),), 2)
    adjoint = analysis(extended_dual, low_reverse, high_reverse)
    returned = jnp.swapaxes(
        lax.all_to_all(outgoing, "row", split_axis=3, concat_axis=2, tiled=True), 2, 3
    )
    gradient = transform(returned[0], returned[1], 1.0)[0]
    adjoint_rows = lax.all_to_all(adjoint, "chan", split_axis=0, concat_axis=1, tiled=True)
    image_new = jnp.maximum(sky_image - primal_step * (gradient + adjoint_rows), 0.0)
    return (image_new, fourier_new, wavelet_new)


def solution(mesh):
    in_specs = (
        P("chan", "row", None),
        P(None, "chan", "row", None),
        P(None, "chan", "row", None),
        P("chan", "row", None),
        P("chan"),
        P(None, ("row", "chan"), None),
        P(("row", "chan"), None),
    )
    out_specs = (
        P("chan", "row", None),
        P(None, "chan", "row", None),
        P(None, ("row", "chan"), None),
    )
    return jax.shard_map(
        per_device, mesh=mesh, in_specs=in_specs, out_specs=out_specs, check_vma=False
    )
```

profile of v0, /device:TPU:15, one launch (start us, length us, event | category | flops | bytes accessed | tf_op | source)
XLA Modules:
  0.0 822.6 jit_solution(10746996493191833592)
XLA Ops:
  0.6 8.5 %copy.181 = f32[1,256,4096]{2,0,1:T(1,128)} copy(f32[1,256,4096]{2,1,0:T(8,128)} %param.7) | data formatting | bytes 8388608 | tf_op args[0]
  20.7 8.8 %fusion.84 = f32[64,256,64]{1,0,2:T(8,128)S(1)} fusion(f32[256,64,64]{0,2,1:T(8,128)} %bitcast.273), kind=kOutput, calls=%fused_computation.140 | convolution fusion | flops 805367808 | bytes 8388608 | tf_op jit(solution)/shard_map/...pq,pk->...kq/dot_general | solution.py:79
  29.5 7.8 fusion.25
  37.3 6.4 fusion.78
  43.8 6.6 multiply_bitcast_fusion.6
  52.8 6.2 fusion.76
  59.0 6.6 multiply_bitcast_fusion.5
  68.8 22.8 %copy.141 = f32[2,1,256,4096]{2,1,0,3:T(1,128)} copy(f32[2,1,256,4096]{2,3,1,0:T(8,128)S(1)} %pad_maximum_fusion) | data formatting | bytes 16777216 | tf_op jit(solution)/shard_map/stack | solution.py:112
  91.5 6.8 all-to-all-start
  98.3 7.7 fusion.326
  119.4 7.7 fusion.327
  156.3 123.3 %collective-permute-done = f32[2,2,4096]{2,1,0:T(2,128)S(1)} collective-permute-done((f32[2,2,4096]{2,1,0:T(2,128)S(1)}, f32[2,2,4096]{2,1,0:T(2,128)S(1)}, u32[]{:S(2)}, u32[]{:S(2)}) %collective-permute-start) | collective-permute-done | bytes 65568 | tf_op jit(solution)/shard_map/ppermute | solution.py:24
  280.7 14.6 %multiply_add_fusion.3 = (f32[2,128,4096]{2,1,0:T(8,128)}, f32[2,128,4096]{2,1,0:T(8,128)}) fusion(f32[2,128,4096]{2,1,0:T(8,128)} %bitcast.292, f32[2,2,4096]{2,1,0:T(2,128)S(1)} %collective-permute-done, f32[2,2,4096]{2,1,0:T(2,128)S(1)} %collective-permute-done.1), kind=kLoop, calls=%fused_computation.83 | loop fusion | flops 25165824 | bytes 12713984 | tf_op jit(solution)/shard_map/add | solution.py:34
  295.4 21.4 %multiply_reduce_fusion = (f32[128,4096]{1,0:T(8,128)S(1)}, f32[2,128,4096]{2,1,0:T(8,128)}) fusion(f32[2,128,4096]{2,1,0:T(8,128)} %param.12, f32[2,128,4096]{2,1,0:T(8,128)} %get-tuple-element.39, f32[2,128,4096]{2,1,0:T(8,128)} %get-tuple-element.38), kind=kLoop, calls=%fused_computation.76 | loop fusion | flops 22544384 | bytes 18874368 | tf_op jit(solution)/shard_map/reduce_sum | solution.py:54
  336.7 10.3 %add_add_fusion = f32[2,128,4096]{2,1,0:T(8,128)} fusion(f32[2,128,4096]{2,1,0:T(8,128)S(1)} %get-tuple-element.37, f32[2,128,4096]{2,1,0:T(8,128)S(1)} %get-tuple-element.36), kind=kLoop, calls=%fused_computation.69 | loop fusion | flops 19922944 | bytes 12582912 | tf_op jit(solution)/shard_map/add | solution.py:48
  352.7 7.4 copy.142
  360.1 9.0 %copy.143 = f32[2,1,16,256,256]{4,3,2,0,1:T(8,128)} copy(f32[2,1,16,256,256]{3,4,2,0,1:T(8,128)} %bitcast.289) | data formatting | bytes 16777216 | tf_op jit(solution)/shard_map/all_to_all | solution.py:114
  373.1 6.0 fusion.70
  379.1 6.7 fusion.68
  385.8 6.4 fusion.88
  392.2 8.2 fusion.21
  400.5 6.0 fusion.60
  406.5 6.7 fusion.62
  413.2 6.2 multiply_bitcast_fusion.3
  423.8 6.5 multiply_bitcast_fusion.4
  434.8 8.8 %add_reduce_fusion = (f32[]{:T(128)}, f32[1,256,4096]{1,2,0:T(8,128)}, f32[1,256,4096]{1,2,0:T(8,128)}, f32[]{:T(128)}) fusion(f32[1,1,256,4096]{2,3,1,0:T(8,128)S(1)} %copy-done.10, f32[1,256,4096]{1,2,0:T(8,128)S(1)} %copy-done.4, f32[1,256,64,64]{1,3,2,0:T(8,128)} %copy.150, f32[1,1,256,4096]{2,3,1,0:T(8,128)S(1)} %copy-done.9, ...), kind=kLoop, calls=%fused_computation.87 | loop fusion | flops 16777214 | bytes 37748744 | tf_op jit(solution)/shard_map/reduce_sum | solution.py:120
  443.6 22.4 %all-reduce.4 = (f32[1]{0:T(128)}, f32[1]{0:T(128)}) all-reduce(f32[1]{0:T(128)} %bitcast.36, f32[1]{0:T(128)} %bitcast.43), channel_id=1, replica_groups=mesh['row'=16,'chan'=2] {'row'}, use_global_device_ids=true, to_apply=%region_1.2 | all-reduce | flops 2 | bytes 16 | tf_op jit(solution)/shard_map/psum | solution.py:123
  467.2 11.3 %multiply_bitcast_fusion.8 = (f32[1,1,256,4096]{2,3,1,0:T(8,128)}, f32[1,256,4096]{1,2,0:T(8,128)}, f32[1,256,4096]{1,2,0:T(8,128)}, f32[1,1,256,4096]{2,3,1,0:T(8,128)}) fusion(f32[1,256,4096]{1,2,0:T(8,128)} %get-tuple-element.15, f32[]{:T(128)} %bitcast.44, f32[1,256,4096]{1,2,0:T(8,128)} %copy.159, f32[1,256,4096]{1,2,0:T(8,128)} %get-tuple-element.16), kind=kLoop, calls=%fused_computation.146 | loop fusion | flops 4194304 | bytes 29360132 | tf_op jit(solution)/shard_map/stack | solution.py:127
  478.5 9.0 %fusion.54 = f32[64,256,64]{1,0,2:T(8,128)S(1)} fusion(f32[256,64,64]{0,2,1:T(8,128)} %bitcast.281), kind=kOutput, calls=%fused_computation.110 | convolution fusion | flops 805363712 | bytes 8388608 | tf_op jit(solution)/shard_map/...pq,pk->...kq/dot_general | solution.py:81
  487.5 6.3 fusion.52
  493.8 6.4 fusion.94
  500.3 8.2 fusion.12
  508.5 6.3 fusion.46
  514.8 6.2 multiply_bitcast_fusion.2
  523.4 6.5 fusion.44
  529.9 6.2 multiply_bitcast_fusion.1
  539.3 22.7 %copy.171 = f32[2,1,256,4096]{2,1,0,3:T(1,128)} copy(f32[2,1,256,4096]{2,3,1,0:T(8,128)S(1)} %pad_maximum_fusion.1) | data formatting | bytes 16777216 | tf_op jit(solution)/shard_map/stack | solution.py:128
  573.6 7.3 pad_maximum_fusion.2
  580.9 8.9 %copy.185 = f32[2,1,256,4096]{3,2,1,0:T(8,128)} copy(f32[2,1,256,4096]{2,3,1,0:T(8,128)} %pad_maximum_fusion.2) | data formatting | bytes 16777216
  589.8 160.5 %all-to-all-done.1 = f32[2,1,256,4096]{2,1,0,3:T(1,128)} async-done(((f32[2,1,256,4096]{2,1,0,3:T(1,128)}), f32[2,1,256,4096]{2,1,0,3:T(1,128)}, u32[]{:S(2)}, u32[]{:S(2)}) %all-to-all-start.1) | async-done | bytes 8388640 | tf_op jit(solution)/shard_map/all_to_all | solution.py:136
  750.3 7.3 copy.172
  757.6 8.8 %copy.173 = f32[2,1,16,256,256]{4,3,2,0,1:T(8,128)} copy(f32[2,1,16,256,256]{3,4,2,0,1:T(8,128)} %bitcast.290) | data formatting | bytes 16777216 | tf_op jit(solution)/shard_map/all_to_all | solution.py:136
  770.3 6.0 fusion.38
  776.4 6.7 fusion.36
  783.1 6.4 fusion.100
  789.5 8.2 %fusion.8 = (f32[256,64,64]{0,1,2:T(8,128)S(1)}, f32[256,64,64]{0,1,2:T(8,128)S(1)}) fusion(f32[64,256,64]{1,0,2:T(8,128)S(1)} %fusion.100, f32[64,64]{0,1:T(8,128)S(1)} %fusion.173, f32[64,64]{0,1:T(8,128)S(1)} %get-tuple-element.49, f32[64,256,64]{1,0,2:T(8,128)S(1)} %fusion.36, f32[256,64,64]{0,2,1:T(8,128)S(1)} %bitcast.278), kind=kOutput, calls=%fused_computation.26 | convolution fusion | flops 812703744 | bytes 21004288 | tf_op jit(solution)/shard_map/...pq,pk->...kq/dot_general | solution.py:82
  797.8 6.0 fusion.28
  803.8 6.4 multiply_bitcast_fusion
  (65 shorter events, 131.6 us)
Async XLA Ops:
  9.1 82.4 %all-to-all-start.2 = ((f32[1,256,4096]{2,0,1:T(1,128)}), f32[1,256,4096]{2,0,1:T(1,128)}, u32[]{:S(2)}, u32[]{:S(2)}) async-start(f32[1,256,4096]{2,0,1:T(1,128)} %copy.181), calls=%async_computation.2 | async-start | bytes 8388608 | tf_op jit(solution)/shard_map/all_to_all | solution.py:129
  20.7 8.8 %copy-start = (f32[1,256,4096]{1,2,0:T(8,128)S(1)}, f32[1,256,4096]{1,2,0:T(8,128)}, u32[]{:S(2)}) copy-start(f32[1,256,4096]{1,2,0:T(8,128)} %copy.183) | copy-start | bytes 12582916
  91.5 255.6 %all-to-all-start = ((f32[2,1,256,4096]{2,1,0,3:T(1,128)}), f32[2,1,256,4096]{2,1,0,3:T(1,128)}, u32[]{:S(2)}, u32[]{:S(2)}) async-start(f32[2,1,256,4096]{2,1,0,3:T(1,128)} %copy.141), calls=%async_computation | async-start | bytes 16777216 | tf_op jit(solution)/shard_map/all_to_all | solution.py:114
  112.1 2.0 copy-start.6
  114.1 165.5 %collective-permute-start = (f32[2,2,4096]{2,1,0:T(2,128)S(1)}, f32[2,2,4096]{2,1,0:T(2,128)S(1)}, u32[]{:S(2)}, u32[]{:S(2)}) collective-permute-start(f32[2,2,4096]{2,1,0:T(2,128)S(1)} %get-tuple-element.47), channel_id=1, source_target_pairs={{0,1},{1,2},{2,3},{3,4},{4,5},{5,6},{6,7},{7,8},{8,9},{9,10},{10,1... | collective-permute-start | bytes 196616 | tf_op jit(solution)/shard_map/ppermute | solution.py:24
  117.0 163.8 %collective-permute-start.1 = (f32[2,2,4096]{2,1,0:T(2,128)S(1)}, f32[2,2,4096]{2,1,0:T(2,128)S(1)}, u32[]{:S(2)}, u32[]{:S(2)}) collective-permute-start(f32[2,2,4096]{2,1,0:T(2,128)S(1)} %get-tuple-element.46), channel_id=1, source_target_pairs={{1,0},{2,1},{3,2},{4,3},{5,4},{6,5},{7,6},{8,7},{9,8},{10,9},{11,1... | collective-permute-start | bytes 196616 | tf_op jit(solution)/shard_map/ppermute | solution.py:25
  316.8 2.8 copy-start.8
  320.1 16.6 %copy-start.5 = (f32[2,128,4096]{2,1,0:T(8,128)}, f32[2,128,4096]{2,1,0:T(8,128)S(1)}, u32[]{:S(2)}) copy-start(f32[2,128,4096]{2,1,0:T(8,128)S(1)} %broadcast_multiply_fusion) | copy-start | bytes 12582916
  320.2 7.1 collective-permute-start.2
  325.2 7.4 collective-permute-start.3
  347.1 214.9 %all-to-all-start.3 = ((f32[2,128,4096]{2,1,0:T(8,128)}), f32[2,128,4096]{2,1,0:T(8,128)}, u32[]{:S(2)}, u32[]{:S(2)}) async-start(f32[2,128,4096]{2,1,0:T(8,128)} %add_add_fusion), calls=%async_computation.3 | async-start | bytes 8388608 | tf_op jit(solution)/shard_map/all_to_all | solution.py:139
  423.8 11.0 %copy-start.10 = (f32[1,1,256,4096]{2,3,1,0:T(8,128)S(1)}, f32[1,1,256,4096]{2,3,1,0:T(8,128)}, u32[]{:S(2)}) copy-start(f32[1,1,256,4096]{2,3,1,0:T(8,128)} %copy.189) | copy-start | bytes 12582916
  423.8 11.0 %copy-start.11 = (f32[1,1,256,4096]{2,3,1,0:T(8,128)S(1)}, f32[1,1,256,4096]{2,3,1,0:T(8,128)}, u32[]{:S(2)}) copy-start(f32[1,1,256,4096]{2,3,1,0:T(8,128)} %copy.190) | copy-start | bytes 12582916
  430.3 4.5 copy-start.4
  430.3 4.5 copy-start.9
  478.5 9.0 %copy-start.3 = (f32[1,256,4096]{1,2,0:T(8,128)S(1)}, f32[1,256,4096]{1,2,0:T(8,128)}, u32[]{:S(2)}) copy-start(f32[1,256,4096]{1,2,0:T(8,128)} %get-tuple-element.42) | copy-start | bytes 12582916
  487.5 6.3 copy-start.2
  562.0 188.3 %all-to-all-start.1 = ((f32[2,1,256,4096]{2,1,0,3:T(1,128)}), f32[2,1,256,4096]{2,1,0,3:T(1,128)}, u32[]{:S(2)}, u32[]{:S(2)}) async-start(f32[2,1,256,4096]{2,1,0,3:T(1,128)} %copy.171), calls=%async_computation.1 | async-start | bytes 16777216 | tf_op jit(solution)/shard_map/all_to_all | solution.py:136
  810.2 2.5 copy-start.1
  810.2 3.5 copy-start.7
where the time goes:
time: 831 us; the launch traced here: 823 us
  waiting for transfers between devices  290 us (35%)
  local copies, waits for them, and re-layouts  195 us (23%)
  matrix products  190 us (23%)
  other arithmetic  85.2 us (10%)
  starting transfers between devices  36.3 us (4%)
  blocking collectives  22.4 us (3%)
    all_to_all x1, waiting for transfers between devices, per_device(): lax.all_to_all(outgoing, 'row', split_axis=3, concat_axis=2, tiled=True)  161 us
    ppermute x2, waiting for transfers between devices, padded_2(): before = lax.ppermute(last, axis, up)  123 us
    unnamed x34, local copies, waits for them, and re-layouts  66.5 us
    dot_general x7, matrix products, complex_mix(): product(left_im, right_im)  46.5 us
    dot_general x7, matrix products, complex_mix(): product(left_re, right_re) - product(left_im, right_im)  44.9 us
    dot_general x6, matrix products, complex_mix(): product(left_re, right_im) + product(left_im, right_re)  43.6 us
    dot_general x6, matrix products, complex_mix(): product(left_im, right_re)  38.4 us
    another operation x1, local copies, waits for them, and re-layouts, per_device(): stacked = jnp.stack(transform(sky_image, None, -1.0))  22.8 us
  transfers between devices with their start and end apart: 8, of which 4 were waited for; matrix products, arithmetic and copies ran while one was open for 47% of the time, Pallas kernels for 0%

commit v1 on v0

v1 whole, which is shorter than its diff:
```python
import math
from functools import partial

import jax
import jax.numpy as jnp
import ml_dtypes
import numpy as np
from jax import lax
from jax.experimental import pallas as pl
from jax.experimental.pallas import tpu as pltpu
from jax.sharding import PartitionSpec as P

data_step = 0.8
primal_step = 0.5
low_taps = (0.0625, 0.25, 0.375, 0.25, 0.0625)
high_taps = (-0.1, -0.3, 0.7, -0.2, -0.1)
low_reverse = (0.0625, 0.25, 0.375, 0.25, 0.0625)
high_reverse = (-0.1, -0.2, 0.7, -0.3, -0.1)

VMEM_LIMIT = 60 * 1024 * 1024


def padded_2(array, sides, width):
    for axis, dim in sides:
        count, length = (lax.axis_size(axis), array.shape[dim])
        up = [(i, (i + 1) % count) for i in range(count - 1)]
        down = [(j, i) for i, j in up]
        last = lax.slice_in_dim(array, length - width, length, axis=dim)
        first = lax.slice_in_dim(array, 0, width, axis=dim)
        before = lax.ppermute(last, axis, up)
        after = lax.ppermute(first, axis, down)
        array = jnp.concatenate([before, array, after], axis=dim)
    return array


def filter_rows(extended, filter_taps):
    count_rows = extended.shape[1] - 4
    total = filter_taps[0] * extended[:, 0:count_rows]
    for offset in range(1, 5):
        total = total + filter_taps[offset] * extended[:, offset : offset + count_rows]
    return total


def filter_columns(values, filter_taps):
    count_cols = values.shape[2]
    padded = jnp.pad(values, ((0, 0), (0, 0), (2, 2)))
    total = filter_taps[0] * padded[:, :, 0:count_cols]
    for offset in range(1, 5):
        total = total + filter_taps[offset] * padded[:, :, offset : offset + count_cols]
    return total


def analysis(extended, low_set, high_set):
    return filter_columns(filter_rows(extended, high_set), low_set) + filter_columns(
        filter_rows(extended, low_set), high_set
    )


def soft_dual(combined, threshold):
    magnitude = jnp.sqrt(jnp.sum(combined * combined, axis=0))
    return combined * (threshold / jnp.maximum(magnitude, threshold))


def c_add(x, y):
    if x[1] is None and y[1] is None:
        return (x[0] + y[0], None)
    if x[1] is None:
        return (x[0] + y[0], y[1])
    if y[1] is None:
        return (x[0] + y[0], x[1])
    return (x[0] + y[0], x[1] + y[1])


def c_sub(x, y):
    if x[1] is None and y[1] is None:
        return (x[0] - y[0], None)
    if x[1] is None:
        return (x[0] - y[0], -y[1])
    if y[1] is None:
        return (x[0] - y[0], x[1])
    return (x[0] - y[0], x[1] - y[1])


def c_rot(x, turn):
    turn = turn % 1.0
    wr, wi = math.cos(2 * math.pi * turn), math.sin(2 * math.pi * turn)
    re, im = x
    if turn == 0.0:
        return x
    if turn == 0.5:
        return (-re, None if im is None else -im)
    if turn == 0.25:
        return (jnp.zeros_like(re) if im is None else -im, re)
    if turn == 0.75:
        return (jnp.zeros_like(re) if im is None else im, -re)
    if im is None:
        return (re * wr, re * wi)
    if abs(abs(wr) - abs(wi)) < 1e-12:
        h = abs(wr)
        p, m = (re + im) * h, (re - im) * h
        if wr > 0:
            return (m, p) if wi > 0 else (p, -m)
        return (-p, m) if wi > 0 else (-m, -p)
    return (re * wr - im * wi, re * wi + im * wr)


def c_rot90_add(x, y, sign):
    re, im = x
    yr, yi = y
    if yi is not None:
        re = re - yi if sign > 0 else re + yi
    if im is None:
        im = yr if sign > 0 else -yr
    else:
        im = im + yr if sign > 0 else im - yr
    return (re, im)


def small_dft(xs, sign):
    n = len(xs)
    if n == 1:
        return list(xs)
    if n == 2:
        return [c_add(xs[0], xs[1]), c_sub(xs[0], xs[1])]
    if n % 4 == 0:
        parts = [small_dft(xs[r::4], sign) for r in range(4)]
        out = [None] * n
        for k in range(n // 4):
            t = [c_rot(parts[r][k], sign * r * k / n) for r in range(4)]
            s0, s1 = c_add(t[0], t[2]), c_sub(t[0], t[2])
            s2, s3 = c_add(t[1], t[3]), c_sub(t[1], t[3])
            out[k] = c_add(s0, s2)
            out[k + n // 2] = c_sub(s0, s2)
            out[k + n // 4] = c_rot90_add(s1, s3, sign)
            out[k + 3 * n // 4] = c_rot90_add(s1, s3, -sign)
        return out
    even, odd = small_dft(xs[0::2], sign), small_dft(xs[1::2], sign)
    out = [None] * n
    for k in range(n // 2):
        t = c_rot(odd[k], sign * k / n)
        out[k], out[k + n // 2] = c_add(even[k], t), c_sub(even[k], t)
    return out


def split_constant(table):
    high = table.astype(ml_dtypes.bfloat16)
    low = (table - high.astype(np.float64)).astype(ml_dtypes.bfloat16)
    return high, low


def dft_matrix(rows, cols, length, sign):
    angle = 2.0 * np.pi * ((np.asarray(rows)[:, None] * np.asarray(cols)[None, :]) % length) / length
    return np.cos(angle), sign * np.sin(angle)


def phase_rows(count, positions, length, sign):
    re, im = dft_matrix(np.arange(count), positions, length, sign)
    wide = lambda t: np.ascontiguousarray(np.broadcast_to(t[:, None, :], (count, 8, t.shape[1]))).astype(np.float32)
    return wide(re), wide(im)


def split_value(value):
    high = value.astype(jnp.bfloat16)
    low = (value - high.astype(jnp.float32)).astype(jnp.bfloat16)
    return high, low


def dot_nt(a, b):
    return lax.dot_general(a, b, (((1,), (1,)), ((), ())), preferred_element_type=jnp.float32)


def dot_split(high, low, value):
    v_high, v_low = split_value(value)
    return dot_nt(high, v_high) + (dot_nt(low, v_high) + dot_nt(high, v_low))


def lane_step(width):
    return 128 if width % 128 == 0 else width


def radix_stage(load, tw_re, tw_im, store, rows, width, count, sign):
    step = lane_step(width)

    def body(i, carry):
        at = pl.ds(pl.multiple_of(i * 8, 8), 8)
        for lane in range(0, width, step):
            lanes = slice(lane, lane + step)
            ys = small_dft([load(p, at, lanes) for p in range(count)], sign)
            for p in range(count):
                re, im = ys[p]
                if p == 0:
                    store(p, at, lanes, re, jnp.zeros_like(re) if im is None else im)
                    continue
                wr, wi = tw_re[p, :, lanes], tw_im[p, :, lanes]
                if im is None:
                    store(p, at, lanes, re * wr, re * wi)
                else:
                    store(p, at, lanes, re * wr - im * wi, re * wi + im * wr)
        return carry

    lax.fori_loop(0, rows // 8, body, 0)


def lane_tiles(width):
    step = lane_step(width)
    return width // step, step


def store_rows(out, lead, p, n, count, value):
    tiles, step = lane_tiles(value.shape[1])
    room = out.shape[-1]
    for t in range(tiles):
        piece = value[:, t * step : (t + 1) * step]
        if room > step:
            piece = jnp.concatenate([piece, jnp.zeros((n, room - step), piece.dtype)], axis=1)
        at = pl.ds(p, n, stride=count) if n > 1 else pl.ds(p, 1)
        out[(*lead, t, at, slice(None))] = piece


def mix_pair(f_high, f_low, y_re, y_im, half):
    a = dot_split(f_high[...], f_low[...], y_re)
    b = dot_split(f_high[...], f_low[...], y_im)
    return a[:half] - b[half:], b[:half] + a[half:]


def first_kernel(count, width, kept, x, tw_re, tw_im, f_high, f_low, out, y_re, y_im):
    rows = x.shape[0]

    def load(p, at, lanes):
        return (x[at, p * width + lanes.start : p * width + lanes.stop], None)

    def store(p, at, lanes, re, im):
        y_re[p, at, lanes] = re
        y_im[p, at, lanes] = im

    radix_stage(load, tw_re, tw_im, store, rows, width, count, -1)

    def body(p, carry):
        z_re, z_im = mix_pair(f_high, f_low, y_re[p], y_im[p], count * kept)
        for m in range(count):
            store_rows(out, (m, 0), p, kept, count, z_re[m * kept : (m + 1) * kept])
            store_rows(out, (m, 1), p, kept, count, z_im[m * kept : (m + 1) * kept])
        return carry

    lax.fori_loop(0, count, body, 0)


def flipped(ref, at, n):
    return jnp.concatenate([ref[t, at, :].T for t in range(ref.shape[0])], axis=0)[:n]


def middle_kernel(
    count, width, got, dual, vis, weights, tw_re, tw_im, f_high, f_low, tv_re, tv_im, g_high, g_low,
    resid, out, sums, y_re, y_im, zt_re, zt_im, s_re, s_im,
):
    batch = got.shape[3]
    length = count * width
    per = width // count

    def load(p, at, lanes):
        tile = lanes.start // got.shape[4]
        return (got[p, 0, tile, at, :], got[p, 1, tile, at, :])

    def store(p, at, lanes, re, im):
        y_re[p, at, lanes] = re
        y_im[p, at, lanes] = im

    radix_stage(load, tw_re, tw_im, store, batch, width, count, -1)

    def forward(p, carry):
        z_re, z_im = mix_pair(f_high, f_low, y_re[p], y_im[p], width)
        store_rows(zt_re, (), p, width, count, z_re)
        store_rows(zt_im, (), p, width, count, z_im)
        return carry

    lax.fori_loop(0, count, forward, 0)

    def residual(i, carry):
        d_sum, v_sum = carry
        start = pl.multiple_of(i * 128, 128)
        at = pl.ds(start, 128)
        w = weights[0, :, at]
        v_re, v_im = vis[0, 0, :, at], vis[1, 0, :, at]
        d_re = dual[0, 0, :, at] * (1.0 / data_step) + w * flipped(zt_re, at, batch) - v_re
        d_im = dual[1, 0, :, at] * (1.0 / data_step) + w * flipped(zt_im, at, batch) - v_im
        resid[0, 0, :, at] = d_re
        resid[1, 0, :, at] = d_im
        s_re[:, at] = w * d_re
        s_im[:, at] = w * d_im
        fold = lambda t: jnp.sum(t.reshape(batch // 8, 8, 128), axis=0)
        return d_sum + fold(d_re * d_re + d_im * d_im), v_sum + fold(v_re * v_re + v_im * v_im)

    zero = jnp.zeros((8, 128), jnp.float32)
    d_sum, v_sum = lax.fori_loop(0, length // 128, residual, (zero, zero))
    sums[0] = d_sum
    sums[1] = v_sum

    def load_2(p, at, lanes):
        lanes = slice(p * width + lanes.start, p * width + lanes.stop)
        return (s_re[at, lanes], s_im[at, lanes])

    radix_stage(load_2, tv_re, tv_im, store, batch, width, count, 1)

    def inverse(p, carry):
        u_re, u_im = mix_pair(g_high, g_low, y_re[p], y_im[p], width)
        for m in range(count):
            store_rows(out, (m, 0), p, per, count, u_re[m * per : (m + 1) * per])
            store_rows(out, (m, 1), p, per, count, u_im[m * per : (m + 1) * per])
        return carry

    lax.fori_loop(0, count, inverse, 0)


def last_kernel(count, width, final, has_part, *refs):
    refs = list(refs)
    got, tw_re, tw_im, e_high, e_low = refs[:5]
    refs = refs[5:]
    part = refs.pop(0) if has_part else None
    if final:
        sky, adjoint, shrink, out, y_re, y_im, gt = refs
    else:
        out, y_re, y_im = refs
    rows, batch = got.shape[3], got.shape[2] * got.shape[4]
    length = count * width

    def load(p, at, lanes):
        tile = lanes.start // got.shape[4]
        return (got[p, 0, tile, at, :], got[p, 1, tile, at, :])

    def store(p, at, lanes, re, im):
        y_re[p, at, lanes] = re
        y_im[p, at, lanes] = im

    radix_stage(load, tw_re, tw_im, store, rows, batch, count, 1)

    def inverse(p, carry):
        u = dot_split(e_high[...], e_low[...], jnp.concatenate([y_re[p], y_im[p]], axis=1))
        if has_part:
            u = u + part[p]
        if final:
            store_rows(gt, (), p, width, count, u)
        else:
            out[p] = u
        return carry

    lax.fori_loop(0, count, inverse, 0)
    if final:
        scale = primal_step * shrink[0]

        def finish(i, carry):
            at = pl.ds(pl.multiple_of(i * 128, 128), 128)
            value = sky[:, at] - (scale * flipped(gt, at, rows) + primal_step * adjoint[:, at])
            out[:, at] = jnp.maximum(value, 0.0)
            return carry

        lax.fori_loop(0, length // 128, finish, 0)


def vmem(shape, dtype=jnp.float32):
    return pltpu.VMEM(shape, dtype)


def whole(shape):
    return pl.BlockSpec(shape, lambda *_: (0,) * len(shape), pipeline_mode=pl.Buffered(1))


def call(kernel, args, specs, out_shape, out_specs, scratch, name, flops, moved):
    return pl.pallas_call(
        kernel,
        grid=(1,),
        in_specs=specs,
        out_specs=out_specs,
        out_shape=out_shape,
        scratch_shapes=scratch,
        name=name,
        cost_estimate=pl.CostEstimate(flops=flops, bytes_accessed=moved, transcendentals=0),
        compiler_params=pltpu.CompilerParams(vmem_limit_bytes=VMEM_LIMIT),
    )(*args)


def per_device(sky_image, fourier_dual, visibilities, weights, radius, wavelet_dual, reweight):
    f32 = jnp.float32
    sky = sky_image[0]
    rows, length = sky.shape
    count = lax.axis_size("row")
    width = length // count
    per = width // count
    chunks = 2 if per % 2 == 0 else 1
    batch = width // chunks
    kept = per // chunks
    scale = 1.0 / math.sqrt(length)
    shape = jax.ShapeDtypeStruct

    def tile(high, wide):
        tiles, step = lane_tiles(wide)
        return tiles, high, step

    lanes = np.arange(width)
    tw = phase_rows(count, lanes, length, -1)
    tv = phase_rows(count, lanes, length, 1)
    f_table = split_constant(scale * np.concatenate(dft_matrix(lanes, lanes, width, -1)))
    g_table = split_constant(scale * np.concatenate(dft_matrix(lanes, lanes, width, 1)))

    sent = []
    for c in range(chunks):
        picked = (np.arange(count)[:, None] * per + c * kept + np.arange(kept)[None, :]).reshape(-1)
        table = split_constant(scale * np.concatenate(dft_matrix(picked, lanes, width, -1)))
        args = (sky, *tw, *table)
        piece = call(
            partial(first_kernel, count, width, kept), args, [whole(a.shape) for a in args],
            shape((count, 2, *tile(batch, rows)), f32), whole((count, 2, *tile(batch, rows))),
            [vmem((count, rows, width))] * 2, "first", 10**10, 10**7,
        )
        sent.append(lax.all_to_all(piece, "row", split_axis=0, concat_axis=0, tiled=True))

    facet_image = lax.all_to_all(sky_image, "chan", split_axis=1, concat_axis=0, tiled=True)
    extended = padded_2(facet_image, ((("row", "chan"), 1),), 2)
    combined = wavelet_dual + analysis(extended, low_taps, high_taps)
    wavelet_new = soft_dual(combined, reweight)
    extended_dual = padded_2(wavelet_new, ((("row", "chan"), 1),), 2)
    adjoint = analysis(extended_dual, low_reverse, high_reverse)
    adjoint_rows = lax.all_to_all(adjoint, "chan", split_axis=0, concat_axis=1, tiled=True)

    resid, returned, sums = [], [], 0.0
    for c in range(chunks):
        block = lambda lead, c=c: pl.BlockSpec(
            (*lead, batch, length), lambda i: (0,) * len(lead) + (c, 0), pipeline_mode=pl.Buffered(1)
        )
        tables = (*tw, *f_table, *tv, *g_table)
        outs = (
            shape((2, 1, batch, length), f32),
            shape((count, 2, *tile(rows, batch)), f32),
            shape((2, 8, 128), f32),
        )
        d, piece, part = call(
            partial(middle_kernel, count, width), (sent[c], fourier_dual, visibilities, weights, *tables),
            [whole(sent[c].shape), block((2, 1)), block((2, 1)), block((1,)), *(whole(t.shape) for t in tables)],
            outs, tuple(whole(o.shape) for o in outs),
            [vmem((count, batch, width))] * 2 + [vmem((-(-batch // 128), length, 128))] * 2 + [vmem((batch, length))] * 2,
            "middle", 2 * 10**10, 3 * 10**7,
        )
        resid.append(d)
        sums = sums + part
        returned.append(lax.all_to_all(piece, "row", split_axis=0, concat_axis=0, tiled=True))

    spread = jnp.broadcast_to(sums[None], (count, *sums.shape))
    gathered = lax.all_to_all(spread, "row", split_axis=0, concat_axis=0, tiled=True)
    resid_norm = jnp.sum(gathered[:, 0])
    data_norm = jnp.sum(gathered[:, 1])
    shrink = data_step * (1.0 - radius * jnp.sqrt(data_norm) / jnp.sqrt(resid_norm))
    fourier_new = jnp.concatenate([d * shrink for d in resid], axis=2)

    partial_sum = None
    for c in range(chunks):
        q = c * batch + np.arange(batch)
        phases = phase_rows(count, q, length, 1)
        e_re, e_im = dft_matrix(lanes, q, width, 1)
        table = split_constant(scale * np.concatenate([e_re, -e_im], axis=1))
        final = c == chunks - 1
        args = [returned[c], *phases, *table]
        if partial_sum is not None:
            args.append(partial_sum)
        specs = [whole(a.shape) for a in args]
        scratch = [vmem((count, rows, batch))] * 2
        if final:
            args += [sky, adjoint_rows[0], shrink]
            specs += [whole(sky.shape), whole(sky.shape), pl.BlockSpec(memory_space=pltpu.SMEM)]
            scratch.append(vmem((-(-rows // 128), length, 128)))
            out = shape((rows, length), f32)
        else:
            out = shape((count, width, rows), f32)
        partial_sum = call(
            partial(last_kernel, count, width, final, partial_sum is not None), args, specs,
            out, whole(out.shape), scratch, "last", 10**10, 10**7,
        )
    return (partial_sum[None], fourier_new, wavelet_new)


def solution(mesh):
    in_specs = (
        P("chan", "row", None),
        P(None, "chan", "row", None),
        P(None, "chan", "row", None),
        P("chan", "row", None),
        P("chan"),
        P(None, ("row", "chan"), None),
        P(("row", "chan"), None),
    )
    out_specs = (
        P("chan", "row", None),
        P(None, "chan", "row", None),
        P(None, ("row", "chan"), None),
    )
    return jax.shard_map(
        per_device, mesh=mesh, in_specs=in_specs, out_specs=out_specs, check_vma=False
    )
```

time: 831 us -> 579 us (0.70)
  matrix products: 190 us -> 0 us
  local copies, waits for them, and re-layouts: 195 us -> 17 us
  Pallas kernels: 0 us -> 132 us
  blocking collectives: 22.4 us -> 109 us
  waiting for transfers between devices: 290 us -> 213 us
  other arithmetic: 85.2 us -> 63 us
    dot_general x28 -> x0, matrix products: 190 us -> none  [the longest x7 46.5 us: complex_mix(): product(left_im, right_im)]
    pallas_call x0 -> x6, Pallas kernels: none -> 132 us  [call(): pl.pallas_call(kernel, grid=(1,), in_specs=specs, out_specs=out_specs, ou...]
    all_to_all x0 -> x2, blocking collectives: none -> 109 us  [the longest x1 99.5 us: per_device(): lax.all_to_all(piece, 'row', split_axis=0, concat_axis=0, tiled=True)]
    ppermute x2, waiting for transfers between devices: 123 us -> 45 us  [padded_2(): before = lax.ppermute(last, axis, up)]
    unnamed x34 -> x10, local copies, waits for them, and re-layouts: 66.5 us -> 16.9 us
    another operation x2 -> x0, local copies, waits for them, and re-layouts: 45.5 us -> none  [the longest x1 22.8 us: per_device(): stacked = jnp.stack(transform(sky_image, None, -1.0))]
    all_to_all x5 -> x0, local copies, waits for them, and re-layouts: 38.1 us -> none  [the longest x2 16.4 us: per_device(): lax.all_to_all(stacked, 'row', split_axis=3, concat_axis=2, tiled=True)]
    all_to_all x1, waiting for transfers between devices: 0.01 us -> 31 us  [per_device(): lax.all_to_all(sky_image, 'chan', split_axis=1, concat_axis=0, tiled=True)]
  transfers between devices with their start and end apart: 8 -> 9, of which waited for: 4 -> 5; matrix products, arithmetic and copies ran while one was open for 47% -> 12% of each run, Pallas kernels for 0% -> 19%
where the time goes in v1:
time: 579 us; the launch traced here: 578 us
  waiting for transfers between devices  213 us (37%)
  Pallas kernels  132 us (23%)
  blocking collectives  109 us (19%)
  other arithmetic  63 us (11%)
  starting transfers between devices  41.4 us (7%)
  local copies, waits for them, and re-layouts  17 us (3%)
    all_to_all x3, waiting for transfers between devices, per_device(): lax.all_to_all(piece, 'row', split_axis=0, concat_axis=0, tiled=True)  134 us
    pallas_call x6, Pallas kernels, call(): pl.pallas_call(kernel, grid=(1,), in_specs=specs, out_specs=out_specs, ou...  132 us
    all_to_all x1, blocking collectives, per_device(): lax.all_to_all(piece, 'row', split_axis=0, concat_axis=0, tiled=True)  99.5 us
    ppermute x2, waiting for transfers between devices, padded_2(): before = lax.ppermute(last, axis, up)  45 us
    all_to_all x1, waiting for transfers between devices, per_device(): lax.all_to_all(sky_image, 'chan', split_axis=1, concat_axis=0, tiled=True)  31 us
    reduce_sum x1, other arithmetic, soft_dual(): magnitude = jnp.sqrt(jnp.sum(combined * combined, axis=0))  21.6 us
    add x2, other arithmetic, filter_rows(): total + filter_taps[offset] * extended[:, offset:offset + count_rows]  18.7 us
    all_to_all x3, starting transfers between devices, per_device(): lax.all_to_all(piece, 'row', split_axis=0, concat_axis=0, tiled=True)  17 us
  transfers between devices with their start and end apart: 9, of which 5 were waited for; matrix products, arithmetic and copies ran while one was open for 12% of the time, Pallas kernels for 19%

profile of v1, /device:TPU:15, one launch (start us, length us, event | category | flops | bytes accessed | tf_op | source)
XLA Modules:
  0.0 578.0 jit_solution(4677144043038952236)
XLA Ops:
  0.6 8.5 %copy.32 = f32[1,256,4096]{2,0,1:T(1,128)} copy(f32[1,256,4096]{2,1,0:T(8,128)} %param.27) | data formatting | bytes 8388608 | tf_op args[0]
  9.1 5.8 %all-to-all-start.4 = ((f32[1,256,4096]{2,0,1:T(1,128)}), f32[1,256,4096]{2,0,1:T(1,128)}, u32[]{:S(2)}, u32[]{:S(2)}) async-start(f32[1,256,4096]{2,0,1:T(1,128)} %copy.32), calls=%async_computation.4 | async-start | bytes 8388608 | tf_op jit(solution)/shard_map/all_to_all | solution.py:416
  15.0 14.6 %first.3 = f32[16,2,2,128,128]{4,3,2,1,0:T(8,128)} custom-call(f32[256,4096]{1,0:T(8,128)} %bitcast.9, f32[16,8,256]{2,1,0:T(8,128)} %constant.60.clone.tw_re.tv_re, f32[16,8,256]{2,1,0:T(8,128)} %constant.61.clone.tw_im, bf16[256,256]{1,0:T(8,128)(2,1)} %constant.62.clone.f_high, bf16[256,256]{1,0:T(8,128)(2,1)} %constant.63.clone.f_low), custom_call_target="tpu_custom_call" | custom-call | flops 10000000000 | bytes 10000000 | tf_op jit(solution)/shard_map/first/pallas_call | solution.py:368
  29.6 31.0 %all-to-all-done.4 = f32[1,256,4096]{2,0,1:T(1,128)} async-done(((f32[1,256,4096]{2,0,1:T(1,128)}), f32[1,256,4096]{2,0,1:T(1,128)}, u32[]{:S(2)}, u32[]{:S(2)}) %all-to-all-start.4) | async-done | bytes 4194336 | tf_op jit(solution)/shard_map/all_to_all | solution.py:416
  60.6 7.1 %all-to-all-start.2 = ((f32[16,2,2,128,128]{4,3,2,1,0:T(8,128)}), f32[16,2,2,128,128]{4,3,2,1,0:T(8,128)}, u32[]{:S(2)}, u32[]{:S(2)}) async-start(f32[16,2,2,128,128]{4,3,2,1,0:T(8,128)} %first.3), calls=%async_computation.2 | async-start | bytes 8388608 | tf_op jit(solution)/shard_map/all_to_all | solution.py:414
  67.7 6.0 %copy.33 = f32[1,256,4096]{2,1,0:T(8,128)S(1)} copy(f32[1,256,4096]{2,0,1:T(1,128)} %all-to-all-done.4) | data formatting | bytes 8388608
  73.7 0.0 copy-start.1
  73.7 2.0 copy-done.1
  75.8 4.5 collective-permute-start
  80.3 1.9 collective-permute-start.1
  82.2 14.6 %first.2 = f32[16,2,2,128,128]{4,3,2,1,0:T(8,128)} custom-call(f32[256,4096]{1,0:T(8,128)} %bitcast.10, f32[16,8,256]{2,1,0:T(8,128)} %constant.60.clone.tw_re.tv_re, f32[16,8,256]{2,1,0:T(8,128)} %constant.61.clone.tw_im, bf16[256,256]{1,0:T(8,128)(2,1)} %constant.64.clone.f_high, bf16[256,256]{1,0:T(8,128)(2,1)} %constant.65.clone.f_low), custom_call_target="tpu_custom_call" | custom-call | flops 10000000000 | bytes 10000000 | tf_op jit(solution)/shard_map/first/pallas_call | solution.py:368
  96.9 63.3 %all-to-all-done.2.got = f32[16,2,2,128,128]{4,3,2,1,0:T(8,128)} async-done(((f32[16,2,2,128,128]{4,3,2,1,0:T(8,128)}), f32[16,2,2,128,128]{4,3,2,1,0:T(8,128)}, u32[]{:S(2)}, u32[]{:S(2)}) %all-to-all-start.2) | async-done | bytes 4194336 | tf_op jit(solution)/shard_map/all_to_all | solution.py:414
  160.2 5.0 all-to-all-start
  165.2 0.0 collective-permute-done
  165.2 0.0 collective-permute-done.1
  165.2 14.8 %multiply_add_fusion.3 = (f32[2,128,4096]{2,1,0:T(8,128)}, f32[2,128,4096]{2,1,0:T(8,128)}) fusion(f32[2,128,4096]{2,1,0:T(8,128)} %bitcast.8, f32[2,2,4096]{2,1,0:T(2,128)S(1)} %collective-permute-done, f32[2,2,4096]{2,1,0:T(2,128)S(1)} %collective-permute-done.1), kind=kLoop, calls=%fused_computation.31 | loop fusion | flops 25165824 | bytes 12713984 | tf_op jit(solution)/shard_map/add | solution.py:40
  180.0 21.6 %multiply_reduce_fusion = (f32[128,4096]{1,0:T(8,128)S(1)}, f32[2,128,4096]{2,1,0:T(8,128)}) fusion(f32[2,128,4096]{2,1,0:T(8,128)} %param.32, f32[2,128,4096]{2,1,0:T(8,128)} %get-tuple-element.22, f32[2,128,4096]{2,1,0:T(8,128)} %get-tuple-element.21), kind=kLoop, calls=%fused_computation.24 | loop fusion | flops 22544384 | bytes 18874368 | tf_op jit(solution)/shard_map/reduce_sum | solution.py:60
  201.6 0.0 copy-start.2
  201.6 2.5 maximum_divide_fusion
  204.0 0.4 copy-done.2
  204.4 0.5 broadcast_multiply_fusion.2
  204.9 0.0 copy-start
  205.0 4.4 collective-permute-start.2
  209.4 2.1 collective-permute-start.3
  211.6 45.0 %collective-permute-done.2 = f32[2,2,4096]{2,1,0:T(2,128)S(1)} collective-permute-done((f32[2,2,4096]{2,1,0:T(2,128)S(1)}, f32[2,2,4096]{2,1,0:T(2,128)S(1)}, u32[]{:S(2)}, u32[]{:S(2)}) %collective-permute-start.2) | collective-permute-done | bytes 65568 | tf_op jit(solution)/shard_map/ppermute | solution.py:30
  256.6 2.6 collective-permute-done.3
  259.2 3.9 multiply_add_fusion.1
  263.1 0.0 copy-done
  263.1 10.2 %add_add_fusion = f32[2,128,4096]{2,1,0:T(8,128)} fusion(f32[2,128,4096]{2,1,0:T(8,128)S(1)} %get-tuple-element.20, f32[2,128,4096]{2,1,0:T(8,128)S(1)} %get-tuple-element.19), kind=kLoop, calls=%fused_computation.17 | loop fusion | flops 19922944 | bytes 12582912 | tf_op jit(solution)/shard_map/add | solution.py:54
  273.4 0.0 all-to-all-done.got
  273.4 5.6 all-to-all-start.5
  279.0 35.9 %middle.3 = (f32[2,1,128,4096]{3,2,1,0:T(8,128)}, f32[16,2,1,256,128]{4,3,2,1,0:T(8,128)}, f32[2,8,128]{2,1,0:T(8,128)}) custom-call(f32[16,2,2,128,128]{4,3,2,1,0:T(8,128)} %all-to-all-done.2.got, f32[2,1,256,4096]{3,2,1,0:T(8,128)} %dual.3, f32[2,1,256,4096]{3,2,1,0:T(8,128)} %vis.3, f32[1,256,4096]{2,1,0:T(8,128)} %weights.3, ...), custom_call_target="tpu_custom_call" | custom-call | flops 20000000000 | bytes 30000000 | tf_op jit(solution)/shard_map/middle/pallas_call | solution.py:368
  314.9 0.0 copy-start.3
  314.9 36.0 %middle.2 = (f32[2,1,128,4096]{3,2,1,0:T(8,128)}, f32[16,2,1,256,128]{4,3,2,1,0:T(8,128)}, f32[2,8,128]{2,1,0:T(8,128)}) custom-call(f32[16,2,2,128,128]{4,3,2,1,0:T(8,128)} %all-to-all-done.got, f32[2,1,256,4096]{3,2,1,0:T(8,128)} %dual.3, f32[2,1,256,4096]{3,2,1,0:T(8,128)} %vis.3, f32[1,256,4096]{2,1,0:T(8,128)} %weights.3, ...), custom_call_target="tpu_custom_call" | custom-call | flops 20000000000 | bytes 30000000 | tf_op jit(solution)/shard_map/middle/pallas_call | solution.py:368
  350.9 0.0 copy-done.3
  350.9 0.7 add.151
  351.6 0.0 all-to-all-done.5
  351.6 9.9 %all_to_all.46 = f32[16,2,8,128]{3,2,1,0:T(8,128)S(1)} all-to-all(f32[16,2,8,128]{3,2,1,0:T(8,128)S(1)} %broadcast_in_dim.4), channel_id=1, replica_groups=mesh['row'=16,'chan'=2] {'row'}, dimensions={0} | all-to-all | bytes 262144 | tf_op jit(solution)/shard_map/all_to_all | solution.py:447
  361.4 99.5 %all_to_all.47.refs_0_ = f32[16,2,1,256,128]{4,3,2,1,0:T(8,128)} all-to-all(f32[16,2,1,256,128]{4,3,2,1,0:T(8,128)} %get-tuple-element.10), channel_id=1, replica_groups=mesh['row'=16,'chan'=2] {'row'}, dimensions={0} | all-to-all | bytes 8388608 | tf_op jit(solution)/shard_map/all_to_all | solution.py:444
  460.9 4.9 all-to-all-start.1
  466.5 0.7 slice_reduce_fusion
  468.6 4.1 broadcast_multiply_fusion
  472.7 3.9 pad_maximum_fusion
  476.6 10.6 %last.2.refs_5_ = f32[16,256,256]{2,1,0:T(8,128)} custom-call(f32[16,2,1,256,128]{4,3,2,1,0:T(8,128)} %all_to_all.47.refs_0_, f32[16,8,128]{2,1,0:T(8,128)} %constant.71.clone.refs_1_, f32[16,8,128]{2,1,0:T(8,128)} %constant.72.clone.refs_2_, bf16[256,256]{1,0:T(8,128)(2,1)} %constant.73.clone.refs_3_, bf16[256,256]{1,0:T(8,128)(2,1)} %constant.74.clone.refs_4_), custom_call_target="tpu_custom_call" | custom-call | flops 10000000000 | bytes 10000000 | tf_op jit(solution)/shard_map/last/pallas_call | solution.py:368
  487.2 71.1 %all-to-all-done.1.refs_0_ = f32[16,2,1,256,128]{4,3,2,1,0:T(8,128)} async-done(((f32[16,2,1,256,128]{4,3,2,1,0:T(8,128)}), f32[16,2,1,256,128]{4,3,2,1,0:T(8,128)}, u32[]{:S(2)}, u32[]{:S(2)}) %all-to-all-start.1) | async-done | bytes 4194336 | tf_op jit(solution)/shard_map/all_to_all | solution.py:444
  558.3 19.7 %last.3 = f32[256,4096]{1,0:T(8,128)} custom-call(f32[16,2,1,256,128]{4,3,2,1,0:T(8,128)} %all-to-all-done.1.refs_0_, f32[16,8,128]{2,1,0:T(8,128)} %constant.75.clone.refs_1_, f32[16,8,128]{2,1,0:T(8,128)} %constant.76.clone.refs_2_, bf16[256,256]{1,0:T(8,128)(2,1)} %constant.77.clone.refs_3_, bf16[256,256]{1,0:T(8,128)(2,1)} %constant.78.clone.refs_4_, ...), custom_call_target="tpu_custom_call" | custom-call | flops 10000000000 | bytes 10000000 | tf_op jit(solution)/shard_map/last/pallas_call | solution.py:368
  (3 shorter events, 0.1 us)
Async XLA Ops:
  9.1 51.5 %all-to-all-start.4 = ((f32[1,256,4096]{2,0,1:T(1,128)}), f32[1,256,4096]{2,0,1:T(1,128)}, u32[]{:S(2)}, u32[]{:S(2)}) async-start(f32[1,256,4096]{2,0,1:T(1,128)} %copy.32), calls=%async_computation.4 | async-start | bytes 8388608 | tf_op jit(solution)/shard_map/all_to_all | solution.py:416
  60.6 99.6 %all-to-all-start.2 = ((f32[16,2,2,128,128]{4,3,2,1,0:T(8,128)}), f32[16,2,2,128,128]{4,3,2,1,0:T(8,128)}, u32[]{:S(2)}, u32[]{:S(2)}) async-start(f32[16,2,2,128,128]{4,3,2,1,0:T(8,128)} %first.3), calls=%async_computation.2 | async-start | bytes 8388608 | tf_op jit(solution)/shard_map/all_to_all | solution.py:414
  73.7 2.0 copy-start.1
  75.8 89.4 %collective-permute-start = (f32[2,2,4096]{2,1,0:T(2,128)S(1)}, f32[2,2,4096]{2,1,0:T(2,128)S(1)}, u32[]{:S(2)}, u32[]{:S(2)}) collective-permute-start(f32[2,2,4096]{2,1,0:T(2,128)S(1)} %get-tuple-element.26), channel_id=1, source_target_pairs={{0,1},{1,2},{2,3},{3,4},{4,5},{5,6},{6,7},{7,8},{8,9},{9,10},{10,1... | collective-permute-start | bytes 196616 | tf_op jit(solution)/shard_map/ppermute | solution.py:30
  80.3 84.9 %collective-permute-start.1 = (f32[2,2,4096]{2,1,0:T(2,128)S(1)}, f32[2,2,4096]{2,1,0:T(2,128)S(1)}, u32[]{:S(2)}, u32[]{:S(2)}) collective-permute-start(f32[2,2,4096]{2,1,0:T(2,128)S(1)} %get-tuple-element.25), channel_id=1, source_target_pairs={{1,0},{2,1},{3,2},{4,3},{5,4},{6,5},{7,6},{8,7},{9,8},{10,9},{11,1... | collective-permute-start | bytes 196616 | tf_op jit(solution)/shard_map/ppermute | solution.py:31
  160.2 113.2 %all-to-all-start = ((f32[16,2,2,128,128]{4,3,2,1,0:T(8,128)}), f32[16,2,2,128,128]{4,3,2,1,0:T(8,128)}, u32[]{:S(2)}, u32[]{:S(2)}) async-start(f32[16,2,2,128,128]{4,3,2,1,0:T(8,128)} %first.2), calls=%async_computation | async-start | bytes 8388608 | tf_op jit(solution)/shard_map/all_to_all | solution.py:414
  201.6 2.8 copy-start.2
  204.9 58.2 %copy-start = (f32[2,128,4096]{2,1,0:T(8,128)}, f32[2,128,4096]{2,1,0:T(8,128)S(1)}, u32[]{:S(2)}) copy-start(f32[2,128,4096]{2,1,0:T(8,128)S(1)} %broadcast_multiply_fusion.2) | copy-start | bytes 12582916
  205.0 51.6 %collective-permute-start.2 = (f32[2,2,4096]{2,1,0:T(2,128)S(1)}, f32[2,2,4096]{2,1,0:T(2,128)S(1)}, u32[]{:S(2)}, u32[]{:S(2)}) collective-permute-start(f32[2,2,4096]{2,1,0:T(2,128)S(1)} %get-tuple-element.24), channel_id=1, source_target_pairs={{0,1},{1,2},{2,3},{3,4},{4,5},{5,6},{6,7},{7,8},{8,9},{9,10},{10,1... | collective-permute-start | bytes 196616 | tf_op jit(solution)/shard_map/ppermute | solution.py:30
  209.4 49.8 %collective-permute-start.3 = (f32[2,2,4096]{2,1,0:T(2,128)S(1)}, f32[2,2,4096]{2,1,0:T(2,128)S(1)}, u32[]{:S(2)}, u32[]{:S(2)}) collective-permute-start(f32[2,2,4096]{2,1,0:T(2,128)S(1)} %get-tuple-element.23), channel_id=1, source_target_pairs={{1,0},{2,1},{3,2},{4,3},{5,4},{6,5},{7,6},{8,7},{9,8},{10,9},{11,1... | collective-permute-start | bytes 196616 | tf_op jit(solution)/shard_map/ppermute | solution.py:31
  273.4 78.2 %all-to-all-start.5 = ((f32[2,128,4096]{2,1,0:T(8,128)}), f32[2,128,4096]{2,1,0:T(8,128)}, u32[]{:S(2)}, u32[]{:S(2)}) async-start(f32[2,128,4096]{2,1,0:T(8,128)} %add_add_fusion), calls=%async_computation.5 | async-start | bytes 8388608 | tf_op jit(solution)/shard_map/all_to_all | solution.py:422
  314.9 36.0 %copy-start.3 = (f32[2,8,128]{2,1,0:T(8,128)S(1)}, f32[2,8,128]{2,1,0:T(8,128)}, u32[]{:S(2)}) copy-start(f32[2,8,128]{2,1,0:T(8,128)} %get-tuple-element.11) | copy-start | bytes 24580
  460.9 97.4 %all-to-all-start.1 = ((f32[16,2,1,256,128]{4,3,2,1,0:T(8,128)}), f32[16,2,1,256,128]{4,3,2,1,0:T(8,128)}, u32[]{:S(2)}, u32[]{:S(2)}) async-start(f32[16,2,1,256,128]{4,3,2,1,0:T(8,128)} %get-tuple-element.9), calls=%async_computation.1 | async-start | bytes 8388608 | tf_op jit(solution)/shard_map/all_to_all | solution.py:444

commit v2 on v1

--- a/solution.py
+++ b/solution.py
@@ -10,6 +10,7 @@
 from jax.experimental.pallas import tpu as pltpu
 from jax.sharding import PartitionSpec as P
 
+
 data_step = 0.8
 primal_step = 0.5
 low_taps = (0.0625, 0.25, 0.375, 0.25, 0.0625)
@@ -18,47 +19,6 @@
 high_reverse = (-0.1, -0.2, 0.7, -0.3, -0.1)
 
 VMEM_LIMIT = 60 * 1024 * 1024
-
-
-def padded_2(array, sides, width):
-    for axis, dim in sides:
-        count, length = (lax.axis_size(axis), array.shape[dim])
-        up = [(i, (i + 1) % count) for i in range(count - 1)]
-        down = [(j, i) for i, j in up]
-        last = lax.slice_in_dim(array, length - width, length, axis=dim)
-        first = lax.slice_in_dim(array, 0, width, axis=dim)
-        before = lax.ppermute(last, axis, up)
-        after = lax.ppermute(first, axis, down)
-        array = jnp.concatenate([before, array, after], axis=dim)
-    return array
-
-
-def filter_rows(extended, filter_taps):
-    count_rows = extended.shape[1] - 4
-    total = filter_taps[0] * extended[:, 0:count_rows]
-    for offset in range(1, 5):
-        total = total + filter_taps[offset] * extended[:, offset : offset + count_rows]
-    return total
-
-
-def filter_columns(values, filter_taps):
-    count_cols = values.shape[2]
-    padded = jnp.pad(values, ((0, 0), (0, 0), (2, 2)))
-    total = filter_taps[0] * padded[:, :, 0:count_cols]
-    for offset in range(1, 5):
-        total = total + filter_taps[offset] * padded[:, :, offset : offset + count_cols]
-    return total
-
-
-def analysis(extended, low_set, high_set):
-    return filter_columns(filter_rows(extended, high_set), low_set) + filter_columns(
-        filter_rows(extended, low_set), high_set
-    )
-
-
-def soft_dual(combined, threshold):
-    magnitude = jnp.sqrt(jnp.sum(combined * combined, axis=0))
-    return combined * (threshold / jnp.maximum(magnitude, threshold))
 
 
 def c_add(x, y):
@@ -250,7 +210,7 @@
 
 
 def middle_kernel(
-    count, width, got, dual, vis, weights, tw_re, tw_im, f_high, f_low, tv_re, tv_im, g_high, g_low,
+    count, width, rows, got, dual, vis, weights, before, tw_re, tw_im, f_high, f_low, tv_re, tv_im, g_high, g_low,
     resid, out, sums, y_re, y_im, zt_re, zt_im, s_re, s_im,
 ):
     batch = got.shape[3]
@@ -290,10 +250,14 @@
         fold = lambda t: jnp.sum(t.reshape(batch // 8, 8, 128), axis=0)
         return d_sum + fold(d_re * d_re + d_im * d_im), v_sum + fold(v_re * v_re + v_im * v_im)
 
-    zero = jnp.zeros((8, 128), jnp.float32)
-    d_sum, v_sum = lax.fori_loop(0, length // 128, residual, (zero, zero))
+    d_sum, v_sum = lax.fori_loop(0, length // 128, residual, (before[0], before[1]))
     sums[0] = d_sum
     sums[1] = v_sum
+    if out.shape[3] > rows:
+        step = out.shape[4]
+        for m in range(count):
+            for i, total in enumerate((d_sum, v_sum)):
+                out[m, i, 0, rows:, :] = sum(total[:, at : at + step] for at in range(0, 128, step))
 
     def load_2(p, at, lanes):
         lanes = slice(p * width + lanes.start, p * width + lanes.stop)
@@ -311,17 +275,8 @@
     lax.fori_loop(0, count, inverse, 0)
 
 
-def last_kernel(count, width, final, has_part, *refs):
-    refs = list(refs)
-    got, tw_re, tw_im, e_high, e_low = refs[:5]
-    refs = refs[5:]
-    part = refs.pop(0) if has_part else None
-    if final:
-        sky, adjoint, shrink, out, y_re, y_im, gt = refs
-    else:
-        out, y_re, y_im = refs
+def part_kernel(count, got, tw_re, tw_im, e_high, e_low, out, y_re, y_im):
     rows, batch = got.shape[3], got.shape[2] * got.shape[4]
-    length = count * width
 
     def load(p, at, lanes):
         tile = lanes.start // got.shape[4]
@@ -334,26 +289,103 @@
     radix_stage(load, tw_re, tw_im, store, rows, batch, count, 1)
 
     def inverse(p, carry):
+        out[p] = dot_split(e_high[...], e_low[...], jnp.concatenate([y_re[p], y_im[p]], axis=1))
+        return carry
+
+    lax.fori_loop(0, count, inverse, 0)
+
+
+def last_kernel(count, width, rows, chunks, *refs):
+    refs = list(refs)
+    take = lambda n: [refs.pop(0) for _ in range(n)]
+    (got_hbm,) = take(1)
+    parts_hbm = take(chunks - 1)
+    sky_hbm, own_hbm, other_hbm = take(3)
+    resid_hbm = take(chunks)
+    tw_re, tw_im, e_high, e_low, radius = take(5)
+    out, fourier_hbm = take(2)
+    got, part, sky, adjoint, resid, y_re, y_im, gt, sem = take(9)
+    batch = got.shape[2] * got.shape[4]
+    length = count * width
+    half = rows // 2
+    me = lax.axis_index("chan")
+    copies = []
+
+    def fetch(source, target):
+        copy = pltpu.make_async_copy(source, target, sem.at[len(copies)])
+        copies.append(copy)
+        copy.start()
+        return copy
+
+    fetch_got = fetch(got_hbm, got)
+    fetch_resid = [fetch(resid_hbm[c].at[:, 0], resid.at[c]) for c in range(chunks)]
+    fetch_part = [fetch(p, part.at[i]) for i, p in enumerate(parts_hbm)]
+    fetch_rest = [
+        fetch(sky_hbm, sky),
+        fetch(own_hbm, adjoint.at[pl.ds(pl.multiple_of(half * me, 8), half)]),
+        fetch(other_hbm, adjoint.at[pl.ds(pl.multiple_of(half * (1 - me), 8), half)]),
+    ]
+    fetch_got.wait()
+    totals = []
+    for i in range(2):
+        total = got[0, i, 0, rows:, :]
+        for m in range(1, count):
+            total = total + got[m, i, 0, rows:, :]
+        totals.append(jnp.sum(total, keepdims=True))
+    resid_norm, data_norm = totals
+    shrink = data_step * (1.0 - radius[0] * jnp.sqrt(data_norm) / jnp.sqrt(resid_norm))
+
+    def load(p, at, lanes):
+        tile = lanes.start // got.shape[4]
+        return (got[p, 0, tile, at, :], got[p, 1, tile, at, :])
+
+    def store(p, at, lanes, re, im):
+        y_re[p, at, lanes] = re
+        y_im[p, at, lanes] = im
+
+    radix_stage(load, tw_re, tw_im, store, rows, batch, count, 1)
+
+    stores = []
+    for c in range(chunks):
+        fetch_resid[c].wait()
+        per_chunk = resid.shape[2]
+        for i in range(2):
+
+            def scaled(j, carry, c=c, i=i):
+                at = pl.ds(pl.multiple_of(j * 8, 8), 8)
+                resid[c, i, at, :] = resid[c, i, at, :] * shrink
+                return carry
+
+            lax.fori_loop(0, per_chunk // 8, scaled, 0)
+            copy = pltpu.make_async_copy(
+                resid.at[c, i], fourier_hbm.at[i, 0, pl.ds(c * per_chunk, per_chunk)], sem.at[len(copies) + len(stores)]
+            )
+            copy.start()
+            stores.append(copy)
+    for copy in fetch_part:
+        copy.wait()
+
+    def inverse(p, carry):
         u = dot_split(e_high[...], e_low[...], jnp.concatenate([y_re[p], y_im[p]], axis=1))
-        if has_part:
-            u = u + part[p]
-        if final:
-            store_rows(gt, (), p, width, count, u)
-        else:
-            out[p] = u
+        for i in range(chunks - 1):
+            u = u + part[i, p]
+        store_rows(gt, (), p, width, count, u)
         return carry
 
     lax.fori_loop(0, count, inverse, 0)
-    if final:
-        scale = primal_step * shrink[0]
-
-        def finish(i, carry):
-            at = pl.ds(pl.multiple_of(i * 128, 128), 128)
-            value = sky[:, at] - (scale * flipped(gt, at, rows) + primal_step * adjoint[:, at])
-            out[:, at] = jnp.maximum(value, 0.0)
-            return carry
-
-        lax.fori_loop(0, length // 128, finish, 0)
+    for copy in fetch_rest:
+        copy.wait()
+    scale = primal_step * shrink
+
+    def finish(i, carry):
+        at = pl.ds(pl.multiple_of(i * 128, 128), 128)
+        value = sky[:, at] - (scale * flipped(gt, at, rows) + primal_step * adjoint[:, at])
+        out[:, at] = jnp.maximum(value, 0.0)
+        return carry
+
+    lax.fori_loop(0, length // 128, finish, 0)
+    for copy in stores:
+        copy.wait()
 
 
 def vmem(shape, dtype=jnp.float32):
@@ -364,7 +396,7 @@
     return pl.BlockSpec(shape, lambda *_: (0,) * len(shape), pipeline_mode=pl.Buffered(1))
 
 
-def call(kernel, args, specs, out_shape, out_specs, scratch, name, flops, moved):
+def call(kernel, args, specs, out_shape, out_specs, scratch, flops, moved):
     return pl.pallas_call(
         kernel,
         grid=(1,),
@@ -372,10 +404,108 @@
         out_specs=out_specs,
         out_shape=out_shape,
         scratch_shapes=scratch,
-        name=name,
         cost_estimate=pl.CostEstimate(flops=flops, bytes_accessed=moved, transcendentals=0),
         compiler_params=pltpu.CompilerParams(vmem_limit_bytes=VMEM_LIMIT),
     )(*args)
+
+
+def wave_kernel(
+    count, sky, other, edge_own, edge_other, dual, above, below, limit,
+    wave, own_out, other_out, x, w, sem,
+):
+    me = lax.axis_index("chan")
+    row = lax.axis_index("row")
+    half, width = limit.shape
+    base = pl.multiple_of(8 * (1 - me), 8)
+    copies = [
+        pltpu.make_async_copy(
+            sky.at[pl.ds(pl.multiple_of((half - 8) * me, 8), half + 8)], x.at[0, pl.ds(base, half + 8)], sem.at[0]
+        ),
+        pltpu.make_async_copy(other, x.at[1, pl.ds(base, half + 8)], sem.at[1]),
+    ]
+    edge = pl.ds(pl.multiple_of((half + 8) * me, 8), 8)
+    copies.append(pltpu.make_async_copy(edge_own, x.at[0, edge], sem.at[2]))
+    copies.append(pltpu.make_async_copy(edge_other, x.at[1, edge], sem.at[3]))
+    for copy in copies:
+        copy.start()
+    for copy in copies:
+        copy.wait()
+
+    def analysis(source, start, n, low, high):
+        if isinstance(start, int):
+            taps = [source[start + p : start + p + n, :] for p in range(5)]
+        else:
+            window = source[pl.ds(pl.multiple_of(start - 6, 8), n + 16), :]
+            taps = [window[6 + p : 6 + p + n] for p in range(5)]
+        a = sum(high[p] * taps[p] for p in range(1, 5)) + high[0] * taps[0]
+        b = sum(low[p] * taps[p] for p in range(1, 5)) + low[0] * taps[0]
+        total = low[2] * a + high[2] * b
+        pad = jnp.zeros((n, 128), jnp.float32)
+        for p in (0, 1, 3, 4):
+            mixed = jnp.concatenate([low[p] * a + high[p] * b, pad], axis=1)
+            total = total + pltpu.roll(mixed, (2 - p) % (width + 128), 1)[:, :width]
+        return total
+
+    def shrunk(start, n, dual_own, dual_other, bound):
+        s_own = dual_own + analysis(x.at[0], start - 2, n, low_taps, high_taps)
+        s_other = dual_other + analysis(x.at[1], start - 2, n, low_taps, high_taps)
+        factor = bound / jnp.maximum(jnp.sqrt(s_own * s_own + s_other * s_other), bound)
+        return s_own * factor, s_other * factor
+
+    first = jnp.logical_and(row == 0, me == 0)
+    last = jnp.logical_and(row == count - 1, me == 1)
+    for ref, start, out_side in ((above, 6, first), (below, half + 8, last)):
+        a, b = shrunk(start, 2, ref[me], ref[1 - me], ref[2])
+        w[0, pl.ds(start, 2), :] = jnp.where(out_side, 0.0, a)
+        w[1, pl.ds(start, 2), :] = jnp.where(out_side, 0.0, b)
+
+    def body(i, carry):
+        at = pl.ds(pl.multiple_of(i * 8, 8), 8)
+        a, b = shrunk(i * 8 + 8, 8, dual[me, at, :], dual[1 - me, at, :], limit[at, :])
+        wave[me, at, :] = a
+        wave[1 - me, at, :] = b
+        inner = pl.ds(pl.multiple_of(i * 8 + 8, 8), 8)
+        w[0, inner, :] = a
+        w[1, inner, :] = b
+        return carry
+
+    lax.fori_loop(0, half // 8, body, 0)
+
+    def back(i, carry):
+        at = pl.ds(pl.multiple_of(i * 8, 8), 8)
+        own_out[at, :] = analysis(w.at[0], i * 8 + 6, 8, low_reverse, high_reverse)
+        other_out[at, :] = analysis(w.at[1], i * 8 + 6, 8, low_reverse, high_reverse)
+        return carry
+
+    lax.fori_loop(0, half // 8, back, 0)
+
+
+def chan_swap(value):
+    size = lax.axis_size("chan")
+    return lax.ppermute(value, "chan", [(i, (i + 1) % size) for i in range(size)])
+
+
+def edges_of(sky):
+    count, size = lax.axis_size("row"), lax.axis_size("chan")
+    top, bottom = sky[:8], sky[-8:]
+    me = lax.axis_index("chan")
+    at = lambda r, c: r * size + c
+    own = [(at(r, 0), at(r + 1, 0)) for r in range(count - 1)] + [(at(r + 1, 1), at(r, 1)) for r in range(count - 1)]
+    cross = [(at(r, 1), at(r + 1, 0)) for r in range(count - 1)] + [(at(r + 1, 0), at(r, 1)) for r in range(count - 1)]
+    sent_own = jnp.where(me == 0, bottom, top)
+    sent_cross = jnp.where(me == 0, top, bottom)
+    axes = ("row", "chan")
+    return lax.ppermute(sent_own, axes, own), lax.ppermute(sent_cross, axes, cross)
+
+
+def facet_neighbours(wavelet_dual, reweight):
+    axes = ("row", "chan")
+    count = lax.axis_size(axes)
+    up = [(i, i + 1) for i in range(count - 1)]
+    down = [(j, i) for i, j in up]
+    last = jnp.concatenate([wavelet_dual[:, -2:], reweight[None, -2:]])
+    first = jnp.concatenate([wavelet_dual[:, :2], reweight[None, :2]])
+    return lax.ppermute(last, axes, up), lax.ppermute(first, axes, down)
 
 
 def per_device(sky_image, fourier_dual, visibilities, weights, radius, wavelet_dual, reweight):
@@ -409,19 +539,27 @@
         piece = call(
             partial(first_kernel, count, width, kept), args, [whole(a.shape) for a in args],
             shape((count, 2, *tile(batch, rows)), f32), whole((count, 2, *tile(batch, rows))),
-            [vmem((count, rows, width))] * 2, "first", 10**10, 10**7,
+            [vmem((count, rows, width))] * 2, 10**10, 10**7,
         )
         sent.append(lax.all_to_all(piece, "row", split_axis=0, concat_axis=0, tiled=True))
 
-    facet_image = lax.all_to_all(sky_image, "chan", split_axis=1, concat_axis=0, tiled=True)
-    extended = padded_2(facet_image, ((("row", "chan"), 1),), 2)
-    combined = wavelet_dual + analysis(extended, low_taps, high_taps)
-    wavelet_new = soft_dual(combined, reweight)
-    extended_dual = padded_2(wavelet_new, ((("row", "chan"), 1),), 2)
-    adjoint = analysis(extended_dual, low_reverse, high_reverse)
-    adjoint_rows = lax.all_to_all(adjoint, "chan", split_axis=0, concat_axis=1, tiled=True)
-
-    resid, returned, sums = [], [], 0.0
+    half = rows // 2
+    me = lax.axis_index("chan")
+    theirs = lax.dynamic_slice_in_dim(sky, (1 - me) * (half - 8), half + 8, 0)
+    other = chan_swap(theirs)
+    edge_own, edge_other = edges_of(sky)
+    above, below = facet_neighbours(wavelet_dual, reweight)
+    any_space = pl.BlockSpec(memory_space=pl.ANY)
+    args = (sky, other, edge_own, edge_other, wavelet_dual, above, below, reweight)
+    outs = (shape((2, half, length), f32), shape((half, length), f32), shape((half, length), f32))
+    wavelet_new, adjoint_own, adjoint_other = call(
+        partial(wave_kernel, count), args, [any_space] * 4 + [whole(a.shape) for a in args[4:]],
+        outs, tuple(whole(o.shape) for o in outs),
+        [vmem((2, half + 16, length))] * 2 + [pltpu.SemaphoreType.DMA((4,))], 10**10, 3 * 10**7,
+    )
+    adjoint_got = chan_swap(adjoint_other)
+
+    resid, returned, sums = [], [], np.zeros((2, 8, 128), np.float32)
     for c in range(chunks):
         block = lambda lead, c=c: pl.BlockSpec(
             (*lead, batch, length), lambda i: (0,) * len(lead) + (c, 0), pipeline_mode=pl.Buffered(1)
@@ -429,51 +567,52 @@
         tables = (*tw, *f_table, *tv, *g_table)
         outs = (
             shape((2, 1, batch, length), f32),
-            shape((count, 2, *tile(rows, batch)), f32),
+            shape((count, 2, *tile(rows + (8 if c == chunks - 1 else 0), batch)), f32),
             shape((2, 8, 128), f32),
         )
         d, piece, part = call(
-            partial(middle_kernel, count, width), (sent[c], fourier_dual, visibilities, weights, *tables),
-            [whole(sent[c].shape), block((2, 1)), block((2, 1)), block((1,)), *(whole(t.shape) for t in tables)],
+            partial(middle_kernel, count, width, rows),
+            (sent[c], fourier_dual, visibilities, weights, sums, *tables),
+            [whole(sent[c].shape), block((2, 1)), block((2, 1)), block((1,)), *(whole(t.shape) for t in (sums, *tables))],
             outs, tuple(whole(o.shape) for o in outs),
             [vmem((count, batch, width))] * 2 + [vmem((-(-batch // 128), length, 128))] * 2 + [vmem((batch, length))] * 2,
-            "middle", 2 * 10**10, 3 * 10**7,
+            2 * 10**10, 3 * 10**7,
         )
         resid.append(d)
-        sums = sums + part
+        sums = part
         returned.append(lax.all_to_all(piece, "row", split_axis=0, concat_axis=0, tiled=True))
 
-    spread = jnp.broadcast_to(sums[None], (count, *sums.shape))
-    gathered = lax.all_to_all(spread, "row", split_axis=0, concat_axis=0, tiled=True)
-    resid_norm = jnp.sum(gathered[:, 0])
-    data_norm = jnp.sum(gathered[:, 1])
-    shrink = data_step * (1.0 - radius * jnp.sqrt(data_norm) / jnp.sqrt(resid_norm))
-    fourier_new = jnp.concatenate([d * shrink for d in resid], axis=2)
-
-    partial_sum = None
+    parts = []
     for c in range(chunks):
         q = c * batch + np.arange(batch)
         phases = phase_rows(count, q, length, 1)
         e_re, e_im = dft_matrix(lanes, q, width, 1)
         table = split_constant(scale * np.concatenate([e_re, -e_im], axis=1))
-        final = c == chunks - 1
-        args = [returned[c], *phases, *table]
-        if partial_sum is not None:
-            args.append(partial_sum)
-        specs = [whole(a.shape) for a in args]
         scratch = [vmem((count, rows, batch))] * 2
-        if final:
-            args += [sky, adjoint_rows[0], shrink]
-            specs += [whole(sky.shape), whole(sky.shape), pl.BlockSpec(memory_space=pltpu.SMEM)]
-            scratch.append(vmem((-(-rows // 128), length, 128)))
-            out = shape((rows, length), f32)
-        else:
+        if c < chunks - 1:
+            args = (returned[c], *phases, *table)
             out = shape((count, width, rows), f32)
-        partial_sum = call(
-            partial(last_kernel, count, width, final, partial_sum is not None), args, specs,
-            out, whole(out.shape), scratch, "last", 10**10, 10**7,
+            parts.append(
+                call(
+                    partial(part_kernel, count), args, [whole(a.shape) for a in args],
+                    out, whole(out.shape), scratch, 10**10, 10**7,
+                )
+            )
+            continue
+        args = (returned[c], *parts, sky, adjoint_own, adjoint_got, *resid, *phases, *table, radius)
+        specs = [any_space] * (4 + len(parts) + len(resid)) + [whole(a.shape) for a in (*phases, *table)]
+        specs.append(pl.BlockSpec(memory_space=pltpu.SMEM))
+        outs = (shape((rows, length), f32), shape((2, 1, width, length), f32))
+        scratch = [
+            vmem(returned[c].shape), vmem((max(1, chunks - 1), count, width, rows)), vmem((rows, length)),
+            vmem((rows, length)), vmem((chunks, 2, batch, length)), *scratch,
+            vmem((-(-rows // 128), length, 128)), pltpu.SemaphoreType.DMA((4 * chunks + 3,)),
+        ]
+        image_new, fourier_new = call(
+            partial(last_kernel, count, width, rows, chunks), args, specs,
+            outs, (whole(outs[0].shape), any_space), scratch, 10**10, 3 * 10**7,
         )
-    return (partial_sum[None], fourier_new, wavelet_new)
+    return (image_new[None], fourier_new, wavelet_new)
 
 
 def solution(mesh):
@@ -491,6 +630,5 @@
         P(None, "chan", "row", None),
         P(None, ("row", "chan"), None),
     )
-    return jax.shard_map(
-        per_device, mesh=mesh, in_specs=in_specs, out_specs=out_specs, check_vma=False
-    )
+
+    return jax.shard_map(per_device, mesh=mesh, in_specs=in_specs, out_specs=out_specs, check_vma=False)

time: 579 us -> 502 us (0.87)
  blocking collectives: 109 us -> 0 us
  waiting for transfers between devices: 213 us -> 283 us
  other arithmetic: 63 us -> 1.09 us
  Pallas kernels: 132 us -> 172 us
  local copies, waits for them, and re-layouts: 17 us -> 6.47 us
  starting transfers between devices: 41.4 us -> 35.4 us
    all_to_all x2 -> x0, blocking collectives: 109 us -> none  [the longest x1 99.5 us: per_device(): lax.all_to_all(piece, 'row', split_axis=0, concat_axis=0, tiled=True)]
    all_to_all x3 -> x4, waiting for transfers between devices: 134 us -> 191 us  [per_device(): lax.all_to_all(piece, 'row', split_axis=0, concat_axis=0, tiled=True)]
    ppermute x4 -> x6, waiting for transfers between devices: 47.6 us -> 91.9 us  [the longest x2 78.1 us: facet_neighbours(): return (lax.ppermute(last, axes, up), lax.ppermute(first, axes, down))]
    pallas_call x6 -> x7, Pallas kernels: 132 us -> 172 us  [call(): pl.pallas_call(kernel, grid=(1,), in_specs=specs, out_specs=out_specs, ou...]
    all_to_all x2 -> x0, waiting for transfers between devices: 31 us -> none  [the longest x1 31 us: per_device(): lax.all_to_all(sky_image, 'chan', split_axis=1, concat_axis=0, tiled=True)]
    add x4 -> x0, other arithmetic: 29.7 us -> none  [the longest x2 18.7 us: filter_rows(): total + filter_taps[offset] * extended[:, offset:offset + count_rows]]
    reduce_sum x2 -> x0, other arithmetic: 22.3 us -> none  [the longest x1 21.6 us: soft_dual(): magnitude = jnp.sqrt(jnp.sum(combined * combined, axis=0))]
    unnamed x10, local copies, waits for them, and re-layouts: 16.9 us -> 2.01 us
  transfers between devices with their start and end apart: 9 -> 10, of which waited for: 5 -> 6; matrix products, arithmetic and copies ran while one was open for 12% -> 1% of each run, Pallas kernels for 19% -> 27%
where the time goes in v2:
time: 502 us; the launch traced here: 500 us
  waiting for transfers between devices  283 us (56%)
  Pallas kernels  172 us (34%)
  starting transfers between devices  35.4 us (7%)
  local copies, waits for them, and re-layouts  6.47 us (1%)
    all_to_all x4, waiting for transfers between devices, per_device(): lax.all_to_all(piece, 'row', split_axis=0, concat_axis=0, tiled=True)  191 us
    pallas_call x7, Pallas kernels, call(): pl.pallas_call(kernel, grid=(1,), in_specs=specs, out_specs=out_specs, ou...  172 us
    ppermute x2, waiting for transfers between devices, facet_neighbours(): return (lax.ppermute(last, axes, up), lax.ppermute(first, axes, down))  78.1 us
    all_to_all x4, starting transfers between devices, per_device(): lax.all_to_all(piece, 'row', split_axis=0, concat_axis=0, tiled=True)  20.9 us
    ppermute x2, waiting for transfers between devices, chan_swap(): lax.ppermute(value, 'chan', [(i, (i + 1) % size) for i in range(size)])  13.8 us
  transfers between devices with their start and end apart: 10, of which 6 were waited for; matrix products, arithmetic and copies ran while one was open for 1% of the time, Pallas kernels for 27%

profile of v2, /device:TPU:15, one launch (start us, length us, event | category | flops | bytes accessed | tf_op | source)
XLA Modules:
  0.0 499.8 jit_solution(6993557310097747203)
XLA Ops:
  0.6 14.6 %shard_map.284 = f32[16,2,2,128,128]{4,3,2,1,0:T(8,128)} custom-call(f32[256,4096]{1,0:T(8,128)} %bitcast.12, f32[16,8,256]{2,1,0:T(8,128)} %constant.53.clone.tw_re.tv_re, f32[16,8,256]{2,1,0:T(8,128)} %constant.54.clone.tw_im, bf16[256,256]{1,0:T(8,128)(2,1)} %constant.55.clone.f_high, bf16[256,256]{1,0:T(8,128)(2,1)} %constant.56.clone.f_low), custom_call_target="tpu_custom_call" | custom-call | flops 10000000000 | bytes 10000000 | tf_op jit(solution)/shard_map/pallas_call | solution.py:400
  15.3 6.5 %all-to-all-start.1 = ((f32[16,2,2,128,128]{4,3,2,1,0:T(8,128)}), f32[16,2,2,128,128]{4,3,2,1,0:T(8,128)}, u32[]{:S(2)}, u32[]{:S(2)}) async-start(f32[16,2,2,128,128]{4,3,2,1,0:T(8,128)} %shard_map.284), calls=%async_computation.1 | async-start | bytes 8388608 | tf_op jit(solution)/shard_map/all_to_all | solution.py:544
  21.8 14.6 %shard_map.283 = f32[16,2,2,128,128]{4,3,2,1,0:T(8,128)} custom-call(f32[256,4096]{1,0:T(8,128)} %bitcast.13, f32[16,8,256]{2,1,0:T(8,128)} %constant.53.clone.tw_re.tv_re, f32[16,8,256]{2,1,0:T(8,128)} %constant.54.clone.tw_im, bf16[256,256]{1,0:T(8,128)(2,1)} %constant.57.clone.f_high, bf16[256,256]{1,0:T(8,128)(2,1)} %constant.58.clone.f_low), custom_call_target="tpu_custom_call" | custom-call | flops 10000000000 | bytes 10000000 | tf_op jit(solution)/shard_map/pallas_call | solution.py:400
  36.4 77.8 %all-to-all-done.1.got = f32[16,2,2,128,128]{4,3,2,1,0:T(8,128)} async-done(((f32[16,2,2,128,128]{4,3,2,1,0:T(8,128)}), f32[16,2,2,128,128]{4,3,2,1,0:T(8,128)}, u32[]{:S(2)}, u32[]{:S(2)}) %all-to-all-start.1) | async-done | bytes 4194336 | tf_op jit(solution)/shard_map/all_to_all | solution.py:544
  114.3 4.8 all-to-all-start
  119.0 0.6 jit_solution_.3.before
  119.6 35.6 %shard_map.285 = (f32[2,1,128,4096]{3,2,1,0:T(8,128)}, f32[16,2,1,256,128]{4,3,2,1,0:T(8,128)}, f32[2,8,128]{2,1,0:T(8,128)}) custom-call(f32[16,2,2,128,128]{4,3,2,1,0:T(8,128)} %all-to-all-done.1.got, f32[2,1,256,4096]{3,2,1,0:T(8,128)} %dual.4, f32[2,1,256,4096]{3,2,1,0:T(8,128)} %vis.3, f32[1,256,4096]{2,1,0:T(8,128)} %weights.3, ...), custom_call_target="tpu_custom_call" | custom-call | flops 20000000000 | bytes 30000000 | tf_op jit(solution)/shard_map/pallas_call | solution.py:400
  155.2 56.3 %all-to-all-done.got = f32[16,2,2,128,128]{4,3,2,1,0:T(8,128)} async-done(((f32[16,2,2,128,128]{4,3,2,1,0:T(8,128)}), f32[16,2,2,128,128]{4,3,2,1,0:T(8,128)}, u32[]{:S(2)}, u32[]{:S(2)}) %all-to-all-start) | async-done | bytes 4194336 | tf_op jit(solution)/shard_map/all_to_all | solution.py:544
  211.5 4.8 all-to-all-start.3
  216.3 35.1 %shard_map.286 = (f32[2,1,128,4096]{3,2,1,0:T(8,128)}, f32[16,2,1,264,128]{4,3,2,1,0:T(8,128)}, f32[2,8,128]{2,1,0:T(8,128)}) custom-call(f32[16,2,2,128,128]{4,3,2,1,0:T(8,128)} %all-to-all-done.got, f32[2,1,256,4096]{3,2,1,0:T(8,128)} %dual.4, f32[2,1,256,4096]{3,2,1,0:T(8,128)} %vis.3, f32[1,256,4096]{2,1,0:T(8,128)} %weights.3, ...), custom_call_target="tpu_custom_call" | custom-call | flops 20000000000 | bytes 30000000 | tf_op jit(solution)/shard_map/pallas_call | solution.py:400
  251.3 57.4 %all-to-all-done.3.got = f32[16,2,1,256,128]{4,3,2,1,0:T(8,128)} async-done(((f32[16,2,1,256,128]{4,3,2,1,0:T(8,128)}), f32[16,2,1,256,128]{4,3,2,1,0:T(8,128)}, u32[]{:S(2)}, u32[]{:S(2)}) %all-to-all-start.3) | async-done | bytes 4194336 | tf_op jit(solution)/shard_map/all_to_all | solution.py:583
  308.7 4.8 all-to-all-start.2
  313.5 1.8 dynamic-slice_bitcast_fusion
  315.3 0.3 collective-permute-start
  315.6 1.1 fusion
  316.7 1.0 slice_bitcast_fusion
  317.7 4.6 collective-permute-start.3
  322.4 1.0 select_bitcast_fusion
  323.4 2.4 collective-permute-start.2
  325.8 1.9 collective-permute-start.1
  327.8 5.2 %collective-permute-start.4 = (f32[3,2,4096]{2,1,0:T(2,128)S(1)}, f32[3,2,4096]{2,1,0:T(2,128)S(1)}, u32[]{:S(2)}, u32[]{:S(2)}) collective-permute-start(f32[3,2,4096]{2,1,0:T(2,128)S(1)} %pad_maximum_fusion.1), channel_id=1, source_target_pairs={{1,0},{2,1},{3,2},{4,3},{5,4},{6,5},{7,6},{8,7},{9,8},{10,9},{11,1... | collective-permute-start | bytes 294920 | tf_op jit(solution)/shard_map/ppermute | solution.py:508
  333.0 75.0 %collective-permute-done.3.above = f32[3,2,4096]{2,1,0:T(2,128)S(1)} collective-permute-done((f32[3,2,4096]{2,1,0:T(2,128)S(1)}, f32[3,2,4096]{2,1,0:T(2,128)S(1)}, u32[]{:S(2)}, u32[]{:S(2)}) %collective-permute-start.3) | collective-permute-done | bytes 98336 | tf_op jit(solution)/shard_map/ppermute | solution.py:508
  408.0 0.0 copy-start.3
  408.0 3.1 collective-permute-done.4.below
  411.1 0.0 copy-start.4
  411.1 0.0 collective-permute-done.2.edge_other
  411.1 0.0 copy-start.1
  411.1 0.0 collective-permute-done.1.edge_own
  411.1 0.0 copy-start.2
  411.1 0.0 collective-permute-done.other
  411.1 0.0 copy-done.3
  411.1 0.6 copy-done.4
  411.7 0.1 copy-done.1
  411.8 0.1 copy-done.2
  411.8 39.9 %shard_map.288 = (f32[2,128,4096]{2,1,0:T(8,128)}, f32[128,4096]{1,0:T(8,128)}, f32[128,4096]{1,0:T(8,128)}) custom-call(f32[256,4096]{1,0:T(8,128)} %bitcast.14, f32[136,4096]{1,0:T(8,128)} %collective-permute-done.other, f32[8,4096]{1,0:T(8,128)} %copy-done.2, f32[8,4096]{1,0:T(8,128)} %copy-done.1, f32[2,128,4096]{2,1,0:T(8,128)} %dual.5, ...), custom_call_target="tpu_custom_call" | custom-call | flops 10000000000 | bytes 30000000 | tf_op jit(solution)/shard_map/pallas_call | solution.py:400
  451.7 0.1 collective-permute-start.5
  452.4 10.6 %shard_map.287.refs_1_ = f32[16,256,256]{2,1,0:T(8,128)} custom-call(f32[16,2,1,256,128]{4,3,2,1,0:T(8,128)} %all-to-all-done.3.got, f32[16,8,128]{2,1,0:T(8,128)} %constant.65.clone.tw_re, f32[16,8,128]{2,1,0:T(8,128)} %constant.66.clone.tw_im, bf16[256,256]{1,0:T(8,128)(2,1)} %constant.67.clone.e_high, bf16[256,256]{1,0:T(8,128)(2,1)} %constant.68.clone.e_low), custom_call_target="tpu_custom_call" | custom-call | flops 10000000000 | bytes 10000000 | tf_op jit(solution)/shard_map/pallas_call | solution.py:400
  463.1 13.8 %collective-permute-done.5.refs_4_ = f32[128,4096]{1,0:T(8,128)S(1)} collective-permute-done((f32[128,4096]{1,0:T(8,128)}, f32[128,4096]{1,0:T(8,128)S(1)}, u32[]{:S(2)}, u32[]{:S(2)}) %collective-permute-start.5) | collective-permute-done | bytes 2097184 | tf_op jit(solution)/shard_map/ppermute | solution.py:485
  476.9 0.0 copy-start
  476.9 0.0 all-to-all-done.2.refs_0_
  476.9 1.3 copy-done
  478.2 21.6 %shard_map.289 = (f32[256,4096]{1,0:T(8,128)}, f32[2,1,256,4096]{3,2,1,0:T(8,128)}) custom-call(f32[16,2,1,264,128]{4,3,2,1,0:T(8,128)} %all-to-all-done.2.refs_0_, f32[16,256,256]{2,1,0:T(8,128)} %shard_map.287.refs_1_, f32[256,4096]{1,0:T(8,128)} %bitcast.15, f32[128,4096]{1,0:T(8,128)} %get-tuple-element.16.refs_3_, f32[128,4096]{1,0:T(8,128)} %copy-done, ...), custom_call_target="tpu_custom_call" | custom-call | flops 10000000000 | bytes 30000000 | tf_op jit(solution)/shard_map/pallas_call | solution.py:400
  (2 shorter events, 0.1 us)
Async XLA Ops:
  15.3 99.0 %all-to-all-start.1 = ((f32[16,2,2,128,128]{4,3,2,1,0:T(8,128)}), f32[16,2,2,128,128]{4,3,2,1,0:T(8,128)}, u32[]{:S(2)}, u32[]{:S(2)}) async-start(f32[16,2,2,128,128]{4,3,2,1,0:T(8,128)} %shard_map.284), calls=%async_computation.1 | async-start | bytes 8388608 | tf_op jit(solution)/shard_map/all_to_all | solution.py:544
  114.3 97.2 %all-to-all-start = ((f32[16,2,2,128,128]{4,3,2,1,0:T(8,128)}), f32[16,2,2,128,128]{4,3,2,1,0:T(8,128)}, u32[]{:S(2)}, u32[]{:S(2)}) async-start(f32[16,2,2,128,128]{4,3,2,1,0:T(8,128)} %shard_map.283), calls=%async_computation | async-start | bytes 8388608 | tf_op jit(solution)/shard_map/all_to_all | solution.py:544
  211.5 97.2 %all-to-all-start.3 = ((f32[16,2,1,256,128]{4,3,2,1,0:T(8,128)}), f32[16,2,1,256,128]{4,3,2,1,0:T(8,128)}, u32[]{:S(2)}, u32[]{:S(2)}) async-start(f32[16,2,1,256,128]{4,3,2,1,0:T(8,128)} %get-tuple-element.15), calls=%async_computation.3 | async-start | bytes 8388608 | tf_op jit(solution)/shard_map/all_to_all | solution.py:583
  308.7 168.1 %all-to-all-start.2 = ((f32[16,2,1,264,128]{4,3,2,1,0:T(8,128)}), f32[16,2,1,264,128]{4,3,2,1,0:T(8,128)}, u32[]{:S(2)}, u32[]{:S(2)}) async-start(f32[16,2,1,264,128]{4,3,2,1,0:T(8,128)} %get-tuple-element.14), calls=%async_computation.2 | async-start | bytes 8650752 | tf_op jit(solution)/shard_map/all_to_all | solution.py:583
  315.3 95.8 %collective-permute-start = (f32[136,4096]{1,0:T(8,128)S(1)}, f32[136,4096]{1,0:T(8,128)}, u32[]{:S(2)}, u32[]{:S(2)}) collective-permute-start(f32[136,4096]{1,0:T(8,128)S(1)} %dynamic-slice_bitcast_fusion), channel_id=1, source_target_pairs={{0,1},{1,0},{2,3},{3,2},{4,5},{5,4},{6,7},{7,6},{8,9},{9,8},{10,11... | collective-permute-start | bytes 6684680 | tf_op jit(solution)/shard_map/ppermute | solution.py:485
  317.7 90.3 %collective-permute-start.3 = (f32[3,2,4096]{2,1,0:T(2,128)S(1)}, f32[3,2,4096]{2,1,0:T(2,128)S(1)}, u32[]{:S(2)}, u32[]{:S(2)}) collective-permute-start(f32[3,2,4096]{2,1,0:T(2,128)S(1)} %pad_maximum_fusion), channel_id=1, source_target_pairs={{0,1},{1,2},{2,3},{3,4},{4,5},{5,6},{6,7},{7,8},{8,9},{9,10},{10,1... | collective-permute-start | bytes 294920 | tf_op jit(solution)/shard_map/ppermute | solution.py:508
  323.4 87.7 %collective-permute-start.2 = (f32[8,4096]{1,0:T(8,128)S(1)}, f32[8,4096]{1,0:T(8,128)S(1)}, u32[]{:S(2)}, u32[]{:S(2)}) collective-permute-start(f32[8,4096]{1,0:T(8,128)S(1)} %get-tuple-element.25), channel_id=1, source_target_pairs={{1,2},{3,4},{5,6},{7,8},{9,10},{11,12},{13,14},{15,16},{17,18},{19... | collective-permute-start | bytes 393224 | tf_op jit(solution)/shard_map/ppermute | solution.py:498
  325.8 85.3 %collective-permute-start.1 = (f32[8,4096]{1,0:T(8,128)S(1)}, f32[8,4096]{1,0:T(8,128)S(1)}, u32[]{:S(2)}, u32[]{:S(2)}) collective-permute-start(f32[8,4096]{1,0:T(8,128)S(1)} %get-tuple-element.26), channel_id=1, source_target_pairs={{0,2},{2,4},{4,6},{6,8},{8,10},{10,12},{12,14},{14,16},{16,18},{18... | collective-permute-start | bytes 393224 | tf_op jit(solution)/shard_map/ppermute | solution.py:498
  327.8 83.3 %collective-permute-start.4 = (f32[3,2,4096]{2,1,0:T(2,128)S(1)}, f32[3,2,4096]{2,1,0:T(2,128)S(1)}, u32[]{:S(2)}, u32[]{:S(2)}) collective-permute-start(f32[3,2,4096]{2,1,0:T(2,128)S(1)} %pad_maximum_fusion.1), channel_id=1, source_target_pairs={{1,0},{2,1},{3,2},{4,3},{5,4},{6,5},{7,6},{8,7},{9,8},{10,9},{11,1... | collective-permute-start | bytes 294920 | tf_op jit(solution)/shard_map/ppermute | solution.py:508
  408.0 3.1 copy-start.3
  411.1 0.6 copy-start.4
  411.1 0.7 copy-start.1
  411.1 0.7 copy-start.2
  451.7 25.2 %collective-permute-start.5 = (f32[128,4096]{1,0:T(8,128)}, f32[128,4096]{1,0:T(8,128)S(1)}, u32[]{:S(2)}, u32[]{:S(2)}) collective-permute-start(f32[128,4096]{1,0:T(8,128)} %get-tuple-element.17), channel_id=1, source_target_pairs={{0,1},{1,0},{2,3},{3,2},{4,5},{5,4},{6,7},{7,6},{8,9},{9,8},{10,11... | collective-permute-start | bytes 6291464 | tf_op jit(solution)/shard_map/ppermute | solution.py:485
  476.9 1.3 copy-start

commit v3 on v2

v3 whole, which is shorter than its diff:
```python
import math
from functools import partial

import jax
import jax.numpy as jnp
import ml_dtypes
import numpy as np
from jax import lax
from jax.experimental import pallas as pl
from jax.experimental.pallas import tpu as pltpu
from jax.sharding import PartitionSpec as P


data_step = 0.8
primal_step = 0.5
low_taps = (0.0625, 0.25, 0.375, 0.25, 0.0625)
high_taps = (-0.1, -0.3, 0.7, -0.2, -0.1)
low_reverse = (0.0625, 0.25, 0.375, 0.25, 0.0625)
high_reverse = (-0.1, -0.2, 0.7, -0.3, -0.1)

VMEM_LIMIT = 60 * 1024 * 1024


def c_add(x, y):
    if x[1] is None and y[1] is None:
        return (x[0] + y[0], None)
    if x[1] is None:
        return (x[0] + y[0], y[1])
    if y[1] is None:
        return (x[0] + y[0], x[1])
    return (x[0] + y[0], x[1] + y[1])


def c_sub(x, y):
    if x[1] is None and y[1] is None:
        return (x[0] - y[0], None)
    if x[1] is None:
        return (x[0] - y[0], -y[1])
    if y[1] is None:
        return (x[0] - y[0], x[1])
    return (x[0] - y[0], x[1] - y[1])


def c_rot(x, turn):
    turn = turn % 1.0
    wr, wi = math.cos(2 * math.pi * turn), math.sin(2 * math.pi * turn)
    re, im = x
    if turn == 0.0:
        return x
    if turn == 0.5:
        return (-re, None if im is None else -im)
    if turn == 0.25:
        return (jnp.zeros_like(re) if im is None else -im, re)
    if turn == 0.75:
        return (jnp.zeros_like(re) if im is None else im, -re)
    if im is None:
        return (re * wr, re * wi)
    if abs(abs(wr) - abs(wi)) < 1e-12:
        h = abs(wr)
        p, m = (re + im) * h, (re - im) * h
        if wr > 0:
            return (m, p) if wi > 0 else (p, -m)
        return (-p, m) if wi > 0 else (-m, -p)
    return (re * wr - im * wi, re * wi + im * wr)


def c_rot90_add(x, y, sign):
    re, im = x
    yr, yi = y
    if yi is not None:
        re = re - yi if sign > 0 else re + yi
    if im is None:
        im = yr if sign > 0 else -yr
    else:
        im = im + yr if sign > 0 else im - yr
    return (re, im)


def small_dft(xs, sign):
    n = len(xs)
    if n == 1:
        return list(xs)
    if n == 2:
        return [c_add(xs[0], xs[1]), c_sub(xs[0], xs[1])]
    if n % 4 == 0:
        parts = [small_dft(xs[r::4], sign) for r in range(4)]
        out = [None] * n
        for k in range(n // 4):
            t = [c_rot(parts[r][k], sign * r * k / n) for r in range(4)]
            s0, s1 = c_add(t[0], t[2]), c_sub(t[0], t[2])
            s2, s3 = c_add(t[1], t[3]), c_sub(t[1], t[3])
            out[k] = c_add(s0, s2)
            out[k + n // 2] = c_sub(s0, s2)
            out[k + n // 4] = c_rot90_add(s1, s3, sign)
            out[k + 3 * n // 4] = c_rot90_add(s1, s3, -sign)
        return out
    even, odd = small_dft(xs[0::2], sign), small_dft(xs[1::2], sign)
    out = [None] * n
    for k in range(n // 2):
        t = c_rot(odd[k], sign * k / n)
        out[k], out[k + n // 2] = c_add(even[k], t), c_sub(even[k], t)
    return out


def split_constant(table):
    high = table.astype(ml_dtypes.bfloat16)
    low = (table - high.astype(np.float64)).astype(ml_dtypes.bfloat16)
    return high, low


def dft_matrix(rows, cols, length, sign):
    angle = 2.0 * np.pi * ((np.asarray(rows)[:, None] * np.asarray(cols)[None, :]) % length) / length
    return np.cos(angle), sign * np.sin(angle)


def phase_rows(count, positions, length):
    wide = lambda t: np.ascontiguousarray(np.broadcast_to(t[:, None, :], (count, 8, t.shape[1]))).astype(np.float32)
    re, im = dft_matrix(np.arange(count), positions, length, 1)
    return wide(re), wide(im)


def split_value(value):
    high = value.astype(jnp.bfloat16)
    low = (value - high.astype(jnp.float32)).astype(jnp.bfloat16)
    return high, low


def dot_nt(a, b):
    return lax.dot_general(a, b, (((1,), (1,)), ((), ())), preferred_element_type=jnp.float32)


def dot_split(high, low, value):
    v_high, v_low = split_value(value)
    return dot_nt(high, v_high) + (dot_nt(low, v_high) + dot_nt(high, v_low))


def lane_step(width):
    return 128 if width % 128 == 0 else width


def radix_stage(load, tw_re, tw_im, store, rows, width, count, sign, shift=0):
    step = lane_step(width)
    low, high = rows if isinstance(rows, tuple) else (0, rows)

    def body(i, carry):
        at = pl.ds(pl.multiple_of(i * 8, 8), 8)
        for lane in range(0, width, step):
            lanes = slice(lane, lane + step)
            ys = small_dft([load(p, at, lanes) for p in range(count)], sign)
            for p in range(count):
                re, im = ys[p]
                if p == 0:
                    store(p, at, lanes, re, jnp.zeros_like(re) if im is None else im)
                    continue
                from_table = slice(shift + lane, shift + lane + step)
                wr, wi = tw_re[p, :, from_table], tw_im[p, :, from_table]
                if im is None:
                    store(p, at, lanes, re * wr, re * wi if sign > 0 else -(re * wi))
                elif sign > 0:
                    store(p, at, lanes, re * wr - im * wi, re * wi + im * wr)
                else:
                    store(p, at, lanes, re * wr + im * wi, im * wr - re * wi)
        return carry

    lax.fori_loop(low // 8, high // 8, body, 0)


def lane_tiles(width):
    step = lane_step(width)
    return width // step, step


def store_rows(out, lead, p, n, count, value):
    tiles, step = lane_tiles(value.shape[1])
    room = out.shape[-1]
    for t in range(tiles):
        piece = value[:, t * step : (t + 1) * step]
        if room > step:
            piece = jnp.concatenate([piece, jnp.zeros((n, room - step), piece.dtype)], axis=1)
        at = pl.ds(p, n, stride=count) if n > 1 else pl.ds(p, 1)
        out[(*lead, t, at, slice(None))] = piece


def mix_pair(g_high, g_low, y_re, y_im, half, sign):
    a = dot_split(g_high[...], g_low[...], y_re)
    b = dot_split(g_high[...], g_low[...], y_im)
    if sign > 0:
        return a[:half] - b[half:], b[:half] + a[half:]
    return a[:half] + b[half:], b[:half] - a[half:]


def fetch_pieces(pieces, target, sem):
    me = lax.axis_index("row")
    copies = []
    for d, piece in enumerate(pieces):
        place = target if len(pieces) == 1 else target.at[jnp.bitwise_xor(me, d)]
        copies.append(pltpu.make_async_copy(piece, place, sem.at[d]))
        copies[-1].start()
    return copies


def store_pieces(source, pieces, sem):
    me = lax.axis_index("row")
    copies = []
    for d, piece in enumerate(pieces):
        place = source if len(pieces) == 1 else source.at[jnp.bitwise_xor(me, d)]
        copies.append(pltpu.make_async_copy(place, piece, sem.at[d]))
        copies[-1].start()
    for copy in copies:
        copy.wait()


def first_kernel(count, width, kept, n, x_hbm, tw_re, tw_im, f_high, f_low, *refs):
    pieces, (x, out, y_re, y_im, x_sem, sem) = refs[:n], refs[n:]
    rows = x.shape[0]
    parts = SKY_PARTS if rows % (8 * SKY_PARTS) == 0 else 1
    copies = []
    for i in range(parts):
        at = pl.ds(i * (rows // parts), rows // parts)
        copies.append(pltpu.make_async_copy(x_hbm.at[at], x.at[at], x_sem.at[i]))
        copies[-1].start()

    def load(p, at, lanes):
        return (x[at, p * width + lanes.start : p * width + lanes.stop], None)

    def store(p, at, lanes, re, im):
        y_re[p, at, lanes] = re
        y_im[p, at, lanes] = im

    for i in range(parts):
        copies[i].wait()
        span = (i * (rows // parts), (i + 1) * (rows // parts))
        radix_stage(load, tw_re, tw_im, store, span, width, count, -1)

    def body(p, carry):
        z_re, z_im = mix_pair(f_high, f_low, y_re[p], y_im[p], count * kept, -1)
        for m in range(count):
            store_rows(out, (m, 0), p, kept, count, z_re[m * kept : (m + 1) * kept])
            store_rows(out, (m, 1), p, kept, count, z_im[m * kept : (m + 1) * kept])
        return carry

    lax.fori_loop(0, count, body, 0, unroll=UNROLL)
    store_pieces(out, pieces, sem)


def flipped(ref, at, n):
    return jnp.concatenate([ref[t, at, :].T for t in range(ref.shape[0])], axis=0)[:n]


def middle_kernel(count, width, n, *refs):
    came, refs = refs[:n], refs[n:]
    dual, vis, weights, before, tw_re, tw_im, g_high, g_low, resid, sums = refs[:10]
    pieces, refs = refs[10 : 10 + n], refs[10 + n :]
    got, out, y_re, y_im, zt_re, zt_im, s_re, s_im, sem = refs
    for copy in fetch_pieces(came, got, sem):
        copy.wait()
    batch = got.shape[3]
    length = count * width
    per = width // count

    def load(p, at, lanes):
        tile = lanes.start // got.shape[4]
        return (got[p, 0, tile, at, :], got[p, 1, tile, at, :])

    def store(p, at, lanes, re, im):
        y_re[p, at, lanes] = re
        y_im[p, at, lanes] = im

    radix_stage(load, tw_re, tw_im, store, batch, width, count, -1)

    def forward(p, carry):
        z_re, z_im = mix_pair(g_high, g_low, y_re[p], y_im[p], width, -1)
        store_rows(zt_re, (), p, width, count, z_re)
        store_rows(zt_im, (), p, width, count, z_im)
        return carry

    lax.fori_loop(0, count, forward, 0, unroll=UNROLL)

    def residual(i, carry):
        d_sum, v_sum = carry
        start = pl.multiple_of(i * 128, 128)
        at = pl.ds(start, 128)
        w = weights[0, :, at]
        v_re, v_im = vis[0, 0, :, at], vis[1, 0, :, at]
        d_re = dual[0, 0, :, at] * (1.0 / data_step) + w * flipped(zt_re, at, batch) - v_re
        d_im = dual[1, 0, :, at] * (1.0 / data_step) + w * flipped(zt_im, at, batch) - v_im
        resid[0, 0, :, at] = d_re
        resid[1, 0, :, at] = d_im
        s_re[:, at] = w * d_re
        s_im[:, at] = w * d_im
        fold = lambda t: jnp.sum(t.reshape(batch // 8, 8, 128), axis=0)
        return d_sum + fold(d_re * d_re + d_im * d_im), v_sum + fold(v_re * v_re + v_im * v_im)

    d_sum, v_sum = lax.fori_loop(0, length // 128, residual, (before[0], before[1]))
    sums[0] = d_sum
    sums[1] = v_sum

    def load_2(p, at, lanes):
        lanes = slice(p * width + lanes.start, p * width + lanes.stop)
        return (s_re[at, lanes], s_im[at, lanes])

    radix_stage(load_2, tw_re, tw_im, store, batch, width, count, 1)

    def inverse(p, carry):
        u_re, u_im = mix_pair(g_high, g_low, y_re[p], y_im[p], width, 1)
        for m in range(count):
            store_rows(out, (m, 0), p, per, count, u_re[m * per : (m + 1) * per])
            store_rows(out, (m, 1), p, per, count, u_im[m * per : (m + 1) * per])
        return carry

    lax.fori_loop(0, count, inverse, 0, unroll=UNROLL)
    store_pieces(out, pieces, sem)


def last_kernel(count, width, start, n, is_first, is_last, *refs):
    came, refs = refs[:n], list(refs[n:])
    take = lambda k: [refs.pop(0) for _ in range(k)]
    base_hbm = take(3 if is_first else 1)
    tw_re, tw_im, g_high, g_low, shrink, out_hbm, got, base, y_re, y_im, gt, sem, came_sem = take(13)
    adjoint = refs.pop(0) if is_first else None
    rows, batch = got.shape[3], got.shape[2] * got.shape[4]
    length = count * width
    me = lax.axis_index("chan")
    fetch_got = fetch_pieces(came, got, came_sem)
    half = rows // 2
    fetch_base = [pltpu.make_async_copy(base_hbm[0], base, sem.at[0])]
    if is_first:
        for i, side in enumerate((me, 1 - me)):
            place = adjoint.at[pl.ds(pl.multiple_of(half * side, 8), half)]
            fetch_base.append(pltpu.make_async_copy(base_hbm[1 + i], place, sem.at[1 + i]))
    for copy in fetch_base:
        copy.start()
    for copy in fetch_got:
        copy.wait()

    def load(p, at, lanes):
        tile = lanes.start // got.shape[4]
        return (got[p, 0, tile, at, :], got[p, 1, tile, at, :])

    def store(p, at, lanes, re, im):
        y_re[p, at, lanes] = re
        y_im[p, at, lanes] = im

    radix_stage(load, tw_re, tw_im, store, rows, batch, count, 1, start)
    cols = slice(start, start + batch)
    e_high = jnp.concatenate([g_high[:width, cols], -g_high[width:, cols]], axis=1)
    e_low = jnp.concatenate([g_low[:width, cols], -g_low[width:, cols]], axis=1)

    def inverse(p, carry):
        u = dot_split(e_high, e_low, jnp.concatenate([y_re[p], y_im[p]], axis=1))
        store_rows(gt, (), p, width, count, u)
        return carry

    lax.fori_loop(0, count, inverse, 0, unroll=UNROLL)
    for copy in fetch_base:
        copy.wait()
    scale = primal_step * shrink[0]
    groups = 4
    stores = []
    for g in range(groups):
        tiles = length // 128 // groups

        def finish(i, carry):
            at = pl.ds(pl.multiple_of(i * 128, 128), 128)
            value = base[:, at] - scale * flipped(gt, at, rows)
            if is_first:
                value = value - primal_step * adjoint[:, at]
            base[:, at] = jnp.maximum(value, 0.0) if is_last else value
            return carry

        lax.fori_loop(g * tiles, (g + 1) * tiles, finish, 0, unroll=UNROLL)
        at = pl.ds(g * tiles * 128, tiles * 128)
        stores.append(pltpu.make_async_copy(base.at[:, at], out_hbm.at[:, at], sem.at[3 + g]))
        stores[-1].start()
    for copy in stores:
        copy.wait()


def vmem(shape, dtype=jnp.float32):
    return pltpu.VMEM(shape, dtype)


def whole(shape):
    return pl.BlockSpec(shape, lambda *_: (0,) * len(shape), pipeline_mode=pl.Buffered(1))


def call(kernel, args, specs, out_shape, out_specs, scratch, flops, moved):
    return pl.pallas_call(
        kernel,
        grid=(1,),
        in_specs=specs,
        out_specs=out_specs,
        out_shape=out_shape,
        scratch_shapes=scratch,
        cost_estimate=pl.CostEstimate(flops=flops, bytes_accessed=moved, transcendentals=0),
        compiler_params=pltpu.CompilerParams(vmem_limit_bytes=VMEM_LIMIT),
    )(*args)


def analysis(source, start, n, low, high):
    if isinstance(start, int):
        taps = [source[start + p : start + p + n, :] for p in range(5)]
    else:
        window = source[pl.ds(pl.multiple_of(start - 6, 8), n + 16), :]
        taps = [window[6 + p : 6 + p + n] for p in range(5)]
    width = taps[0].shape[1]

    def along(coefs):
        if coefs[0] == coefs[4]:
            total = coefs[2] * taps[2] + coefs[0] * (taps[0] + taps[4])
        else:
            total = coefs[2] * taps[2] + (coefs[0] * taps[0] + coefs[4] * taps[4])
        if coefs[1] == coefs[3]:
            return total + coefs[1] * (taps[1] + taps[3])
        return total + (coefs[1] * taps[1] + coefs[3] * taps[3])

    a, b = along(high), along(low)
    total = low[2] * a + high[2] * b
    pad = jnp.zeros((n, 128), jnp.float32)
    mixed = {}
    for p in (0, 1, 3, 4):
        pair = (low[p], high[p])
        if pair not in mixed:
            mixed[pair] = jnp.concatenate([low[p] * a + high[p] * b, pad], axis=1)
        total = total + pltpu.roll(mixed[pair], (2 - p) % (width + 128), 1)[:, :width]
    return total


def wave_kernel(
    count, sky, other, edge_own, edge_other, dual, above, below, limit, wave, outside, x, sem
):
    me = lax.axis_index("chan")
    row = lax.axis_index("row")
    half = limit.shape[0]
    base = pl.multiple_of(8 * (1 - me), 8)
    edge = pl.ds(pl.multiple_of((half + 8) * me, 8), 8)
    own_rows = pl.ds(pl.multiple_of((half - 8) * me, 8), half + 8)
    copies = [
        pltpu.make_async_copy(sky.at[own_rows], x.at[0, pl.ds(base, half + 8)], sem.at[0]),
        pltpu.make_async_copy(other, x.at[1, pl.ds(base, half + 8)], sem.at[1]),
        pltpu.make_async_copy(edge_own, x.at[0, edge], sem.at[2]),
        pltpu.make_async_copy(edge_other, x.at[1, edge], sem.at[3]),
    ]
    for copy in copies:
        copy.start()
    for copy in copies:
        copy.wait()

    def shrunk(start, n, dual_own, dual_other, bound):
        s_own = dual_own + analysis(x.at[0], start - 2, n, low_taps, high_taps)
        s_other = dual_other + analysis(x.at[1], start - 2, n, low_taps, high_taps)
        factor = bound / jnp.maximum(jnp.sqrt(s_own * s_own + s_other * s_other), bound)
        return s_own * factor, s_other * factor

    first = jnp.logical_and(row == 0, me == 0)
    last = jnp.logical_and(row == count - 1, me == 1)
    outside[...] = jnp.zeros_like(outside)
    for side, (ref, start, beyond) in enumerate(((above, 6, first), (below, half + 8, last))):
        a, b = shrunk(start, 2, ref[me], ref[1 - me], ref[2])
        at = slice(6, 8) if side == 0 else slice(0, 2)
        outside[0, side, at, :] = jnp.where(beyond, 0.0, a)
        outside[1, side, at, :] = jnp.where(beyond, 0.0, b)

    def body(i, carry):
        at = pl.ds(pl.multiple_of(i * 8, 8), 8)
        a, b = shrunk(i * 8 + 8, 8, dual[me, at, :], dual[1 - me, at, :], limit[at, :])
        wave[me, at, :] = a
        wave[1 - me, at, :] = b
        return carry

    lax.fori_loop(0, half // 8, body, 0)


def adjoint_kernel(wave, outside, own_out, other_out, w, sem):
    me = lax.axis_index("chan")
    half = own_out.shape[0]
    copies = []
    for i, plane in enumerate((me, 1 - me)):
        copies.append(pltpu.make_async_copy(wave.at[plane], w.at[i, pl.ds(8, half)], sem.at[i, 0]))
        copies.append(pltpu.make_async_copy(outside.at[i, 0], w.at[i, pl.ds(0, 8)], sem.at[i, 1]))
        copies.append(pltpu.make_async_copy(outside.at[i, 1], w.at[i, pl.ds(half + 8, 8)], sem.at[i, 2]))
    for copy in copies:
        copy.start()
    for copy in copies:
        copy.wait()

    def back(i, carry):
        at = pl.ds(pl.multiple_of(i * 8, 8), 8)
        own_out[at, :] = analysis(w.at[0], i * 8 + 6, 8, low_reverse, high_reverse)
        other_out[at, :] = analysis(w.at[1], i * 8 + 6, 8, low_reverse, high_reverse)
        return carry

    lax.fori_loop(0, half // 8, back, 0)


def chan_swap(value):
    size = lax.axis_size("chan")
    return lax.ppermute(value, "chan", [(i, (i + 1) % size) for i in range(size)])


UNROLL = 2
SKY_PARTS = 4


def partners(size):
    quarter = size // 4
    far = [d for i in range(quarter) for d in (2 * quarter + i, 3 * quarter + i)]
    return far[:2] + [*range(quarter, 2 * quarter), *range(1, quarter)] + far[2:]


def row_exchange(pieces):
    if len(pieces) == 1:
        return [lax.all_to_all(pieces[0], "row", split_axis=0, concat_axis=0, tiled=True)]
    size = len(pieces)
    got = list(pieces)
    for d in reversed(partners(size)):
        got[d] = lax.ppermute(pieces[d], "row", [(i, i ^ d) for i in range(size)])
    return got


def row_total(value):
    size = lax.axis_size("row")
    away = lambda v, d: lax.ppermute(v, "row", [(i, i ^ d) for i in range(size)])
    value = value + away(value, 1)
    return value + sum(away(value, d) for d in range(2, size, 2))


def edges_of(sky):
    count, size = lax.axis_size("row"), lax.axis_size("chan")
    top, bottom = sky[:8], sky[-8:]
    me = lax.axis_index("chan")
    at = lambda r, c: r * size + c
    own = [(at(r, 0), at(r + 1, 0)) for r in range(count - 1)] + [(at(r + 1, 1), at(r, 1)) for r in range(count - 1)]
    cross = [(at(r, 1), at(r + 1, 0)) for r in range(count - 1)] + [(at(r + 1, 0), at(r, 1)) for r in range(count - 1)]
    sent_own = jnp.where(me == 0, bottom, top)
    sent_cross = jnp.where(me == 0, top, bottom)
    axes = ("row", "chan")
    return lax.ppermute(sent_own, axes, own), lax.ppermute(sent_cross, axes, cross)


def facet_neighbours(wavelet_dual, reweight):
    axes = ("row", "chan")
    count = lax.axis_size(axes)
    up = [(i, i + 1) for i in range(count - 1)]
    down = [(j, i) for i, j in up]
    last = jnp.concatenate([wavelet_dual[:, -2:], reweight[None, -2:]])
    first = jnp.concatenate([wavelet_dual[:, :2], reweight[None, :2]])
    return lax.ppermute(last, axes, up), lax.ppermute(first, axes, down)


def per_device(sky_image, fourier_dual, visibilities, weights, radius, wavelet_dual, reweight):
    f32 = jnp.float32
    sky = sky_image[0]
    rows, length = sky.shape
    count = lax.axis_size("row")
    width = length // count
    per = width // count
    chunks = 2 if per % 2 == 0 else 1
    batch = width // chunks
    kept = per // chunks
    scale = 1.0 / math.sqrt(length)
    shape = jax.ShapeDtypeStruct

    any_space = pl.BlockSpec(memory_space=pl.ANY)
    dma = lambda n: pltpu.SemaphoreType.DMA((n,))
    n = count if count & (count - 1) == 0 and count <= 16 else 1
    pieces_of = lambda packed: [shape(packed[1:], f32)] * n if n > 1 else [shape(packed, f32)]

    def tile(high, wide):
        tiles, step = lane_tiles(wide)
        return tiles, high, step

    lanes = np.arange(width)
    tw = phase_rows(count, lanes, length)
    g_table = split_constant(scale * np.concatenate(dft_matrix(lanes, lanes, width, 1)))

    sent = []
    for c in range(chunks):
        picked = (np.arange(count)[:, None] * per + c * kept + np.arange(kept)[None, :]).reshape(-1)
        table = split_constant(scale * np.concatenate(dft_matrix(picked, lanes, width, 1)))
        args = (sky, *tw, *table)
        packed = (count, 2, *tile(batch, rows))
        piece = call(
            partial(first_kernel, count, width, kept, n), args,
            [any_space] + [whole(a.shape) for a in args[1:]], pieces_of(packed), [any_space] * n,
            [vmem(sky.shape), vmem(packed)] + [vmem((count, rows, width))] * 2 + [dma(SKY_PARTS), dma(n)],
            10**10, 10**7,
        )
        sent.append(row_exchange(piece))

    half = rows // 2
    me = lax.axis_index("chan")
    theirs = lax.dynamic_slice_in_dim(sky, (1 - me) * (half - 8), half + 8, 0)
    other = chan_swap(theirs)
    edge_own, edge_other = edges_of(sky)
    above, below = facet_neighbours(wavelet_dual, reweight)
    args = (sky, other, edge_own, edge_other, wavelet_dual, above, below, reweight)
    outs = (shape((2, half, length), f32), shape((2, 2, 8, length), f32))
    wavelet_new, outside = call(
        partial(wave_kernel, count), args, [any_space] * 4 + [whole(a.shape) for a in args[4:]],
        outs, tuple(whole(o.shape) for o in outs),
        [vmem((2, half + 16, length)), dma(4)], 10**10, 3 * 10**7,
    )
    outs = (shape((half, length), f32), shape((half, length), f32))
    adjoint_own, adjoint_other = call(
        adjoint_kernel, (wavelet_new, outside), [any_space] * 2, outs, tuple(whole(o.shape) for o in outs),
        [vmem((2, half + 16, length)), pltpu.SemaphoreType.DMA((2, 3))], 10**10, 3 * 10**7,
    )
    adjoint_got = chan_swap(adjoint_other)

    resid, returned, sums = [], [], np.zeros((2, 8, 128), np.float32)
    for c in range(chunks):
        block = lambda lead, c=c: pl.BlockSpec(
            (*lead, batch, length), lambda i: (0,) * len(lead) + (c, 0), pipeline_mode=pl.Buffered(1)
        )
        tables = (*tw, *g_table)
        coming = (count, 2, *tile(batch, rows))
        packed = (count, 2, *tile(rows, batch))
        outs = (shape((2, 1, batch, length), f32), shape((2, 8, 128), f32))
        d, part, *piece = call(
            partial(middle_kernel, count, width, n),
            (*sent[c], fourier_dual, visibilities, weights, sums, *tables),
            [any_space] * n + [block((2, 1)), block((2, 1)), block((1,)), *(whole(t.shape) for t in (sums, *tables))],
            [*outs, *pieces_of(packed)], [whole(o.shape) for o in outs] + [any_space] * n,
            [vmem(coming), vmem(packed)] + [vmem((count, batch, width))] * 2 + [vmem((-(-batch // 128), length, 128))] * 2 + [vmem((batch, length))] * 2 + [dma(n)],
            2 * 10**10, 3 * 10**7,
        )
        resid.append(d)
        sums = part
        returned.append(row_exchange(piece))

    total = row_total(sums) if n > 1 else lax.psum(sums, "row")
    data_norm = jnp.sum(total[1])
    resid_norm = jnp.sum(total[0])
    shrink = data_step * (1.0 - radius * jnp.sqrt(data_norm) / jnp.sqrt(resid_norm))
    fourier_new = jnp.concatenate([d * shrink for d in resid], axis=2)

    base = (sky, adjoint_own, adjoint_got)
    for c in range(chunks):
        packed = (count, 2, *tile(rows, batch))
        args = (*returned[c], *base, *tw, *g_table, shrink)
        specs = [any_space] * (n + len(base)) + [whole(a.shape) for a in (*tw, *g_table)]
        specs.append(pl.BlockSpec(memory_space=pltpu.SMEM))
        scratch = [
            vmem(packed), vmem((rows, length)), *[vmem((count, rows, batch))] * 2,
            vmem((-(-rows // 128), length, 128)), dma(7), dma(n), *[vmem((rows, length))] * (c == 0),
        ]
        image_new = call(
            partial(last_kernel, count, width, c * batch, n, c == 0, c == chunks - 1), args, specs,
            shape((rows, length), f32), any_space, scratch, 10**10, 3 * 10**7,
        )
        base = (image_new,)
    return (image_new[None], fourier_new, wavelet_new)


def solution(mesh):
    in_specs = (
        P("chan", "row", None),
        P(None, "chan", "row", None),
        P(None, "chan", "row", None),
        P("chan", "row", None),
        P("chan"),
        P(None, ("row", "chan"), None),
        P(("row", "chan"), None),
    )
    out_specs = (
        P("chan", "row", None),
        P(None, "chan", "row", None),
        P(None, ("row", "chan"), None),
    )

    return jax.shard_map(per_device, mesh=mesh, in_specs=in_specs, out_specs=out_specs, check_vma=False)
```

time: 502 us -> 540 us (1.076)
  starting transfers between devices: 35.4 us -> 118 us
  waiting for transfers between devices: 283 us -> 245 us
  Pallas kernels: 172 us -> 153 us
  other arithmetic: 1.09 us -> 10.5 us
    ppermute x0 -> x68, waiting for transfers between devices: none -> 238 us  [the longest x60 216 us: row_exchange(): got[d] = lax.ppermute(pieces[d], 'row', [(i, i ^ d) for i in range(size)])]
    all_to_all x4 -> x0, waiting for transfers between devices: 191 us -> none  [per_device(): lax.all_to_all(piece, 'row', split_axis=0, concat_axis=0, tiled=True)]
    ppermute x0 -> x68, starting transfers between devices: none -> 106 us  [the longest x60 105 us: row_exchange(): got[d] = lax.ppermute(pieces[d], 'row', [(i, i ^ d) for i in range(size)])]
    ppermute x2, waiting for transfers between devices: 78.1 us -> 3.12 us  [facet_neighbours(): return (lax.ppermute(last, axes, up), lax.ppermute(first, axes, down))]
    all_to_all x4 -> x0, starting transfers between devices: 20.9 us -> none  [per_device(): lax.all_to_all(piece, 'row', split_axis=0, concat_axis=0, tiled=True)]
    pallas_call x7 -> x8, Pallas kernels: 172 us -> 153 us  [call(): pl.pallas_call(kernel, grid=(1,), in_specs=specs, out_specs=out_specs, ou...]
    ppermute x2, waiting for transfers between devices: 13.8 us -> 0.01 us  [chan_swap(): lax.ppermute(value, 'chan', [(i, (i + 1) % size) for i in range(size)])]
  transfers between devices with their start and end apart: 10 -> 74, of which waited for: 6 -> 40; matrix products, arithmetic and copies ran while one was open for 1% -> 3% of each run, Pallas kernels for 27% -> 24%
where the time goes in v3:
time: 540 us; the launch traced here: 538 us
  waiting for transfers between devices  245 us (45%)
  Pallas kernels  153 us (28%)
  starting transfers between devices  118 us (22%)
  other arithmetic  10.5 us (2%)
  local copies, waits for them, and re-layouts  7.51 us (1%)
    ppermute x60, waiting for transfers between devices, row_exchange(): got[d] = lax.ppermute(pieces[d], 'row', [(i, i ^ d) for i in range(size)])  216 us
    pallas_call x8, Pallas kernels, call(): pl.pallas_call(kernel, grid=(1,), in_specs=specs, out_specs=out_specs, ou...  153 us
    ppermute x60, starting transfers between devices, row_exchange(): got[d] = lax.ppermute(pieces[d], 'row', [(i, i ^ d) for i in range(size)])  105 us
    ppermute x8, waiting for transfers between devices, row_total(): lax.ppermute(v, 'row', [(i, i ^ d) for i in range(size)])  21.9 us
  transfers between devices with their start and end apart: 74, of which 40 were waited for; matrix products, arithmetic and copies ran while one was open for 3% of the time, Pallas kernels for 24%

profile of v3, /device:TPU:15, one launch (start us, length us, event | category | flops | bytes accessed | tf_op | source)
XLA Modules:
  0.0 538.3 jit_solution(5742404044588473302)
XLA Ops:
  0.6 12.3 %shard_map.176 = (f32[2,2,128,128]{3,2,1,0:T(8,128)}, f32[2,2,128,128]{3,2,1,0:T(8,128)}, f32[2,2,128,128]{3,2,1,0:T(8,128)}, f32[2,2,128,128]{3,2,1,0:T(8,128)}...) custom-call(f32[256,4096]{1,0:T(8,128)} %bitcast.15, ...), custom_call_target="tpu_custom_call" | custom-call | flops 10000000000 | bytes 10000000 | tf_op jit(solution)/shard_map/pallas_call | solution.py:388
  23.7 3.1 collective-permute-done.64.below
  31.3 4.2 collective-permute-done.17.refs_3_
  40.0 13.1 %collective-permute-done.20.refs_6_ = f32[2,2,128,128]{3,2,1,0:T(8,128)S(1)} collective-permute-done((f32[2,2,128,128]{3,2,1,0:T(8,128)}, f32[2,2,128,128]{3,2,1,0:T(8,128)S(1)}, u32[]{:S(2)}, u32[]{:S(2)}) %collective-permute-start.20) | collective-permute-done | bytes 262176 | tf_op jit(solution)/shard_map/ppermute | solution.py:517
  53.1 3.4 collective-permute-start.25
  56.6 12.3 %shard_map.175 = (f32[2,2,128,128]{3,2,1,0:T(8,128)}, f32[2,2,128,128]{3,2,1,0:T(8,128)}, f32[2,2,128,128]{3,2,1,0:T(8,128)}, f32[2,2,128,128]{3,2,1,0:T(8,128)}...) custom-call(f32[256,4096]{1,0:T(8,128)} %bitcast.16, ...), custom_call_target="tpu_custom_call" | custom-call | flops 10000000000 | bytes 10000000 | tf_op jit(solution)/shard_map/pallas_call | solution.py:388
  71.4 12.1 %collective-permute-done.23.refs_9_ = f32[2,2,128,128]{3,2,1,0:T(8,128)} collective-permute-done((f32[2,2,128,128]{3,2,1,0:T(8,128)}, f32[2,2,128,128]{3,2,1,0:T(8,128)}, u32[]{:S(2)}, u32[]{:S(2)}) %collective-permute-start.23) | collective-permute-done | bytes 262176 | tf_op jit(solution)/shard_map/ppermute | solution.py:517
  83.6 11.2 %collective-permute-done.24.refs_10_ = f32[2,2,128,128]{3,2,1,0:T(8,128)} collective-permute-done((f32[2,2,128,128]{3,2,1,0:T(8,128)}, f32[2,2,128,128]{3,2,1,0:T(8,128)}, u32[]{:S(2)}, u32[]{:S(2)}) %collective-permute-start.24) | collective-permute-done | bytes 262176 | tf_op jit(solution)/shard_map/ppermute | solution.py:517
  94.8 5.6 %collective-permute-done.25.refs_11_ = f32[2,2,128,128]{3,2,1,0:T(8,128)} collective-permute-done((f32[2,2,128,128]{3,2,1,0:T(8,128)}, f32[2,2,128,128]{3,2,1,0:T(8,128)}, u32[]{:S(2)}, u32[]{:S(2)}) %collective-permute-start.25) | collective-permute-done | bytes 262176 | tf_op jit(solution)/shard_map/ppermute | solution.py:517
  100.4 11.2 %collective-permute-done.26.refs_12_ = f32[2,2,128,128]{3,2,1,0:T(8,128)S(1)} collective-permute-done((f32[2,2,128,128]{3,2,1,0:T(8,128)}, f32[2,2,128,128]{3,2,1,0:T(8,128)S(1)}, u32[]{:S(2)}, u32[]{:S(2)}) %collective-permute-start.26) | collective-permute-done | bytes 262176 | tf_op jit(solution)/shard_map/ppermute | solution.py:517
  111.9 5.3 collective-permute-done.27.refs_13_
  117.2 33.7 %collective-permute-done.28.refs_14_ = f32[2,2,128,128]{3,2,1,0:T(8,128)S(1)} collective-permute-done((f32[2,2,128,128]{3,2,1,0:T(8,128)S(1)}, f32[2,2,128,128]{3,2,1,0:T(8,128)S(1)}, u32[]{:S(2)}, u32[]{:S(2)}) %collective-permute-start.28) | collective-permute-done | bytes 262176 | tf_op jit(solution)/shard_map/ppermute | solution.py:517
  153.0 3.5 collective-permute-done.29.refs_15_
  163.9 3.9 collective-permute-done.11.refs_12_
  167.9 5.6 %collective-permute-done.12.refs_13_ = f32[2,2,128,128]{3,2,1,0:T(8,128)S(1)} collective-permute-done((f32[2,2,128,128]{3,2,1,0:T(8,128)}, f32[2,2,128,128]{3,2,1,0:T(8,128)S(1)}, u32[]{:S(2)}, u32[]{:S(2)}) %collective-permute-start.12) | collective-permute-done | bytes 262176 | tf_op jit(solution)/shard_map/ppermute | solution.py:517
  173.5 5.6 %collective-permute-done.13.refs_14_ = f32[2,2,128,128]{3,2,1,0:T(8,128)S(1)} collective-permute-done((f32[2,2,128,128]{3,2,1,0:T(8,128)}, f32[2,2,128,128]{3,2,1,0:T(8,128)S(1)}, u32[]{:S(2)}, u32[]{:S(2)}) %collective-permute-start.13) | collective-permute-done | bytes 262176 | tf_op jit(solution)/shard_map/ppermute | solution.py:517
  181.6 3.1 collective-permute-done.14.refs_15_
  184.8 5.5 %collective-permute-start.7 = (f32[2,2,128,128]{3,2,1,0:T(8,128)S(1)}, f32[2,2,128,128]{3,2,1,0:T(8,128)}, u32[]{:S(2)}, u32[]{:S(2)}) collective-permute-start(f32[2,2,128,128]{3,2,1,0:T(8,128)S(1)} %copy-done.35), channel_id=1, source_target_pairs={{0,16},{2,18},{4,20},{6,22},{8,24},{10,26},{12,28},{14,30},{16,0},... | collective-permute-start | bytes 786440 | tf_op jit(solution)/shard_map/ppermute | solution.py:517
  194.0 33.5 %shard_map.177 = (f32[2,1,128,4096]{3,2,1,0:T(8,128)}, f32[2,8,128]{2,1,0:T(8,128)}, f32[2,1,256,128]{3,2,1,0:T(8,128)}, f32[2,1,256,128]{3,2,1,0:T(8,128)}, f32...) custom-call(f32[2,2,128,128]{3,2,1,0:T(8,128)} %get-tuple-element.91, ...), custom_call_target="tpu_custom_call" | custom-call | flops 20000000000 | bytes 30000000 | tf_op jit(solution)/shard_map/pallas_call | solution.py:388
  232.9 33.5 %shard_map.178 = (f32[2,1,128,4096]{3,2,1,0:T(8,128)}, f32[2,8,128]{2,1,0:T(8,128)}, f32[2,1,256,128]{3,2,1,0:T(8,128)}, f32[2,1,256,128]{3,2,1,0:T(8,128)}, f32...) custom-call(f32[2,2,128,128]{3,2,1,0:T(8,128)} %get-tuple-element.75, ...), custom_call_target="tpu_custom_call" | custom-call | flops 20000000000 | bytes 30000000 | tf_op jit(solution)/shard_map/pallas_call | solution.py:388
  267.8 3.4 collective-permute-start.62
  271.9 3.9 collective-permute-done.62.edge_other
  281.2 3.1 collective-permute-done.69
  284.3 3.4 collective-permute-done.70
  287.7 4.3 collective-permute-done.71
  297.9 3.6 collective-permute-start.48
  301.5 9.2 %collective-permute-start.49 = (f32[2,1,256,128]{3,2,1,0:T(8,128)}, f32[2,1,256,128]{3,2,1,0:T(8,128)S(1)}, u32[]{:S(2)}, u32[]{:S(2)}) collective-permute-start(f32[2,1,256,128]{3,2,1,0:T(8,128)} %get-tuple-element.129), channel_id=1, source_target_pairs={{0,10},{2,8},{4,14},{6,12},{8,2},{10,0},{12,6},{14,4},{16,26},{18,... | collective-permute-start | bytes 786440 | tf_op jit(solution)/shard_map/ppermute | solution.py:517
  313.8 19.3 %shard_map.179 = (f32[2,128,4096]{2,1,0:T(8,128)}, f32[2,2,8,4096]{3,2,1,0:T(8,128)}) custom-call(f32[256,4096]{1,0:T(8,128)} %bitcast.17, f32[136,4096]{1,0:T(8,128)} %collective-permute-done.60.other, f32[8,4096]{1,0:T(8,128)} %copy-done.72, f32[8,4096]{1,0:T(8,128)} %copy-done.73, f32[2,128,4096]{2,1,0:T(8,128)} %dual.1, f32[3,2,4096]{2,1,0:T(2,128)} %copy-done.74, ...), custom_call_target="tpu_custom_call" | custom-call | flops 10000000000 | bytes 30000000 | tf_op jit(solution)/shard_map/pallas_call | solution.py:388
  335.7 3.6 collective-permute-start.55
  341.0 14.5 %shard_map.180 = (f32[128,4096]{1,0:T(8,128)}, f32[128,4096]{1,0:T(8,128)}) custom-call(f32[2,128,4096]{2,1,0:T(8,128)} %get-tuple-element.74.wave, f32[2,2,8,4096]{3,2,1,0:T(8,128)} %get-tuple-element.141.outside), custom_call_target="tpu_custom_call" | custom-call | flops 10000000000 | bytes 30000000 | tf_op jit(solution)/shard_map/pallas_call | solution.py:388
  355.5 14.9 %collective-permute-done.53.refs_9_ = f32[2,1,256,128]{3,2,1,0:T(8,128)S(1)} collective-permute-done((f32[2,1,256,128]{3,2,1,0:T(8,128)}, f32[2,1,256,128]{3,2,1,0:T(8,128)S(1)}, u32[]{:S(2)}, u32[]{:S(2)}) %collective-permute-start.53) | collective-permute-done | bytes 262176 | tf_op jit(solution)/shard_map/ppermute | solution.py:517
  370.4 11.2 %collective-permute-done.54.refs_10_ = f32[2,1,256,128]{3,2,1,0:T(8,128)} collective-permute-done((f32[2,1,256,128]{3,2,1,0:T(8,128)}, f32[2,1,256,128]{3,2,1,0:T(8,128)}, u32[]{:S(2)}, u32[]{:S(2)}) %collective-permute-start.54) | collective-permute-done | bytes 262176 | tf_op jit(solution)/shard_map/ppermute | solution.py:517
  381.6 5.5 %collective-permute-done.55.refs_11_ = f32[2,1,256,128]{3,2,1,0:T(8,128)} collective-permute-done((f32[2,1,256,128]{3,2,1,0:T(8,128)S(1)}, f32[2,1,256,128]{3,2,1,0:T(8,128)}, u32[]{:S(2)}, u32[]{:S(2)}) %collective-permute-start.55) | collective-permute-done | bytes 262176 | tf_op jit(solution)/shard_map/ppermute | solution.py:517
  387.7 11.4 %collective-permute-done.56.refs_12_ = f32[2,1,256,128]{3,2,1,0:T(8,128)} collective-permute-done((f32[2,1,256,128]{3,2,1,0:T(8,128)S(1)}, f32[2,1,256,128]{3,2,1,0:T(8,128)}, u32[]{:S(2)}, u32[]{:S(2)}) %collective-permute-start.56) | collective-permute-done | bytes 262176 | tf_op jit(solution)/shard_map/ppermute | solution.py:517
  399.0 5.6 %collective-permute-done.57.refs_13_ = f32[2,1,256,128]{3,2,1,0:T(8,128)} collective-permute-done((f32[2,1,256,128]{3,2,1,0:T(8,128)S(1)}, f32[2,1,256,128]{3,2,1,0:T(8,128)}, u32[]{:S(2)}, u32[]{:S(2)}) %collective-permute-start.57) | collective-permute-done | bytes 262176 | tf_op jit(solution)/shard_map/ppermute | solution.py:517
  411.8 3.5 collective-permute-done.59.refs_15_
  418.8 4.2 broadcast_multiply_fusion
  426.9 3.4 collective-permute-done.34.refs_5_
  431.5 11.1 %collective-permute-done.35.refs_6_ = f32[2,1,256,128]{3,2,1,0:T(8,128)S(1)} collective-permute-done((f32[2,1,256,128]{3,2,1,0:T(8,128)S(1)}, f32[2,1,256,128]{3,2,1,0:T(8,128)S(1)}, u32[]{:S(2)}, u32[]{:S(2)}) %collective-permute-start.35) | collective-permute-done | bytes 262176 | tf_op jit(solution)/shard_map/ppermute | solution.py:517
  445.3 3.9 pad_maximum_fusion
  454.2 16.7 %collective-permute-start.42 = (f32[2,1,256,128]{3,2,1,0:T(8,128)S(1)}, f32[2,1,256,128]{3,2,1,0:T(8,128)S(1)}, u32[]{:S(2)}, u32[]{:S(2)}) collective-permute-start(f32[2,1,256,128]{3,2,1,0:T(8,128)S(1)} %copy-done.4), channel_id=1, source_target_pairs={{0,26},{2,24},{4,30},{6,28},{8,18},{10,16},{12,22},{14,20},{16,10}... | collective-permute-start | bytes 786440 | tf_op jit(solution)/shard_map/ppermute | solution.py:517
  470.9 5.1 collective-permute-done.39.refs_10_
  476.5 13.4 %collective-permute-start.44 = (f32[2,1,256,128]{3,2,1,0:T(8,128)S(1)}, f32[2,1,256,128]{3,2,1,0:T(8,128)S(1)}, u32[]{:S(2)}, u32[]{:S(2)}) collective-permute-start(f32[2,1,256,128]{3,2,1,0:T(8,128)S(1)} %copy-done.1), channel_id=1, source_target_pairs={{0,30},{2,28},{4,26},{6,24},{8,22},{10,20},{12,18},{14,16},{16,14}... | collective-permute-start | bytes 786440 | tf_op jit(solution)/shard_map/ppermute | solution.py:517
  489.9 14.3 %shard_map.181.refs_16_ = f32[256,4096]{1,0:T(8,128)} custom-call(f32[2,1,256,128]{3,2,1,0:T(8,128)} %get-tuple-element.124.refs_0_, f32[2,1,256,128]{3,2,1,0:T(8,128)} %copy-done, f32[2,1,256,128]{3,2,1,0:T(8,128)} %copy-done.3, f32[2,1,256,128]{3,2,1,0:T(8,128)} %copy-done.7, f32[2,1,256,128]{3,2,1,0:T(8,128)} %copy-done.27, ...), custom_call_target="tpu_custom_call" | custom-call | flops 10000000000 | bytes 30000000 | tf_op jit(solution)/shard_map/pallas_call | solution.py:388
  504.3 6.1 %collective-permute-done.42.refs_13_ = f32[2,1,256,128]{3,2,1,0:T(8,128)S(1)} collective-permute-done((f32[2,1,256,128]{3,2,1,0:T(8,128)S(1)}, f32[2,1,256,128]{3,2,1,0:T(8,128)S(1)}, u32[]{:S(2)}, u32[]{:S(2)}) %collective-permute-start.42) | collective-permute-done | bytes 262176 | tf_op jit(solution)/shard_map/ppermute | solution.py:517
  510.4 6.1 %collective-permute-done.43.refs_14_ = f32[2,1,256,128]{3,2,1,0:T(8,128)S(1)} collective-permute-done((f32[2,1,256,128]{3,2,1,0:T(8,128)S(1)}, f32[2,1,256,128]{3,2,1,0:T(8,128)S(1)}, u32[]{:S(2)}, u32[]{:S(2)}) %collective-permute-start.43) | collective-permute-done | bytes 262176 | tf_op jit(solution)/shard_map/ppermute | solution.py:517
  516.5 7.4 %collective-permute-done.44.refs_15_ = f32[2,1,256,128]{3,2,1,0:T(8,128)S(1)} collective-permute-done((f32[2,1,256,128]{3,2,1,0:T(8,128)S(1)}, f32[2,1,256,128]{3,2,1,0:T(8,128)S(1)}, u32[]{:S(2)}, u32[]{:S(2)}) %collective-permute-start.44) | collective-permute-done | bytes 262176 | tf_op jit(solution)/shard_map/ppermute | solution.py:517
  524.6 13.6 %shard_map.182 = f32[256,4096]{1,0:T(8,128)} custom-call(f32[2,1,256,128]{3,2,1,0:T(8,128)} %get-tuple-element.108.refs_0_, f32[2,1,256,128]{3,2,1,0:T(8,128)} %copy-done.43, f32[2,1,256,128]{3,2,1,0:T(8,128)} %copy-done.46, f32[2,1,256,128]{3,2,1,0:T(8,128)} %copy-done.57, f32[2,1,256,128]{3,2,1,0:T(8,128)} %copy-done.59, f32[2,1,256,128]{3,2,1,0:T(8,128)} %copy-done.61, ...), custom_call_target="tpu_custom_call" | custom-call | flops 10000000000 | bytes 30000000 | tf_op jit(solution)/shard_map/pallas_call | solution.py:388
  (272 shorter events, 87.0 us)
Async XLA Ops:
  26.8 26.3 %collective-permute-start.20 = (f32[2,2,128,128]{3,2,1,0:T(8,128)}, f32[2,2,128,128]{3,2,1,0:T(8,128)S(1)}, u32[]{:S(2)}, u32[]{:S(2)}) collective-permute-start(f32[2,2,128,128]{3,2,1,0:T(8,128)} %get-tuple-element.97), channel_id=1, source_target_pairs={{0,12},{2,14},{4,8},{6,10},{8,4},{10,6},{12,0},{14,2},{16,28},{18,... | collective-permute-start | bytes 786440 | tf_op jit(solution)/shard_map/ppermute | solution.py:517
  28.8 40.2 %collective-permute-start.21 = (f32[2,2,128,128]{3,2,1,0:T(8,128)}, f32[2,2,128,128]{3,2,1,0:T(8,128)S(1)}, u32[]{:S(2)}, u32[]{:S(2)}) collective-permute-start(f32[2,2,128,128]{3,2,1,0:T(8,128)} %get-tuple-element.98), channel_id=1, source_target_pairs={{0,14},{2,12},{4,10},{6,8},{8,6},{10,4},{12,2},{14,0},{16,30},{18,... | collective-permute-start | bytes 786440 | tf_op jit(solution)/shard_map/ppermute | solution.py:517
  35.4 35.6 %collective-permute-start.22 = (f32[2,2,128,128]{3,2,1,0:T(8,128)}, f32[2,2,128,128]{3,2,1,0:T(8,128)}, u32[]{:S(2)}, u32[]{:S(2)}) collective-permute-start(f32[2,2,128,128]{3,2,1,0:T(8,128)} %get-tuple-element.99), channel_id=1, source_target_pairs={{0,16},{2,18},{4,20},{6,22},{8,24},{10,26},{12,28},{14,30},{16,0},... | collective-permute-start | bytes 786440 | tf_op jit(solution)/shard_map/ppermute | solution.py:517
  37.7 45.8 %collective-permute-start.23 = (f32[2,2,128,128]{3,2,1,0:T(8,128)}, f32[2,2,128,128]{3,2,1,0:T(8,128)}, u32[]{:S(2)}, u32[]{:S(2)}) collective-permute-start(f32[2,2,128,128]{3,2,1,0:T(8,128)} %get-tuple-element.100), channel_id=1, source_target_pairs={{0,18},{2,16},{4,22},{6,20},{8,26},{10,24},{12,30},{14,28},{16,2},... | collective-permute-start | bytes 786440 | tf_op jit(solution)/shard_map/ppermute | solution.py:517
  37.8 57.0 %collective-permute-start.24 = (f32[2,2,128,128]{3,2,1,0:T(8,128)}, f32[2,2,128,128]{3,2,1,0:T(8,128)}, u32[]{:S(2)}, u32[]{:S(2)}) collective-permute-start(f32[2,2,128,128]{3,2,1,0:T(8,128)} %get-tuple-element.101), channel_id=1, source_target_pairs={{0,20},{2,22},{4,16},{6,18},{8,28},{10,30},{12,24},{14,26},{16,4},... | collective-permute-start | bytes 786440 | tf_op jit(solution)/shard_map/ppermute | solution.py:517
  53.1 47.3 %collective-permute-start.25 = (f32[2,2,128,128]{3,2,1,0:T(8,128)}, f32[2,2,128,128]{3,2,1,0:T(8,128)}, u32[]{:S(2)}, u32[]{:S(2)}) collective-permute-start(f32[2,2,128,128]{3,2,1,0:T(8,128)} %get-tuple-element.102), channel_id=1, source_target_pairs={{0,22},{2,20},{4,18},{6,16},{8,30},{10,28},{12,26},{14,24},{16,6},... | collective-permute-start | bytes 786440 | tf_op jit(solution)/shard_map/ppermute | solution.py:517
  69.7 41.9 %collective-permute-start.26 = (f32[2,2,128,128]{3,2,1,0:T(8,128)}, f32[2,2,128,128]{3,2,1,0:T(8,128)S(1)}, u32[]{:S(2)}, u32[]{:S(2)}) collective-permute-start(f32[2,2,128,128]{3,2,1,0:T(8,128)} %get-tuple-element.103), channel_id=1, source_target_pairs={{0,24},{2,26},{4,28},{6,30},{8,16},{10,18},{12,20},{14,22},{16,8},... | collective-permute-start | bytes 786440 | tf_op jit(solution)/shard_map/ppermute | solution.py:517
  71.1 46.1 %collective-permute-start.27 = (f32[2,2,128,128]{3,2,1,0:T(8,128)S(1)}, f32[2,2,128,128]{3,2,1,0:T(8,128)S(1)}, u32[]{:S(2)}, u32[]{:S(2)}) collective-permute-start(f32[2,2,128,128]{3,2,1,0:T(8,128)S(1)} %copy-done.53), channel_id=1, source_target_pairs={{0,26},{2,24},{4,30},{6,28},{8,18},{10,16},{12,22},{14,20},{16,10}... | collective-permute-start | bytes 786440 | tf_op jit(solution)/shard_map/ppermute | solution.py:517
  83.6 67.4 %collective-permute-start.28 = (f32[2,2,128,128]{3,2,1,0:T(8,128)S(1)}, f32[2,2,128,128]{3,2,1,0:T(8,128)S(1)}, u32[]{:S(2)}, u32[]{:S(2)}) collective-permute-start(f32[2,2,128,128]{3,2,1,0:T(8,128)S(1)} %copy-done.52), channel_id=1, source_target_pairs={{0,28},{2,30},{4,24},{6,26},{8,20},{10,22},{12,16},{14,18},{16,12}... | collective-permute-start | bytes 786440 | tf_op jit(solution)/shard_map/ppermute | solution.py:517
  94.8 61.7 %collective-permute-start.29 = (f32[2,2,128,128]{3,2,1,0:T(8,128)S(1)}, f32[2,2,128,128]{3,2,1,0:T(8,128)S(1)}, u32[]{:S(2)}, u32[]{:S(2)}) collective-permute-start(f32[2,2,128,128]{3,2,1,0:T(8,128)S(1)} %copy-done.50), channel_id=1, source_target_pairs={{0,30},{2,28},{4,26},{6,24},{8,22},{10,20},{12,18},{14,16},{16,14}... | collective-permute-start | bytes 786440 | tf_op jit(solution)/shard_map/ppermute | solution.py:517
  100.4 58.6 %collective-permute-start = (f32[2,2,128,128]{3,2,1,0:T(8,128)}, f32[2,2,128,128]{3,2,1,0:T(8,128)S(1)}, u32[]{:S(2)}, u32[]{:S(2)}) collective-permute-start(f32[2,2,128,128]{3,2,1,0:T(8,128)} %get-tuple-element.76), channel_id=1, source_target_pairs={{0,2},{2,0},{4,6},{6,4},{8,10},{10,8},{12,14},{14,12},{16,18},{18,... | collective-permute-start | bytes 786440 | tf_op jit(solution)/shard_map/ppermute | solution.py:517
  111.6 48.7 %collective-permute-start.1 = (f32[2,2,128,128]{3,2,1,0:T(8,128)}, f32[2,2,128,128]{3,2,1,0:T(8,128)S(1)}, u32[]{:S(2)}, u32[]{:S(2)}) collective-permute-start(f32[2,2,128,128]{3,2,1,0:T(8,128)} %get-tuple-element.77), channel_id=1, source_target_pairs={{0,4},{2,6},{4,0},{6,2},{8,12},{10,14},{12,8},{14,10},{16,20},{18,... | collective-permute-start | bytes 786440 | tf_op jit(solution)/shard_map/ppermute | solution.py:517
  117.2 45.5 %collective-permute-start.10 = (f32[2,2,128,128]{3,2,1,0:T(8,128)}, f32[2,2,128,128]{3,2,1,0:T(8,128)S(1)}, u32[]{:S(2)}, u32[]{:S(2)}) collective-permute-start(f32[2,2,128,128]{3,2,1,0:T(8,128)} %get-tuple-element.86), channel_id=1, source_target_pairs={{0,22},{2,20},{4,18},{6,16},{8,30},{10,28},{12,26},{14,24},{16,6},... | collective-permute-start | bytes 786440 | tf_op jit(solution)/shard_map/ppermute | solution.py:517
  160.4 24.4 %collective-permute-start.14 = (f32[2,2,128,128]{3,2,1,0:T(8,128)}, f32[2,2,128,128]{3,2,1,0:T(8,128)S(1)}, u32[]{:S(2)}, u32[]{:S(2)}) collective-permute-start(f32[2,2,128,128]{3,2,1,0:T(8,128)} %get-tuple-element.90), channel_id=1, source_target_pairs={{0,30},{2,28},{4,26},{6,24},{8,22},{10,20},{12,18},{14,16},{16,14}... | collective-permute-start | bytes 786440 | tf_op jit(solution)/shard_map/ppermute | solution.py:517
  167.9 22.4 %collective-permute-start.3 = (f32[2,2,128,128]{3,2,1,0:T(8,128)}, f32[2,2,128,128]{3,2,1,0:T(8,128)S(1)}, u32[]{:S(2)}, u32[]{:S(2)}) collective-permute-start(f32[2,2,128,128]{3,2,1,0:T(8,128)} %get-tuple-element.79), channel_id=1, source_target_pairs={{0,8},{2,10},{4,12},{6,14},{8,0},{10,2},{12,4},{14,6},{16,24},{18,... | collective-permute-start | bytes 786440 | tf_op jit(solution)/shard_map/ppermute | solution.py:517
  184.7 42.8 %collective-permute-start.6 = (f32[2,2,128,128]{3,2,1,0:T(8,128)S(1)}, f32[2,2,128,128]{3,2,1,0:T(8,128)}, u32[]{:S(2)}, u32[]{:S(2)}) collective-permute-start(f32[2,2,128,128]{3,2,1,0:T(8,128)S(1)} %copy-done.37), channel_id=1, source_target_pairs={{0,14},{2,12},{4,10},{6,8},{8,6},{10,4},{12,2},{14,0},{16,30},{18,... | collective-permute-start | bytes 786440 | tf_op jit(solution)/shard_map/ppermute | solution.py:517
  184.8 45.8 %collective-permute-start.7 = (f32[2,2,128,128]{3,2,1,0:T(8,128)S(1)}, f32[2,2,128,128]{3,2,1,0:T(8,128)}, u32[]{:S(2)}, u32[]{:S(2)}) collective-permute-start(f32[2,2,128,128]{3,2,1,0:T(8,128)S(1)} %copy-done.35), channel_id=1, source_target_pairs={{0,16},{2,18},{4,20},{6,22},{8,24},{10,26},{12,28},{14,30},{16,0},... | collective-permute-start | bytes 786440 | tf_op jit(solution)/shard_map/ppermute | solution.py:517
  190.3 40.9 %collective-permute-start.8 = (f32[2,2,128,128]{3,2,1,0:T(8,128)S(1)}, f32[2,2,128,128]{3,2,1,0:T(8,128)}, u32[]{:S(2)}, u32[]{:S(2)}) collective-permute-start(f32[2,2,128,128]{3,2,1,0:T(8,128)S(1)} %copy-done.33), channel_id=1, source_target_pairs={{0,18},{2,16},{4,22},{6,20},{8,26},{10,24},{12,30},{14,28},{16,2},... | collective-permute-start | bytes 786440 | tf_op jit(solution)/shard_map/ppermute | solution.py:517
  190.4 41.3 %collective-permute-start.9 = (f32[2,2,128,128]{3,2,1,0:T(8,128)S(1)}, f32[2,2,128,128]{3,2,1,0:T(8,128)}, u32[]{:S(2)}, u32[]{:S(2)}) collective-permute-start(f32[2,2,128,128]{3,2,1,0:T(8,128)S(1)} %copy-done.32), channel_id=1, source_target_pairs={{0,20},{2,22},{4,16},{6,18},{8,28},{10,30},{12,24},{14,26},{16,4},... | collective-permute-start | bytes 786440 | tf_op jit(solution)/shard_map/ppermute | solution.py:517
  192.7 120.9 %collective-permute-start.60 = (f32[136,4096]{1,0:T(8,128)S(1)}, f32[136,4096]{1,0:T(8,128)}, u32[]{:S(2)}, u32[]{:S(2)}) collective-permute-start(f32[136,4096]{1,0:T(8,128)S(1)} %dynamic-slice_bitcast_fusion), channel_id=1, source_target_pairs={{0,1},{1,0},{2,3},{3,2},{4,5},{5,4},{6,7},{7,6},{8,9},{9,8},{10,11... | collective-permute-start | bytes 6684680 | tf_op jit(solution)/shard_map/ppermute | solution.py:498
  227.6 38.8 %collective-permute-start.61 = (f32[8,4096]{1,0:T(8,128)S(1)}, f32[8,4096]{1,0:T(8,128)S(1)}, u32[]{:S(2)}, u32[]{:S(2)}) collective-permute-start(f32[8,4096]{1,0:T(8,128)S(1)} %get-tuple-element.152), channel_id=1, source_target_pairs={{0,2},{2,4},{4,6},{6,8},{8,10},{10,12},{12,14},{14,16},{16,18},{18... | collective-permute-start | bytes 393224 | tf_op jit(solution)/shard_map/ppermute | solution.py:538
  230.6 70.9 %collective-permute-start.45 = (f32[2,1,256,128]{3,2,1,0:T(8,128)}, f32[2,1,256,128]{3,2,1,0:T(8,128)S(1)}, u32[]{:S(2)}, u32[]{:S(2)}) collective-permute-start(f32[2,1,256,128]{3,2,1,0:T(8,128)} %get-tuple-element.125), channel_id=1, source_target_pairs={{0,2},{2,0},{4,6},{6,4},{8,10},{10,8},{12,14},{14,12},{16,18},{18,... | collective-permute-start | bytes 786440 | tf_op jit(solution)/shard_map/ppermute | solution.py:517
  231.1 79.6 %collective-permute-start.46 = (f32[2,1,256,128]{3,2,1,0:T(8,128)}, f32[2,1,256,128]{3,2,1,0:T(8,128)S(1)}, u32[]{:S(2)}, u32[]{:S(2)}) collective-permute-start(f32[2,1,256,128]{3,2,1,0:T(8,128)} %get-tuple-element.126), channel_id=1, source_target_pairs={{0,4},{2,6},{4,0},{6,2},{8,12},{10,14},{12,8},{14,10},{16,20},{18,... | collective-permute-start | bytes 786440 | tf_op jit(solution)/shard_map/ppermute | solution.py:517
  231.7 80.2 %collective-permute-start.47 = (f32[2,1,256,128]{3,2,1,0:T(8,128)}, f32[2,1,256,128]{3,2,1,0:T(8,128)S(1)}, u32[]{:S(2)}, u32[]{:S(2)}) collective-permute-start(f32[2,1,256,128]{3,2,1,0:T(8,128)} %get-tuple-element.127), channel_id=1, source_target_pairs={{0,6},{2,4},{4,2},{6,0},{8,14},{10,12},{12,10},{14,8},{16,22},{18,... | collective-permute-start | bytes 786440 | tf_op jit(solution)/shard_map/ppermute | solution.py:517
  297.9 35.2 %collective-permute-start.48 = (f32[2,1,256,128]{3,2,1,0:T(8,128)}, f32[2,1,256,128]{3,2,1,0:T(8,128)S(1)}, u32[]{:S(2)}, u32[]{:S(2)}) collective-permute-start(f32[2,1,256,128]{3,2,1,0:T(8,128)} %get-tuple-element.128), channel_id=1, source_target_pairs={{0,8},{2,10},{4,12},{6,14},{8,0},{10,2},{12,4},{14,6},{16,24},{18,... | collective-permute-start | bytes 786440 | tf_op jit(solution)/shard_map/ppermute | solution.py:517
  301.5 34.0 %collective-permute-start.49 = (f32[2,1,256,128]{3,2,1,0:T(8,128)}, f32[2,1,256,128]{3,2,1,0:T(8,128)S(1)}, u32[]{:S(2)}, u32[]{:S(2)}) collective-permute-start(f32[2,1,256,128]{3,2,1,0:T(8,128)} %get-tuple-element.129), channel_id=1, source_target_pairs={{0,10},{2,8},{4,14},{6,12},{8,2},{10,0},{12,6},{14,4},{16,26},{18,... | collective-permute-start | bytes 786440 | tf_op jit(solution)/shard_map/ppermute | solution.py:517
  310.7 25.0 %collective-permute-start.50 = (f32[2,1,256,128]{3,2,1,0:T(8,128)}, f32[2,1,256,128]{3,2,1,0:T(8,128)}, u32[]{:S(2)}, u32[]{:S(2)}) collective-permute-start(f32[2,1,256,128]{3,2,1,0:T(8,128)} %get-tuple-element.130), channel_id=1, source_target_pairs={{0,12},{2,14},{4,8},{6,10},{8,4},{10,6},{12,0},{14,2},{16,28},{18,... | collective-permute-start | bytes 786440 | tf_op jit(solution)/shard_map/ppermute | solution.py:517
  311.8 27.5 %collective-permute-start.51 = (f32[2,1,256,128]{3,2,1,0:T(8,128)}, f32[2,1,256,128]{3,2,1,0:T(8,128)}, u32[]{:S(2)}, u32[]{:S(2)}) collective-permute-start(f32[2,1,256,128]{3,2,1,0:T(8,128)} %get-tuple-element.131), channel_id=1, source_target_pairs={{0,14},{2,12},{4,10},{6,8},{8,6},{10,4},{12,2},{14,0},{16,30},{18,... | collective-permute-start | bytes 786440 | tf_op jit(solution)/shard_map/ppermute | solution.py:517
  313.7 26.0 %collective-permute-start.52 = (f32[2,1,256,128]{3,2,1,0:T(8,128)}, f32[2,1,256,128]{3,2,1,0:T(8,128)S(1)}, u32[]{:S(2)}, u32[]{:S(2)}) collective-permute-start(f32[2,1,256,128]{3,2,1,0:T(8,128)} %get-tuple-element.132), channel_id=1, source_target_pairs={{0,16},{2,18},{4,20},{6,22},{8,24},{10,26},{12,28},{14,30},{16,0},... | collective-permute-start | bytes 786440 | tf_op jit(solution)/shard_map/ppermute | solution.py:517
  333.2 37.2 %collective-permute-start.53 = (f32[2,1,256,128]{3,2,1,0:T(8,128)}, f32[2,1,256,128]{3,2,1,0:T(8,128)S(1)}, u32[]{:S(2)}, u32[]{:S(2)}) collective-permute-start(f32[2,1,256,128]{3,2,1,0:T(8,128)} %get-tuple-element.133), channel_id=1, source_target_pairs={{0,18},{2,16},{4,22},{6,20},{8,26},{10,24},{12,30},{14,28},{16,2},... | collective-permute-start | bytes 786440 | tf_op jit(solution)/shard_map/ppermute | solution.py:517
  335.5 46.1 %collective-permute-start.54 = (f32[2,1,256,128]{3,2,1,0:T(8,128)}, f32[2,1,256,128]{3,2,1,0:T(8,128)}, u32[]{:S(2)}, u32[]{:S(2)}) collective-permute-start(f32[2,1,256,128]{3,2,1,0:T(8,128)} %get-tuple-element.134), channel_id=1, source_target_pairs={{0,20},{2,22},{4,16},{6,18},{8,28},{10,30},{12,24},{14,26},{16,4},... | collective-permute-start | bytes 786440 | tf_op jit(solution)/shard_map/ppermute | solution.py:517
  335.7 51.4 %collective-permute-start.55 = (f32[2,1,256,128]{3,2,1,0:T(8,128)S(1)}, f32[2,1,256,128]{3,2,1,0:T(8,128)}, u32[]{:S(2)}, u32[]{:S(2)}) collective-permute-start(f32[2,1,256,128]{3,2,1,0:T(8,128)S(1)} %copy-done.29), channel_id=1, source_target_pairs={{0,22},{2,20},{4,18},{6,16},{8,30},{10,28},{12,26},{14,24},{16,6},... | collective-permute-start | bytes 786440 | tf_op jit(solution)/shard_map/ppermute | solution.py:517
  339.4 59.7 %collective-permute-start.56 = (f32[2,1,256,128]{3,2,1,0:T(8,128)S(1)}, f32[2,1,256,128]{3,2,1,0:T(8,128)}, u32[]{:S(2)}, u32[]{:S(2)}) collective-permute-start(f32[2,1,256,128]{3,2,1,0:T(8,128)S(1)} %copy-done.26), channel_id=1, source_target_pairs={{0,24},{2,26},{4,28},{6,30},{8,16},{10,18},{12,20},{14,22},{16,8},... | collective-permute-start | bytes 786440 | tf_op jit(solution)/shard_map/ppermute | solution.py:517
  339.7 65.0 %collective-permute-start.57 = (f32[2,1,256,128]{3,2,1,0:T(8,128)S(1)}, f32[2,1,256,128]{3,2,1,0:T(8,128)}, u32[]{:S(2)}, u32[]{:S(2)}) collective-permute-start(f32[2,1,256,128]{3,2,1,0:T(8,128)S(1)} %copy-done.23), channel_id=1, source_target_pairs={{0,26},{2,24},{4,30},{6,28},{8,18},{10,16},{12,22},{14,20},{16,10}... | collective-permute-start | bytes 786440 | tf_op jit(solution)/shard_map/ppermute | solution.py:517
  370.4 39.3 %collective-permute-start.58 = (f32[2,1,256,128]{3,2,1,0:T(8,128)S(1)}, f32[2,1,256,128]{3,2,1,0:T(8,128)S(1)}, u32[]{:S(2)}, u32[]{:S(2)}) collective-permute-start(f32[2,1,256,128]{3,2,1,0:T(8,128)S(1)} %copy-done.14), channel_id=1, source_target_pairs={{0,28},{2,30},{4,24},{6,26},{8,20},{10,22},{12,16},{14,18},{16,12}... | collective-permute-start | bytes 786440 | tf_op jit(solution)/shard_map/ppermute | solution.py:517
  381.6 33.6 %collective-permute-start.59 = (f32[2,1,256,128]{3,2,1,0:T(8,128)S(1)}, f32[2,1,256,128]{3,2,1,0:T(8,128)}, u32[]{:S(2)}, u32[]{:S(2)}) collective-permute-start(f32[2,1,256,128]{3,2,1,0:T(8,128)S(1)} %copy-done.12), channel_id=1, source_target_pairs={{0,30},{2,28},{4,26},{6,24},{8,22},{10,20},{12,18},{14,16},{16,14}... | collective-permute-start | bytes 786440 | tf_op jit(solution)/shard_map/ppermute | solution.py:517
  387.2 28.1 %collective-permute-start.30 = (f32[2,1,256,128]{3,2,1,0:T(8,128)S(1)}, f32[2,1,256,128]{3,2,1,0:T(8,128)S(1)}, u32[]{:S(2)}, u32[]{:S(2)}) collective-permute-start(f32[2,1,256,128]{3,2,1,0:T(8,128)S(1)} %copy-done.24), channel_id=1, source_target_pairs={{0,2},{2,0},{4,6},{6,4},{8,10},{10,8},{12,14},{14,12},{16,18},{18,... | collective-permute-start | bytes 786440 | tf_op jit(solution)/shard_map/ppermute | solution.py:517
  404.6 71.8 %collective-permute-start.65 = (f32[128,4096]{1,0:T(8,128)}, f32[128,4096]{1,0:T(8,128)}, u32[]{:S(2)}, u32[]{:S(2)}) collective-permute-start(f32[128,4096]{1,0:T(8,128)} %get-tuple-element.143), channel_id=1, source_target_pairs={{0,1},{1,0},{2,3},{3,2},{4,5},{5,4},{6,7},{7,6},{8,9},{9,8},{10,11... | collective-permute-start | bytes 6291464 | tf_op jit(solution)/shard_map/ppermute | solution.py:498
  417.8 24.8 %collective-permute-start.35 = (f32[2,1,256,128]{3,2,1,0:T(8,128)S(1)}, f32[2,1,256,128]{3,2,1,0:T(8,128)S(1)}, u32[]{:S(2)}, u32[]{:S(2)}) collective-permute-start(f32[2,1,256,128]{3,2,1,0:T(8,128)S(1)} %copy-done.15), channel_id=1, source_target_pairs={{0,12},{2,14},{4,8},{6,10},{8,4},{10,6},{12,0},{14,2},{16,28},{18,... | collective-permute-start | bytes 786440 | tf_op jit(solution)/shard_map/ppermute | solution.py:517
  424.3 25.0 %collective-permute-start.36 = (f32[2,1,256,128]{3,2,1,0:T(8,128)S(1)}, f32[2,1,256,128]{3,2,1,0:T(8,128)S(1)}, u32[]{:S(2)}, u32[]{:S(2)}) collective-permute-start(f32[2,1,256,128]{3,2,1,0:T(8,128)S(1)} %copy-done.11), channel_id=1, source_target_pairs={{0,14},{2,12},{4,10},{6,8},{8,6},{10,4},{12,2},{14,0},{16,30},{18,... | collective-permute-start | bytes 786440 | tf_op jit(solution)/shard_map/ppermute | solution.py:517
  426.8 25.2 %collective-permute-start.37 = (f32[2,1,256,128]{3,2,1,0:T(8,128)S(1)}, f32[2,1,256,128]{3,2,1,0:T(8,128)S(1)}, u32[]{:S(2)}, u32[]{:S(2)}) collective-permute-start(f32[2,1,256,128]{3,2,1,0:T(8,128)S(1)} %copy-done.10), channel_id=1, source_target_pairs={{0,16},{2,18},{4,20},{6,22},{8,24},{10,26},{12,28},{14,30},{16,0},... | collective-permute-start | bytes 786440 | tf_op jit(solution)/shard_map/ppermute | solution.py:517
  430.3 23.9 %collective-permute-start.38 = (f32[2,1,256,128]{3,2,1,0:T(8,128)S(1)}, f32[2,1,256,128]{3,2,1,0:T(8,128)S(1)}, u32[]{:S(2)}, u32[]{:S(2)}) collective-permute-start(f32[2,1,256,128]{3,2,1,0:T(8,128)S(1)} %copy-done.9), channel_id=1, source_target_pairs={{0,18},{2,16},{4,22},{6,20},{8,26},{10,24},{12,30},{14,28},{16,2},... | collective-permute-start | bytes 786440 | tf_op jit(solution)/shard_map/ppermute | solution.py:517
  442.6 33.4 %collective-permute-start.39 = (f32[2,1,256,128]{3,2,1,0:T(8,128)S(1)}, f32[2,1,256,128]{3,2,1,0:T(8,128)S(1)}, u32[]{:S(2)}, u32[]{:S(2)}) collective-permute-start(f32[2,1,256,128]{3,2,1,0:T(8,128)S(1)} %copy-done.8), channel_id=1, source_target_pairs={{0,20},{2,22},{4,16},{6,18},{8,28},{10,30},{12,24},{14,26},{16,4},... | collective-permute-start | bytes 786440 | tf_op jit(solution)/shard_map/ppermute | solution.py:517
  449.3 55.0 %collective-permute-start.40 = (f32[2,1,256,128]{3,2,1,0:T(8,128)S(1)}, f32[2,1,256,128]{3,2,1,0:T(8,128)S(1)}, u32[]{:S(2)}, u32[]{:S(2)}) collective-permute-start(f32[2,1,256,128]{3,2,1,0:T(8,128)S(1)} %copy-done.6), channel_id=1, source_target_pairs={{0,22},{2,20},{4,18},{6,16},{8,30},{10,28},{12,26},{14,24},{16,6},... | collective-permute-start | bytes 786440 | tf_op jit(solution)/shard_map/ppermute | solution.py:517
  452.0 52.3 %collective-permute-start.41 = (f32[2,1,256,128]{3,2,1,0:T(8,128)S(1)}, f32[2,1,256,128]{3,2,1,0:T(8,128)S(1)}, u32[]{:S(2)}, u32[]{:S(2)}) collective-permute-start(f32[2,1,256,128]{3,2,1,0:T(8,128)S(1)} %copy-done.5), channel_id=1, source_target_pairs={{0,24},{2,26},{4,28},{6,30},{8,16},{10,18},{12,20},{14,22},{16,8},... | collective-permute-start | bytes 786440 | tf_op jit(solution)/shard_map/ppermute | solution.py:517
  454.2 56.2 %collective-permute-start.42 = (f32[2,1,256,128]{3,2,1,0:T(8,128)S(1)}, f32[2,1,256,128]{3,2,1,0:T(8,128)S(1)}, u32[]{:S(2)}, u32[]{:S(2)}) collective-permute-start(f32[2,1,256,128]{3,2,1,0:T(8,128)S(1)} %copy-done.4), channel_id=1, source_target_pairs={{0,26},{2,24},{4,30},{6,28},{8,18},{10,16},{12,22},{14,20},{16,10}... | collective-permute-start | bytes 786440 | tf_op jit(solution)/shard_map/ppermute | solution.py:517
  476.0 40.5 %collective-permute-start.43 = (f32[2,1,256,128]{3,2,1,0:T(8,128)S(1)}, f32[2,1,256,128]{3,2,1,0:T(8,128)S(1)}, u32[]{:S(2)}, u32[]{:S(2)}) collective-permute-start(f32[2,1,256,128]{3,2,1,0:T(8,128)S(1)} %copy-done.2), channel_id=1, source_target_pairs={{0,28},{2,30},{4,24},{6,26},{8,20},{10,22},{12,16},{14,18},{16,12}... | collective-permute-start | bytes 786440 | tf_op jit(solution)/shard_map/ppermute | solution.py:517
  476.5 47.4 %collective-permute-start.44 = (f32[2,1,256,128]{3,2,1,0:T(8,128)S(1)}, f32[2,1,256,128]{3,2,1,0:T(8,128)S(1)}, u32[]{:S(2)}, u32[]{:S(2)}) collective-permute-start(f32[2,1,256,128]{3,2,1,0:T(8,128)S(1)} %copy-done.1), channel_id=1, source_target_pairs={{0,30},{2,28},{4,26},{6,24},{8,22},{10,20},{12,18},{14,16},{16,14}... | collective-permute-start | bytes 786440 | tf_op jit(solution)/shard_map/ppermute | solution.py:517
  (102 other events, 2599.6 us)

commit v4 on v3

--- a/solution.py
+++ b/solution.py
@@ -162,7 +162,7 @@
                     store(p, at, lanes, re * wr + im * wi, im * wr - re * wi)
         return carry
 
-    lax.fori_loop(low // 8, high // 8, body, 0)
+    lax.fori_loop(low // 8, high // 8, body, 0, unroll=2)
 
 
 def lane_tiles(width):
@@ -498,7 +498,7 @@
     return lax.ppermute(value, "chan", [(i, (i + 1) % size) for i in range(size)])
 
 
-UNROLL = 2
+UNROLL = 4
 SKY_PARTS = 4
 
 
@@ -521,8 +521,11 @@
 def row_total(value):
     size = lax.axis_size("row")
     away = lambda v, d: lax.ppermute(v, "row", [(i, i ^ d) for i in range(size)])
-    value = value + away(value, 1)
-    return value + sum(away(value, d) for d in range(2, size, 2))
+    step = 1
+    while step < size // 4:
+        value = value + away(value, step)
+        step *= 2
+    return value + (away(value, step) + away(value, 2 * step)) + away(value, 3 * step)
 
 
 def edges_of(sky):

time: 540 us -> 532 us (0.985)
  starting transfers between devices: 118 us -> 132 us
  waiting for transfers between devices: 245 us -> 232 us
  Pallas kernels: 153 us -> 146 us
    ppermute x60, starting transfers between devices: 105 us -> 114 us  [row_exchange(): got[d] = lax.ppermute(pieces[d], 'row', [(i, i ^ d) for i in range(size)])]
    pallas_call x8, Pallas kernels: 153 us -> 146 us  [call(): pl.pallas_call(kernel, grid=(1,), in_specs=specs, out_specs=out_specs, ou...]
    ppermute x60, waiting for transfers between devices: 216 us -> 210 us  [row_exchange(): got[d] = lax.ppermute(pieces[d], 'row', [(i, i ^ d) for i in range(size)])]
    ppermute x8 -> x5, waiting for transfers between devices: 21.9 us -> 17.5 us  [row_total(): lax.ppermute(v, 'row', [(i, i ^ d) for i in range(size)])]
  transfers between devices with their start and end apart: 74 -> 71, of which waited for: 40 -> 33; matrix products, arithmetic and copies ran while one was open for 3% -> 3% of each run, Pallas kernels for 24% -> 23%
where the time goes in v4:
time: 532 us; the launch traced here: 529 us
  waiting for transfers between devices  232 us (44%)
  Pallas kernels  146 us (27%)
  starting transfers between devices  132 us (25%)
  other arithmetic  10.6 us (2%)
    ppermute x60, waiting for transfers between devices, row_exchange(): got[d] = lax.ppermute(pieces[d], 'row', [(i, i ^ d) for i in range(size)])  210 us
    pallas_call x8, Pallas kernels, call(): pl.pallas_call(kernel, grid=(1,), in_specs=specs, out_specs=out_specs, ou...  146 us
    ppermute x60, starting transfers between devices, row_exchange(): got[d] = lax.ppermute(pieces[d], 'row', [(i, i ^ d) for i in range(size)])  114 us
    ppermute x5, waiting for transfers between devices, row_total(): lax.ppermute(v, 'row', [(i, i ^ d) for i in range(size)])  17.5 us
  transfers between devices with their start and end apart: 71, of which 33 were waited for; matrix products, arithmetic and copies ran while one was open for 3% of the time, Pallas kernels for 23%

profile of v4, /device:TPU:15, one launch (start us, length us, event | category | flops | bytes accessed | tf_op | source)
XLA Modules:
  0.0 529.0 jit_solution(691350205939426942)
XLA Ops:
  0.6 11.6 %shard_map.176 = (f32[2,2,128,128]{3,2,1,0:T(8,128)}, f32[2,2,128,128]{3,2,1,0:T(8,128)}, f32[2,2,128,128]{3,2,1,0:T(8,128)}, f32[2,2,128,128]{3,2,1,0:T(8,128)}...) custom-call(f32[256,4096]{1,0:T(8,128)} %bitcast.15, ...), custom_call_target="tpu_custom_call" | custom-call | flops 10000000000 | bytes 10000000 | tf_op jit(solution)/shard_map/pallas_call | solution.py:388
  16.4 11.5 %shard_map.175 = (f32[2,2,128,128]{3,2,1,0:T(8,128)}, f32[2,2,128,128]{3,2,1,0:T(8,128)}, f32[2,2,128,128]{3,2,1,0:T(8,128)}, f32[2,2,128,128]{3,2,1,0:T(8,128)}...) custom-call(f32[256,4096]{1,0:T(8,128)} %bitcast.16, ...), custom_call_target="tpu_custom_call" | custom-call | flops 10000000000 | bytes 10000000 | tf_op jit(solution)/shard_map/pallas_call | solution.py:388
  30.4 2.5 collective-permute-start.21
  38.0 10.0 %collective-permute-start.25 = (f32[2,2,128,128]{3,2,1,0:T(8,128)}, f32[2,2,128,128]{3,2,1,0:T(8,128)}, u32[]{:S(2)}, u32[]{:S(2)}) collective-permute-start(f32[2,2,128,128]{3,2,1,0:T(8,128)} %get-tuple-element.102), channel_id=1, source_target_pairs={{0,22},{2,20},{4,18},{6,16},{8,30},{10,28},{12,26},{14,24},{16,6},... | collective-permute-start | bytes 786440 | tf_op jit(solution)/shard_map/ppermute | solution.py:517
  52.0 28.5 %collective-permute-done.23.refs_9_ = f32[2,2,128,128]{3,2,1,0:T(8,128)S(1)} collective-permute-done((f32[2,2,128,128]{3,2,1,0:T(8,128)}, f32[2,2,128,128]{3,2,1,0:T(8,128)S(1)}, u32[]{:S(2)}, u32[]{:S(2)}) %collective-permute-start.23) | collective-permute-done | bytes 262176 | tf_op jit(solution)/shard_map/ppermute | solution.py:517
  80.4 5.6 %collective-permute-done.24.refs_10_ = f32[2,2,128,128]{3,2,1,0:T(8,128)S(1)} collective-permute-done((f32[2,2,128,128]{3,2,1,0:T(8,128)}, f32[2,2,128,128]{3,2,1,0:T(8,128)S(1)}, u32[]{:S(2)}, u32[]{:S(2)}) %collective-permute-start.24) | collective-permute-done | bytes 262176 | tf_op jit(solution)/shard_map/ppermute | solution.py:517
  86.4 16.5 %collective-permute-done.25.refs_11_ = f32[2,2,128,128]{3,2,1,0:T(8,128)} collective-permute-done((f32[2,2,128,128]{3,2,1,0:T(8,128)}, f32[2,2,128,128]{3,2,1,0:T(8,128)}, u32[]{:S(2)}, u32[]{:S(2)}) %collective-permute-start.25) | collective-permute-done | bytes 262176 | tf_op jit(solution)/shard_map/ppermute | solution.py:517
  108.8 6.2 %collective-permute-done.27.refs_13_ = f32[2,2,128,128]{3,2,1,0:T(8,128)S(1)} collective-permute-done((f32[2,2,128,128]{3,2,1,0:T(8,128)}, f32[2,2,128,128]{3,2,1,0:T(8,128)S(1)}, u32[]{:S(2)}, u32[]{:S(2)}) %collective-permute-start.27) | collective-permute-done | bytes 262176 | tf_op jit(solution)/shard_map/ppermute | solution.py:517
  115.0 32.9 %collective-permute-done.28.refs_14_ = f32[2,2,128,128]{3,2,1,0:T(8,128)S(1)} collective-permute-done((f32[2,2,128,128]{3,2,1,0:T(8,128)}, f32[2,2,128,128]{3,2,1,0:T(8,128)S(1)}, u32[]{:S(2)}, u32[]{:S(2)}) %collective-permute-start.28) | collective-permute-done | bytes 262176 | tf_op jit(solution)/shard_map/ppermute | solution.py:517
  149.9 4.1 collective-permute-done.29.refs_15_
  160.8 3.9 collective-permute-done.11.refs_12_
  164.6 6.6 %collective-permute-done.12.refs_13_ = f32[2,2,128,128]{3,2,1,0:T(8,128)S(1)} collective-permute-done((f32[2,2,128,128]{3,2,1,0:T(8,128)S(1)}, f32[2,2,128,128]{3,2,1,0:T(8,128)S(1)}, u32[]{:S(2)}, u32[]{:S(2)}) %collective-permute-start.12) | collective-permute-done | bytes 262176 | tf_op jit(solution)/shard_map/ppermute | solution.py:517
  171.2 4.6 collective-permute-done.13.refs_14_
  175.9 7.4 %collective-permute-done.14.refs_15_ = f32[2,2,128,128]{3,2,1,0:T(8,128)S(1)} collective-permute-done((f32[2,2,128,128]{3,2,1,0:T(8,128)S(1)}, f32[2,2,128,128]{3,2,1,0:T(8,128)S(1)}, u32[]{:S(2)}, u32[]{:S(2)}) %collective-permute-start.14) | collective-permute-done | bytes 262176 | tf_op jit(solution)/shard_map/ppermute | solution.py:517
  183.4 4.7 collective-permute-start.7
  189.1 2.6 collective-permute-start.9
  193.1 32.0 %shard_map.177 = (f32[2,1,128,4096]{3,2,1,0:T(8,128)}, f32[2,8,128]{2,1,0:T(8,128)}, f32[2,1,256,128]{3,2,1,0:T(8,128)}, f32[2,1,256,128]{3,2,1,0:T(8,128)}, f32...) custom-call(f32[2,2,128,128]{3,2,1,0:T(8,128)} %get-tuple-element.91, ...), custom_call_target="tpu_custom_call" | custom-call | flops 20000000000 | bytes 30000000 | tf_op jit(solution)/shard_map/pallas_call | solution.py:388
  229.3 3.3 collective-permute-start.64
  232.6 32.1 %shard_map.178 = (f32[2,1,128,4096]{3,2,1,0:T(8,128)}, f32[2,8,128]{2,1,0:T(8,128)}, f32[2,1,256,128]{3,2,1,0:T(8,128)}, f32[2,1,256,128]{3,2,1,0:T(8,128)}, f32...) custom-call(f32[2,2,128,128]{3,2,1,0:T(8,128)} %get-tuple-element.75, ...), custom_call_target="tpu_custom_call" | custom-call | flops 20000000000 | bytes 30000000 | tf_op jit(solution)/shard_map/pallas_call | solution.py:388
  270.3 9.9 %collective-permute-done.67 = f32[2,8,128]{2,1,0:T(8,128)S(1)} collective-permute-done((f32[2,8,128]{2,1,0:T(8,128)S(1)}, f32[2,8,128]{2,1,0:T(8,128)S(1)}, u32[]{:S(2)}, u32[]{:S(2)}) %collective-permute-start.67) | collective-permute-done | bytes 8224 | tf_op jit(solution)/shard_map/ppermute | solution.py:523
  280.3 3.9 collective-permute-start.62
  284.2 4.3 collective-permute-done.62.edge_other
  291.0 3.3 collective-permute-done.69
  297.2 2.9 collective-permute-start.48
  300.1 2.8 collective-permute-start.49
  306.0 19.4 %shard_map.179 = (f32[2,128,4096]{2,1,0:T(8,128)}, f32[2,2,8,4096]{3,2,1,0:T(8,128)}) custom-call(f32[256,4096]{1,0:T(8,128)} %bitcast.17, f32[136,4096]{1,0:T(8,128)} %collective-permute-done.60.other, f32[8,4096]{1,0:T(8,128)} %copy-done.72, f32[8,4096]{1,0:T(8,128)} %copy-done.73, f32[2,128,4096]{2,1,0:T(8,128)} %dual.1, f32[3,2,4096]{2,1,0:T(2,128)} %copy-done.74, ...), custom_call_target="tpu_custom_call" | custom-call | flops 10000000000 | bytes 30000000 | tf_op jit(solution)/shard_map/pallas_call | solution.py:388
  325.4 2.4 collective-permute-start.53
  327.8 2.4 collective-permute-start.54
  333.2 14.4 %shard_map.180 = (f32[128,4096]{1,0:T(8,128)}, f32[128,4096]{1,0:T(8,128)}) custom-call(f32[2,128,4096]{2,1,0:T(8,128)} %get-tuple-element.74.wave, f32[2,2,8,4096]{3,2,1,0:T(8,128)} %get-tuple-element.141.outside), custom_call_target="tpu_custom_call" | custom-call | flops 10000000000 | bytes 30000000 | tf_op jit(solution)/shard_map/pallas_call | solution.py:388
  347.6 15.0 %collective-permute-done.53.refs_9_ = f32[2,1,256,128]{3,2,1,0:T(8,128)S(1)} collective-permute-done((f32[2,1,256,128]{3,2,1,0:T(8,128)S(1)}, f32[2,1,256,128]{3,2,1,0:T(8,128)S(1)}, u32[]{:S(2)}, u32[]{:S(2)}) %collective-permute-start.53) | collective-permute-done | bytes 262176 | tf_op jit(solution)/shard_map/ppermute | solution.py:517
  363.7 10.1 %collective-permute-done.54.refs_10_ = f32[2,1,256,128]{3,2,1,0:T(8,128)S(1)} collective-permute-done((f32[2,1,256,128]{3,2,1,0:T(8,128)S(1)}, f32[2,1,256,128]{3,2,1,0:T(8,128)S(1)}, u32[]{:S(2)}, u32[]{:S(2)}) %collective-permute-start.54) | collective-permute-done | bytes 262176 | tf_op jit(solution)/shard_map/ppermute | solution.py:517
  375.3 4.1 collective-permute-done.55.refs_11_
  379.9 11.6 %collective-permute-done.56.refs_12_ = f32[2,1,256,128]{3,2,1,0:T(8,128)S(1)} collective-permute-done((f32[2,1,256,128]{3,2,1,0:T(8,128)S(1)}, f32[2,1,256,128]{3,2,1,0:T(8,128)S(1)}, u32[]{:S(2)}, u32[]{:S(2)}) %collective-permute-start.56) | collective-permute-done | bytes 262176 | tf_op jit(solution)/shard_map/ppermute | solution.py:517
  392.8 4.5 collective-permute-done.57.refs_13_
  401.1 2.8 collective-permute-done.58.refs_14_
  404.5 5.0 collective-permute-done.59.refs_15_
  411.7 4.2 broadcast_multiply_fusion
  417.0 2.6 collective-permute-start.36
  419.6 5.0 collective-permute-done.34.refs_5_
  424.6 10.3 %collective-permute-done.35.refs_6_ = f32[2,1,256,128]{3,2,1,0:T(8,128)S(1)} collective-permute-done((f32[2,1,256,128]{3,2,1,0:T(8,128)S(1)}, f32[2,1,256,128]{3,2,1,0:T(8,128)S(1)}, u32[]{:S(2)}, u32[]{:S(2)}) %collective-permute-start.35) | collective-permute-done | bytes 262176 | tf_op jit(solution)/shard_map/ppermute | solution.py:517
  434.9 3.4 collective-permute-start.39
  438.3 3.9 pad_maximum_fusion
  447.0 21.0 %collective-permute-start.42 = (f32[2,1,256,128]{3,2,1,0:T(8,128)S(1)}, f32[2,1,256,128]{3,2,1,0:T(8,128)}, u32[]{:S(2)}, u32[]{:S(2)}) collective-permute-start(f32[2,1,256,128]{3,2,1,0:T(8,128)S(1)} %copy-done.3), channel_id=1, source_target_pairs={{0,26},{2,24},{4,30},{6,28},{8,18},{10,16},{12,22},{14,20},{16,10}... | collective-permute-start | bytes 786440 | tf_op jit(solution)/shard_map/ppermute | solution.py:517
  469.2 14.4 %collective-permute-start.44 = (f32[2,1,256,128]{3,2,1,0:T(8,128)S(1)}, f32[2,1,256,128]{3,2,1,0:T(8,128)}, u32[]{:S(2)}, u32[]{:S(2)}) collective-permute-start(f32[2,1,256,128]{3,2,1,0:T(8,128)S(1)} %copy-done.1), channel_id=1, source_target_pairs={{0,30},{2,28},{4,26},{6,24},{8,22},{10,20},{12,18},{14,16},{16,14}... | collective-permute-start | bytes 786440 | tf_op jit(solution)/shard_map/ppermute | solution.py:517
  483.7 13.1 %shard_map.181.refs_16_ = f32[256,4096]{1,0:T(8,128)} custom-call(f32[2,1,256,128]{3,2,1,0:T(8,128)} %get-tuple-element.124.refs_0_, f32[2,1,256,128]{3,2,1,0:T(8,128)} %copy-done.9, f32[2,1,256,128]{3,2,1,0:T(8,128)} %copy-done.11, f32[2,1,256,128]{3,2,1,0:T(8,128)} %copy-done.13, f32[2,1,256,128]{3,2,1,0:T(8,128)} %copy-done.26, ...), custom_call_target="tpu_custom_call" | custom-call | flops 10000000000 | bytes 30000000 | tf_op jit(solution)/shard_map/pallas_call | solution.py:388
  496.8 11.0 %collective-permute-done.42.refs_13_ = f32[2,1,256,128]{3,2,1,0:T(8,128)} collective-permute-done((f32[2,1,256,128]{3,2,1,0:T(8,128)S(1)}, f32[2,1,256,128]{3,2,1,0:T(8,128)}, u32[]{:S(2)}, u32[]{:S(2)}) %collective-permute-start.42) | collective-permute-done | bytes 262176 | tf_op jit(solution)/shard_map/ppermute | solution.py:517
  509.1 7.5 %collective-permute-done.44.refs_15_ = f32[2,1,256,128]{3,2,1,0:T(8,128)} collective-permute-done((f32[2,1,256,128]{3,2,1,0:T(8,128)S(1)}, f32[2,1,256,128]{3,2,1,0:T(8,128)}, u32[]{:S(2)}, u32[]{:S(2)}) %collective-permute-start.44) | collective-permute-done | bytes 262176 | tf_op jit(solution)/shard_map/ppermute | solution.py:517
  516.6 12.3 %shard_map.182 = f32[256,4096]{1,0:T(8,128)} custom-call(f32[2,1,256,128]{3,2,1,0:T(8,128)} %get-tuple-element.108.refs_0_, f32[2,1,256,128]{3,2,1,0:T(8,128)} %collective-permute-done.30.refs_1_, f32[2,1,256,128]{3,2,1,0:T(8,128)} %collective-permute-done.31.refs_2_, f32[2,1,256,128]{3,2,1,0:T(8,128)} %copy-done.63, f32[2,1,256,128]{3,2,1,0:T(8,128)} %copy-done.65, ...), custom_call_target="tpu_custom_call" | custom-call | flops 10000000000 | bytes 30000000 | tf_op jit(solution)/shard_map/pallas_call | solution.py:388
  (267 shorter events, 71.1 us)
Async XLA Ops:
  35.2 45.2 %collective-permute-start.23 = (f32[2,2,128,128]{3,2,1,0:T(8,128)}, f32[2,2,128,128]{3,2,1,0:T(8,128)S(1)}, u32[]{:S(2)}, u32[]{:S(2)}) collective-permute-start(f32[2,2,128,128]{3,2,1,0:T(8,128)} %get-tuple-element.100), channel_id=1, source_target_pairs={{0,18},{2,16},{4,22},{6,20},{8,26},{10,24},{12,30},{14,28},{16,2},... | collective-permute-start | bytes 786440 | tf_op jit(solution)/shard_map/ppermute | solution.py:517
  35.6 50.4 %collective-permute-start.24 = (f32[2,2,128,128]{3,2,1,0:T(8,128)}, f32[2,2,128,128]{3,2,1,0:T(8,128)S(1)}, u32[]{:S(2)}, u32[]{:S(2)}) collective-permute-start(f32[2,2,128,128]{3,2,1,0:T(8,128)} %get-tuple-element.101), channel_id=1, source_target_pairs={{0,20},{2,22},{4,16},{6,18},{8,28},{10,30},{12,24},{14,26},{16,4},... | collective-permute-start | bytes 786440 | tf_op jit(solution)/shard_map/ppermute | solution.py:517
  38.0 64.9 %collective-permute-start.25 = (f32[2,2,128,128]{3,2,1,0:T(8,128)}, f32[2,2,128,128]{3,2,1,0:T(8,128)}, u32[]{:S(2)}, u32[]{:S(2)}) collective-permute-start(f32[2,2,128,128]{3,2,1,0:T(8,128)} %get-tuple-element.102), channel_id=1, source_target_pairs={{0,22},{2,20},{4,18},{6,16},{8,30},{10,28},{12,26},{14,24},{16,6},... | collective-permute-start | bytes 786440 | tf_op jit(solution)/shard_map/ppermute | solution.py:517
  49.4 59.1 %collective-permute-start.26 = (f32[2,2,128,128]{3,2,1,0:T(8,128)}, f32[2,2,128,128]{3,2,1,0:T(8,128)S(1)}, u32[]{:S(2)}, u32[]{:S(2)}) collective-permute-start(f32[2,2,128,128]{3,2,1,0:T(8,128)} %get-tuple-element.103), channel_id=1, source_target_pairs={{0,24},{2,26},{4,28},{6,30},{8,16},{10,18},{12,20},{14,22},{16,8},... | collective-permute-start | bytes 786440 | tf_op jit(solution)/shard_map/ppermute | solution.py:517
  50.5 64.5 %collective-permute-start.27 = (f32[2,2,128,128]{3,2,1,0:T(8,128)}, f32[2,2,128,128]{3,2,1,0:T(8,128)S(1)}, u32[]{:S(2)}, u32[]{:S(2)}) collective-permute-start(f32[2,2,128,128]{3,2,1,0:T(8,128)} %get-tuple-element.104), channel_id=1, source_target_pairs={{0,26},{2,24},{4,30},{6,28},{8,18},{10,16},{12,22},{14,20},{16,10}... | collective-permute-start | bytes 786440 | tf_op jit(solution)/shard_map/ppermute | solution.py:517
  80.4 67.5 %collective-permute-start.28 = (f32[2,2,128,128]{3,2,1,0:T(8,128)}, f32[2,2,128,128]{3,2,1,0:T(8,128)S(1)}, u32[]{:S(2)}, u32[]{:S(2)}) collective-permute-start(f32[2,2,128,128]{3,2,1,0:T(8,128)} %get-tuple-element.105), channel_id=1, source_target_pairs={{0,28},{2,30},{4,24},{6,26},{8,20},{10,22},{12,16},{14,18},{16,12}... | collective-permute-start | bytes 786440 | tf_op jit(solution)/shard_map/ppermute | solution.py:517
  86.0 68.0 %collective-permute-start.29 = (f32[2,2,128,128]{3,2,1,0:T(8,128)}, f32[2,2,128,128]{3,2,1,0:T(8,128)S(1)}, u32[]{:S(2)}, u32[]{:S(2)}) collective-permute-start(f32[2,2,128,128]{3,2,1,0:T(8,128)} %get-tuple-element.106), channel_id=1, source_target_pairs={{0,30},{2,28},{4,26},{6,24},{8,22},{10,20},{12,18},{14,16},{16,14}... | collective-permute-start | bytes 786440 | tf_op jit(solution)/shard_map/ppermute | solution.py:517
  102.9 52.9 %collective-permute-start = (f32[2,2,128,128]{3,2,1,0:T(8,128)}, f32[2,2,128,128]{3,2,1,0:T(8,128)S(1)}, u32[]{:S(2)}, u32[]{:S(2)}) collective-permute-start(f32[2,2,128,128]{3,2,1,0:T(8,128)} %get-tuple-element.76), channel_id=1, source_target_pairs={{0,2},{2,0},{4,6},{6,4},{8,10},{10,8},{12,14},{14,12},{16,18},{18,... | collective-permute-start | bytes 786440 | tf_op jit(solution)/shard_map/ppermute | solution.py:517
  108.5 49.1 %collective-permute-start.1 = (f32[2,2,128,128]{3,2,1,0:T(8,128)S(1)}, f32[2,2,128,128]{3,2,1,0:T(8,128)S(1)}, u32[]{:S(2)}, u32[]{:S(2)}) collective-permute-start(f32[2,2,128,128]{3,2,1,0:T(8,128)S(1)} %copy-done.58), channel_id=1, source_target_pairs={{0,4},{2,6},{4,0},{6,2},{8,12},{10,14},{12,8},{14,10},{16,20},{18,... | collective-permute-start | bytes 786440 | tf_op jit(solution)/shard_map/ppermute | solution.py:517
  115.0 44.6 %collective-permute-start.10 = (f32[2,2,128,128]{3,2,1,0:T(8,128)S(1)}, f32[2,2,128,128]{3,2,1,0:T(8,128)S(1)}, u32[]{:S(2)}, u32[]{:S(2)}) collective-permute-start(f32[2,2,128,128]{3,2,1,0:T(8,128)S(1)} %copy-done.55), channel_id=1, source_target_pairs={{0,22},{2,20},{4,18},{6,16},{8,30},{10,28},{12,26},{14,24},{16,6},... | collective-permute-start | bytes 786440 | tf_op jit(solution)/shard_map/ppermute | solution.py:517
  157.6 25.7 %collective-permute-start.14 = (f32[2,2,128,128]{3,2,1,0:T(8,128)S(1)}, f32[2,2,128,128]{3,2,1,0:T(8,128)S(1)}, u32[]{:S(2)}, u32[]{:S(2)}) collective-permute-start(f32[2,2,128,128]{3,2,1,0:T(8,128)S(1)} %copy-done.43), channel_id=1, source_target_pairs={{0,30},{2,28},{4,26},{6,24},{8,22},{10,20},{12,18},{14,16},{16,14}... | collective-permute-start | bytes 786440 | tf_op jit(solution)/shard_map/ppermute | solution.py:517
  159.6 23.7 %collective-permute-start.2 = (f32[2,2,128,128]{3,2,1,0:T(8,128)S(1)}, f32[2,2,128,128]{3,2,1,0:T(8,128)S(1)}, u32[]{:S(2)}, u32[]{:S(2)}) collective-permute-start(f32[2,2,128,128]{3,2,1,0:T(8,128)S(1)} %copy-done.40), channel_id=1, source_target_pairs={{0,6},{2,4},{4,2},{6,0},{8,14},{10,12},{12,10},{14,8},{16,22},{18,... | collective-permute-start | bytes 786440 | tf_op jit(solution)/shard_map/ppermute | solution.py:517
  164.6 23.4 %collective-permute-start.3 = (f32[2,2,128,128]{3,2,1,0:T(8,128)S(1)}, f32[2,2,128,128]{3,2,1,0:T(8,128)S(1)}, u32[]{:S(2)}, u32[]{:S(2)}) collective-permute-start(f32[2,2,128,128]{3,2,1,0:T(8,128)S(1)} %copy-done.37), channel_id=1, source_target_pairs={{0,8},{2,10},{4,12},{6,14},{8,0},{10,2},{12,4},{14,6},{16,24},{18,... | collective-permute-start | bytes 786440 | tf_op jit(solution)/shard_map/ppermute | solution.py:517
  183.3 41.8 %collective-permute-start.6 = (f32[2,2,128,128]{3,2,1,0:T(8,128)}, f32[2,2,128,128]{3,2,1,0:T(8,128)}, u32[]{:S(2)}, u32[]{:S(2)}) collective-permute-start(f32[2,2,128,128]{3,2,1,0:T(8,128)} %get-tuple-element.82), channel_id=1, source_target_pairs={{0,14},{2,12},{4,10},{6,8},{8,6},{10,4},{12,2},{14,0},{16,30},{18,... | collective-permute-start | bytes 786440 | tf_op jit(solution)/shard_map/ppermute | solution.py:517
  183.4 43.7 %collective-permute-start.7 = (f32[2,2,128,128]{3,2,1,0:T(8,128)}, f32[2,2,128,128]{3,2,1,0:T(8,128)}, u32[]{:S(2)}, u32[]{:S(2)}) collective-permute-start(f32[2,2,128,128]{3,2,1,0:T(8,128)} %get-tuple-element.83), channel_id=1, source_target_pairs={{0,16},{2,18},{4,20},{6,22},{8,24},{10,26},{12,28},{14,30},{16,0},... | collective-permute-start | bytes 786440 | tf_op jit(solution)/shard_map/ppermute | solution.py:517
  188.1 41.2 %collective-permute-start.8 = (f32[2,2,128,128]{3,2,1,0:T(8,128)S(1)}, f32[2,2,128,128]{3,2,1,0:T(8,128)}, u32[]{:S(2)}, u32[]{:S(2)}) collective-permute-start(f32[2,2,128,128]{3,2,1,0:T(8,128)S(1)} %copy-done.20), channel_id=1, source_target_pairs={{0,18},{2,16},{4,22},{6,20},{8,26},{10,24},{12,30},{14,28},{16,2},... | collective-permute-start | bytes 786440 | tf_op jit(solution)/shard_map/ppermute | solution.py:517
  189.1 43.5 %collective-permute-start.9 = (f32[2,2,128,128]{3,2,1,0:T(8,128)S(1)}, f32[2,2,128,128]{3,2,1,0:T(8,128)}, u32[]{:S(2)}, u32[]{:S(2)}) collective-permute-start(f32[2,2,128,128]{3,2,1,0:T(8,128)S(1)} %copy-done.17), channel_id=1, source_target_pairs={{0,20},{2,22},{4,16},{6,18},{8,28},{10,30},{12,24},{14,26},{16,4},... | collective-permute-start | bytes 786440 | tf_op jit(solution)/shard_map/ppermute | solution.py:517
  191.7 114.1 %collective-permute-start.60 = (f32[136,4096]{1,0:T(8,128)S(1)}, f32[136,4096]{1,0:T(8,128)}, u32[]{:S(2)}, u32[]{:S(2)}) collective-permute-start(f32[136,4096]{1,0:T(8,128)S(1)} %dynamic-slice_bitcast_fusion), channel_id=1, source_target_pairs={{0,1},{1,0},{2,3},{3,2},{4,5},{5,4},{6,7},{7,6},{8,9},{9,8},{10,11... | collective-permute-start | bytes 6684680 | tf_op jit(solution)/shard_map/ppermute | solution.py:498
  225.1 44.6 %collective-permute-start.61 = (f32[8,4096]{1,0:T(8,128)S(1)}, f32[8,4096]{1,0:T(8,128)S(1)}, u32[]{:S(2)}, u32[]{:S(2)}) collective-permute-start(f32[8,4096]{1,0:T(8,128)S(1)} %get-tuple-element.152), channel_id=1, source_target_pairs={{0,2},{2,4},{4,6},{6,8},{8,10},{10,12},{12,14},{14,16},{16,18},{18... | collective-permute-start | bytes 393224 | tf_op jit(solution)/shard_map/ppermute | solution.py:541
  227.1 39.8 %collective-permute-start.63 = (f32[3,2,4096]{2,1,0:T(2,128)S(1)}, f32[3,2,4096]{2,1,0:T(2,128)S(1)}, u32[]{:S(2)}, u32[]{:S(2)}) collective-permute-start(f32[3,2,4096]{2,1,0:T(2,128)S(1)} %pad_maximum_fusion.1), channel_id=1, source_target_pairs={{0,1},{1,2},{2,3},{3,4},{4,5},{5,6},{6,7},{7,8},{8,9},{9,10},{10,1... | collective-permute-start | bytes 294920 | tf_op jit(solution)/shard_map/ppermute | solution.py:551
  229.3 37.7 %collective-permute-start.64 = (f32[3,2,4096]{2,1,0:T(2,128)S(1)}, f32[3,2,4096]{2,1,0:T(2,128)S(1)}, u32[]{:S(2)}, u32[]{:S(2)}) collective-permute-start(f32[3,2,4096]{2,1,0:T(2,128)S(1)} %pad_maximum_fusion.2), channel_id=1, source_target_pairs={{1,0},{2,1},{3,2},{4,3},{5,4},{6,5},{7,6},{8,7},{9,8},{10,9},{11,1... | collective-permute-start | bytes 294920 | tf_op jit(solution)/shard_map/ppermute | solution.py:551
  266.9 33.2 %collective-permute-start.45 = (f32[2,1,256,128]{3,2,1,0:T(8,128)}, f32[2,1,256,128]{3,2,1,0:T(8,128)S(1)}, u32[]{:S(2)}, u32[]{:S(2)}) collective-permute-start(f32[2,1,256,128]{3,2,1,0:T(8,128)} %get-tuple-element.125), channel_id=1, source_target_pairs={{0,2},{2,0},{4,6},{6,4},{8,10},{10,8},{12,14},{14,12},{16,18},{18,... | collective-permute-start | bytes 786440 | tf_op jit(solution)/shard_map/ppermute | solution.py:517
  267.0 35.9 %collective-permute-start.46 = (f32[2,1,256,128]{3,2,1,0:T(8,128)}, f32[2,1,256,128]{3,2,1,0:T(8,128)S(1)}, u32[]{:S(2)}, u32[]{:S(2)}) collective-permute-start(f32[2,1,256,128]{3,2,1,0:T(8,128)} %get-tuple-element.126), channel_id=1, source_target_pairs={{0,4},{2,6},{4,0},{6,2},{8,12},{10,14},{12,8},{14,10},{16,20},{18,... | collective-permute-start | bytes 786440 | tf_op jit(solution)/shard_map/ppermute | solution.py:517
  267.9 36.7 %collective-permute-start.47 = (f32[2,1,256,128]{3,2,1,0:T(8,128)}, f32[2,1,256,128]{3,2,1,0:T(8,128)S(1)}, u32[]{:S(2)}, u32[]{:S(2)}) collective-permute-start(f32[2,1,256,128]{3,2,1,0:T(8,128)} %get-tuple-element.127), channel_id=1, source_target_pairs={{0,6},{2,4},{4,2},{6,0},{8,14},{10,12},{12,10},{14,8},{16,22},{18,... | collective-permute-start | bytes 786440 | tf_op jit(solution)/shard_map/ppermute | solution.py:517
  297.2 28.2 %collective-permute-start.48 = (f32[2,1,256,128]{3,2,1,0:T(8,128)}, f32[2,1,256,128]{3,2,1,0:T(8,128)S(1)}, u32[]{:S(2)}, u32[]{:S(2)}) collective-permute-start(f32[2,1,256,128]{3,2,1,0:T(8,128)} %get-tuple-element.128), channel_id=1, source_target_pairs={{0,8},{2,10},{4,12},{6,14},{8,0},{10,2},{12,4},{14,6},{16,24},{18,... | collective-permute-start | bytes 786440 | tf_op jit(solution)/shard_map/ppermute | solution.py:517
  300.1 27.7 %collective-permute-start.49 = (f32[2,1,256,128]{3,2,1,0:T(8,128)}, f32[2,1,256,128]{3,2,1,0:T(8,128)}, u32[]{:S(2)}, u32[]{:S(2)}) collective-permute-start(f32[2,1,256,128]{3,2,1,0:T(8,128)} %get-tuple-element.129), channel_id=1, source_target_pairs={{0,10},{2,8},{4,14},{6,12},{8,2},{10,0},{12,6},{14,4},{16,26},{18,... | collective-permute-start | bytes 786440 | tf_op jit(solution)/shard_map/ppermute | solution.py:517
  302.9 27.3 %collective-permute-start.50 = (f32[2,1,256,128]{3,2,1,0:T(8,128)}, f32[2,1,256,128]{3,2,1,0:T(8,128)}, u32[]{:S(2)}, u32[]{:S(2)}) collective-permute-start(f32[2,1,256,128]{3,2,1,0:T(8,128)} %get-tuple-element.130), channel_id=1, source_target_pairs={{0,12},{2,14},{4,8},{6,10},{8,4},{10,6},{12,0},{14,2},{16,28},{18,... | collective-permute-start | bytes 786440 | tf_op jit(solution)/shard_map/ppermute | solution.py:517
  304.7 26.9 %collective-permute-start.51 = (f32[2,1,256,128]{3,2,1,0:T(8,128)}, f32[2,1,256,128]{3,2,1,0:T(8,128)}, u32[]{:S(2)}, u32[]{:S(2)}) collective-permute-start(f32[2,1,256,128]{3,2,1,0:T(8,128)} %get-tuple-element.131), channel_id=1, source_target_pairs={{0,14},{2,12},{4,10},{6,8},{8,6},{10,4},{12,2},{14,0},{16,30},{18,... | collective-permute-start | bytes 786440 | tf_op jit(solution)/shard_map/ppermute | solution.py:517
  305.9 26.0 %collective-permute-start.52 = (f32[2,1,256,128]{3,2,1,0:T(8,128)}, f32[2,1,256,128]{3,2,1,0:T(8,128)S(1)}, u32[]{:S(2)}, u32[]{:S(2)}) collective-permute-start(f32[2,1,256,128]{3,2,1,0:T(8,128)} %get-tuple-element.132), channel_id=1, source_target_pairs={{0,16},{2,18},{4,20},{6,22},{8,24},{10,26},{12,28},{14,30},{16,0},... | collective-permute-start | bytes 786440 | tf_op jit(solution)/shard_map/ppermute | solution.py:517
  325.4 37.2 %collective-permute-start.53 = (f32[2,1,256,128]{3,2,1,0:T(8,128)S(1)}, f32[2,1,256,128]{3,2,1,0:T(8,128)S(1)}, u32[]{:S(2)}, u32[]{:S(2)}) collective-permute-start(f32[2,1,256,128]{3,2,1,0:T(8,128)S(1)} %copy-done.30), channel_id=1, source_target_pairs={{0,18},{2,16},{4,22},{6,20},{8,26},{10,24},{12,30},{14,28},{16,2},... | collective-permute-start | bytes 786440 | tf_op jit(solution)/shard_map/ppermute | solution.py:517
  327.8 46.1 %collective-permute-start.54 = (f32[2,1,256,128]{3,2,1,0:T(8,128)S(1)}, f32[2,1,256,128]{3,2,1,0:T(8,128)S(1)}, u32[]{:S(2)}, u32[]{:S(2)}) collective-permute-start(f32[2,1,256,128]{3,2,1,0:T(8,128)S(1)} %copy-done.28), channel_id=1, source_target_pairs={{0,20},{2,22},{4,16},{6,18},{8,28},{10,30},{12,24},{14,26},{16,4},... | collective-permute-start | bytes 786440 | tf_op jit(solution)/shard_map/ppermute | solution.py:517
  330.2 49.2 %collective-permute-start.55 = (f32[2,1,256,128]{3,2,1,0:T(8,128)S(1)}, f32[2,1,256,128]{3,2,1,0:T(8,128)S(1)}, u32[]{:S(2)}, u32[]{:S(2)}) collective-permute-start(f32[2,1,256,128]{3,2,1,0:T(8,128)S(1)} %copy-done.27), channel_id=1, source_target_pairs={{0,22},{2,20},{4,18},{6,16},{8,30},{10,28},{12,26},{14,24},{16,6},... | collective-permute-start | bytes 786440 | tf_op jit(solution)/shard_map/ppermute | solution.py:517
  331.6 60.0 %collective-permute-start.56 = (f32[2,1,256,128]{3,2,1,0:T(8,128)S(1)}, f32[2,1,256,128]{3,2,1,0:T(8,128)S(1)}, u32[]{:S(2)}, u32[]{:S(2)}) collective-permute-start(f32[2,1,256,128]{3,2,1,0:T(8,128)S(1)} %copy-done.25), channel_id=1, source_target_pairs={{0,24},{2,26},{4,28},{6,30},{8,16},{10,18},{12,20},{14,22},{16,8},... | collective-permute-start | bytes 786440 | tf_op jit(solution)/shard_map/ppermute | solution.py:517
  331.9 65.5 %collective-permute-start.57 = (f32[2,1,256,128]{3,2,1,0:T(8,128)S(1)}, f32[2,1,256,128]{3,2,1,0:T(8,128)}, u32[]{:S(2)}, u32[]{:S(2)}) collective-permute-start(f32[2,1,256,128]{3,2,1,0:T(8,128)S(1)} %copy-done.24), channel_id=1, source_target_pairs={{0,26},{2,24},{4,30},{6,28},{8,18},{10,16},{12,22},{14,20},{16,10}... | collective-permute-start | bytes 786440 | tf_op jit(solution)/shard_map/ppermute | solution.py:517
  362.6 41.3 %collective-permute-start.58 = (f32[2,1,256,128]{3,2,1,0:T(8,128)S(1)}, f32[2,1,256,128]{3,2,1,0:T(8,128)}, u32[]{:S(2)}, u32[]{:S(2)}) collective-permute-start(f32[2,1,256,128]{3,2,1,0:T(8,128)S(1)} %copy-done.15), channel_id=1, source_target_pairs={{0,28},{2,30},{4,24},{6,26},{8,20},{10,22},{12,16},{14,18},{16,12}... | collective-permute-start | bytes 786440 | tf_op jit(solution)/shard_map/ppermute | solution.py:517
  373.8 35.7 %collective-permute-start.59 = (f32[2,1,256,128]{3,2,1,0:T(8,128)S(1)}, f32[2,1,256,128]{3,2,1,0:T(8,128)}, u32[]{:S(2)}, u32[]{:S(2)}) collective-permute-start(f32[2,1,256,128]{3,2,1,0:T(8,128)S(1)} %copy-done.12), channel_id=1, source_target_pairs={{0,30},{2,28},{4,26},{6,24},{8,22},{10,20},{12,18},{14,16},{16,14}... | collective-permute-start | bytes 786440 | tf_op jit(solution)/shard_map/ppermute | solution.py:517
  379.4 30.1 %collective-permute-start.30 = (f32[2,1,256,128]{3,2,1,0:T(8,128)}, f32[2,1,256,128]{3,2,1,0:T(8,128)}, u32[]{:S(2)}, u32[]{:S(2)}) collective-permute-start(f32[2,1,256,128]{3,2,1,0:T(8,128)} %get-tuple-element.109), channel_id=1, source_target_pairs={{0,2},{2,0},{4,6},{6,4},{8,10},{10,8},{12,14},{14,12},{16,18},{18,... | collective-permute-start | bytes 786440 | tf_op jit(solution)/shard_map/ppermute | solution.py:517
  397.3 71.9 %collective-permute-start.65 = (f32[128,4096]{1,0:T(8,128)}, f32[128,4096]{1,0:T(8,128)S(1)}, u32[]{:S(2)}, u32[]{:S(2)}) collective-permute-start(f32[128,4096]{1,0:T(8,128)} %get-tuple-element.143), channel_id=1, source_target_pairs={{0,1},{1,0},{2,3},{3,2},{4,5},{5,4},{6,7},{7,6},{8,9},{9,8},{10,11... | collective-permute-start | bytes 6291464 | tf_op jit(solution)/shard_map/ppermute | solution.py:498
  411.6 23.3 %collective-permute-start.35 = (f32[2,1,256,128]{3,2,1,0:T(8,128)S(1)}, f32[2,1,256,128]{3,2,1,0:T(8,128)S(1)}, u32[]{:S(2)}, u32[]{:S(2)}) collective-permute-start(f32[2,1,256,128]{3,2,1,0:T(8,128)S(1)} %copy-done.14), channel_id=1, source_target_pairs={{0,12},{2,14},{4,8},{6,10},{8,4},{10,6},{12,0},{14,2},{16,28},{18,... | collective-permute-start | bytes 786440 | tf_op jit(solution)/shard_map/ppermute | solution.py:517
  417.0 25.3 %collective-permute-start.36 = (f32[2,1,256,128]{3,2,1,0:T(8,128)S(1)}, f32[2,1,256,128]{3,2,1,0:T(8,128)S(1)}, u32[]{:S(2)}, u32[]{:S(2)}) collective-permute-start(f32[2,1,256,128]{3,2,1,0:T(8,128)S(1)} %copy-done.10), channel_id=1, source_target_pairs={{0,14},{2,12},{4,10},{6,8},{8,6},{10,4},{12,2},{14,0},{16,30},{18,... | collective-permute-start | bytes 786440 | tf_op jit(solution)/shard_map/ppermute | solution.py:517
  419.6 25.0 %collective-permute-start.37 = (f32[2,1,256,128]{3,2,1,0:T(8,128)S(1)}, f32[2,1,256,128]{3,2,1,0:T(8,128)S(1)}, u32[]{:S(2)}, u32[]{:S(2)}) collective-permute-start(f32[2,1,256,128]{3,2,1,0:T(8,128)S(1)} %copy-done.8), channel_id=1, source_target_pairs={{0,16},{2,18},{4,20},{6,22},{8,24},{10,26},{12,28},{14,30},{16,0},... | collective-permute-start | bytes 786440 | tf_op jit(solution)/shard_map/ppermute | solution.py:517
  424.6 22.4 %collective-permute-start.38 = (f32[2,1,256,128]{3,2,1,0:T(8,128)S(1)}, f32[2,1,256,128]{3,2,1,0:T(8,128)S(1)}, u32[]{:S(2)}, u32[]{:S(2)}) collective-permute-start(f32[2,1,256,128]{3,2,1,0:T(8,128)S(1)} %copy-done.7), channel_id=1, source_target_pairs={{0,18},{2,16},{4,22},{6,20},{8,26},{10,24},{12,30},{14,28},{16,2},... | collective-permute-start | bytes 786440 | tf_op jit(solution)/shard_map/ppermute | solution.py:517
  434.9 33.1 %collective-permute-start.39 = (f32[2,1,256,128]{3,2,1,0:T(8,128)S(1)}, f32[2,1,256,128]{3,2,1,0:T(8,128)}, u32[]{:S(2)}, u32[]{:S(2)}) collective-permute-start(f32[2,1,256,128]{3,2,1,0:T(8,128)S(1)} %copy-done.6), channel_id=1, source_target_pairs={{0,20},{2,22},{4,16},{6,18},{8,28},{10,30},{12,24},{14,26},{16,4},... | collective-permute-start | bytes 786440 | tf_op jit(solution)/shard_map/ppermute | solution.py:517
  442.3 54.5 %collective-permute-start.40 = (f32[2,1,256,128]{3,2,1,0:T(8,128)S(1)}, f32[2,1,256,128]{3,2,1,0:T(8,128)}, u32[]{:S(2)}, u32[]{:S(2)}) collective-permute-start(f32[2,1,256,128]{3,2,1,0:T(8,128)S(1)} %copy-done.5), channel_id=1, source_target_pairs={{0,22},{2,20},{4,18},{6,16},{8,30},{10,28},{12,26},{14,24},{16,6},... | collective-permute-start | bytes 786440 | tf_op jit(solution)/shard_map/ppermute | solution.py:517
  444.5 52.3 %collective-permute-start.41 = (f32[2,1,256,128]{3,2,1,0:T(8,128)S(1)}, f32[2,1,256,128]{3,2,1,0:T(8,128)}, u32[]{:S(2)}, u32[]{:S(2)}) collective-permute-start(f32[2,1,256,128]{3,2,1,0:T(8,128)S(1)} %copy-done.4), channel_id=1, source_target_pairs={{0,24},{2,26},{4,28},{6,30},{8,16},{10,18},{12,20},{14,22},{16,8},... | collective-permute-start | bytes 786440 | tf_op jit(solution)/shard_map/ppermute | solution.py:517
  447.0 60.9 %collective-permute-start.42 = (f32[2,1,256,128]{3,2,1,0:T(8,128)S(1)}, f32[2,1,256,128]{3,2,1,0:T(8,128)}, u32[]{:S(2)}, u32[]{:S(2)}) collective-permute-start(f32[2,1,256,128]{3,2,1,0:T(8,128)S(1)} %copy-done.3), channel_id=1, source_target_pairs={{0,26},{2,24},{4,30},{6,28},{8,18},{10,16},{12,22},{14,20},{16,10}... | collective-permute-start | bytes 786440 | tf_op jit(solution)/shard_map/ppermute | solution.py:517
  468.0 41.1 %collective-permute-start.43 = (f32[2,1,256,128]{3,2,1,0:T(8,128)S(1)}, f32[2,1,256,128]{3,2,1,0:T(8,128)}, u32[]{:S(2)}, u32[]{:S(2)}) collective-permute-start(f32[2,1,256,128]{3,2,1,0:T(8,128)S(1)} %copy-done.2), channel_id=1, source_target_pairs={{0,28},{2,30},{4,24},{6,26},{8,20},{10,22},{12,16},{14,18},{16,12}... | collective-permute-start | bytes 786440 | tf_op jit(solution)/shard_map/ppermute | solution.py:517
  469.2 47.4 %collective-permute-start.44 = (f32[2,1,256,128]{3,2,1,0:T(8,128)S(1)}, f32[2,1,256,128]{3,2,1,0:T(8,128)}, u32[]{:S(2)}, u32[]{:S(2)}) collective-permute-start(f32[2,1,256,128]{3,2,1,0:T(8,128)S(1)} %copy-done.1), channel_id=1, source_target_pairs={{0,30},{2,28},{4,26},{6,24},{8,22},{10,20},{12,18},{14,16},{16,14}... | collective-permute-start | bytes 786440 | tf_op jit(solution)/shard_map/ppermute | solution.py:517
  (99 other events, 3805.3 us)

commit v5 on v4

--- a/solution.py
+++ b/solution.py
@@ -189,6 +189,24 @@
     return a[:half] + b[half:], b[:half] - a[half:]
 
 
+def fetch_spans(pieces, target, sem, spans):
+    me = lax.axis_index("row")
+    rows = target.shape[3] // spans
+    starts = []
+    for i in range(spans):
+        at = pl.ds(i * rows, rows)
+        copies = []
+        for d, piece in enumerate(pieces):
+            if len(pieces) == 1:
+                source, place = piece.at[:, :, :, at], target.at[:, :, :, at]
+            else:
+                source, place = piece.at[:, :, at], target.at[jnp.bitwise_xor(me, d), :, :, at]
+            copies.append(pltpu.make_async_copy(source, place, sem.at[i * len(pieces) + d]))
+            copies[-1].start()
+        starts.append(copies)
+    return starts
+
+
 def fetch_pieces(pieces, target, sem):
     me = lax.axis_index("row")
     copies = []
@@ -321,7 +339,8 @@
     rows, batch = got.shape[3], got.shape[2] * got.shape[4]
     length = count * width
     me = lax.axis_index("chan")
-    fetch_got = fetch_pieces(came, got, came_sem)
+    spans = GOT_PARTS if rows % (8 * GOT_PARTS) == 0 else 1
+    fetch_got = fetch_spans(came, got, came_sem, spans)
     half = rows // 2
     fetch_base = [pltpu.make_async_copy(base_hbm[0], base, sem.at[0])]
     if is_first:
@@ -330,8 +349,6 @@
             fetch_base.append(pltpu.make_async_copy(base_hbm[1 + i], place, sem.at[1 + i]))
     for copy in fetch_base:
         copy.start()
-    for copy in fetch_got:
-        copy.wait()
 
     def load(p, at, lanes):
         tile = lanes.start // got.shape[4]
@@ -341,7 +358,11 @@
         y_re[p, at, lanes] = re
         y_im[p, at, lanes] = im
 
-    radix_stage(load, tw_re, tw_im, store, rows, batch, count, 1, start)
+    for i in range(spans):
+        for copy in fetch_got[i]:
+            copy.wait()
+        span = (i * (rows // spans), (i + 1) * (rows // spans))
+        radix_stage(load, tw_re, tw_im, store, span, batch, count, 1, start)
     cols = slice(start, start + batch)
     e_high = jnp.concatenate([g_high[:width, cols], -g_high[width:, cols]], axis=1)
     e_low = jnp.concatenate([g_low[:width, cols], -g_low[width:, cols]], axis=1)
@@ -500,12 +521,14 @@
 
 UNROLL = 4
 SKY_PARTS = 4
+GOT_PARTS = 2
 
 
 def partners(size):
     quarter = size // 4
     far = [d for i in range(quarter) for d in (2 * quarter + i, 3 * quarter + i)]
-    return far[:2] + [*range(quarter, 2 * quarter), *range(1, quarter)] + far[2:]
+    near, half = list(range(quarter, 2 * quarter)), quarter // 2
+    return far[:2] + near[:half] + far[2:4] + near[half:] + far[4:6] + [*range(1, quarter)] + far[6:]
 
 
 def row_exchange(pieces):
@@ -646,7 +669,7 @@
         specs.append(pl.BlockSpec(memory_space=pltpu.SMEM))
         scratch = [
             vmem(packed), vmem((rows, length)), *[vmem((count, rows, batch))] * 2,
-            vmem((-(-rows // 128), length, 128)), dma(7), dma(n), *[vmem((rows, length))] * (c == 0),
+            vmem((-(-rows // 128), length, 128)), dma(7), dma(GOT_PARTS * n), *[vmem((rows, length))] * (c == 0),
         ]
         image_new = call(
             partial(last_kernel, count, width, c * batch, n, c == 0, c == chunks - 1), args, specs,

time: 532 us -> 532 us (level)
  no operation moved by 1% of the time
where the time goes in v5:
time: 532 us; the launch traced here: 529 us
  waiting for transfers between devices  233 us (44%)
  Pallas kernels  145 us (27%)
  starting transfers between devices  132 us (25%)
  other arithmetic  10.6 us (2%)
    ppermute x60, waiting for transfers between devices, row_exchange(): got[d] = lax.ppermute(pieces[d], 'row', [(i, i ^ d) for i in range(size)])  211 us
    pallas_call x8, Pallas kernels, call(): pl.pallas_call(kernel, grid=(1,), in_specs=specs, out_specs=out_specs, ou...  145 us
    ppermute x60, starting transfers between devices, row_exchange(): got[d] = lax.ppermute(pieces[d], 'row', [(i, i ^ d) for i in range(size)])  114 us
    ppermute x5, waiting for transfers between devices, row_total(): lax.ppermute(v, 'row', [(i, i ^ d) for i in range(size)])  17.5 us
  transfers between devices with their start and end apart: 71, of which 33 were waited for; matrix products, arithmetic and copies ran while one was open for 3% of the time, Pallas kernels for 23%

profile of v5, /device:TPU:15, one launch (start us, length us, event | category | flops | bytes accessed | tf_op | source)
XLA Modules:
  0.0 528.6 jit_solution(17003136057956621005)
XLA Ops:
  0.6 11.6 %shard_map.176 = (f32[2,2,128,128]{3,2,1,0:T(8,128)}, f32[2,2,128,128]{3,2,1,0:T(8,128)}, f32[2,2,128,128]{3,2,1,0:T(8,128)}, f32[2,2,128,128]{3,2,1,0:T(8,128)}...) custom-call(f32[256,4096]{1,0:T(8,128)} %bitcast.15, ...), custom_call_target="tpu_custom_call" | custom-call | flops 10000000000 | bytes 10000000 | tf_op jit(solution)/shard_map/pallas_call | solution.py:409
  16.4 11.5 %shard_map.175 = (f32[2,2,128,128]{3,2,1,0:T(8,128)}, f32[2,2,128,128]{3,2,1,0:T(8,128)}, f32[2,2,128,128]{3,2,1,0:T(8,128)}, f32[2,2,128,128]{3,2,1,0:T(8,128)}...) custom-call(f32[256,4096]{1,0:T(8,128)} %bitcast.16, ...), custom_call_target="tpu_custom_call" | custom-call | flops 10000000000 | bytes 10000000 | tf_op jit(solution)/shard_map/pallas_call | solution.py:409
  30.4 2.5 collective-permute-start.21
  38.0 10.0 %collective-permute-start.25 = (f32[2,2,128,128]{3,2,1,0:T(8,128)}, f32[2,2,128,128]{3,2,1,0:T(8,128)}, u32[]{:S(2)}, u32[]{:S(2)}) collective-permute-start(f32[2,2,128,128]{3,2,1,0:T(8,128)} %get-tuple-element.102), channel_id=1, source_target_pairs={{0,22},{2,20},{4,18},{6,16},{8,30},{10,28},{12,26},{14,24},{16,6},... | collective-permute-start | bytes 786440 | tf_op jit(solution)/shard_map/ppermute | solution.py:540
  52.0 28.5 %collective-permute-done.23.refs_9_ = f32[2,2,128,128]{3,2,1,0:T(8,128)S(1)} collective-permute-done((f32[2,2,128,128]{3,2,1,0:T(8,128)}, f32[2,2,128,128]{3,2,1,0:T(8,128)S(1)}, u32[]{:S(2)}, u32[]{:S(2)}) %collective-permute-start.23) | collective-permute-done | bytes 262176 | tf_op jit(solution)/shard_map/ppermute | solution.py:540
  80.4 5.6 %collective-permute-done.24.refs_10_ = f32[2,2,128,128]{3,2,1,0:T(8,128)S(1)} collective-permute-done((f32[2,2,128,128]{3,2,1,0:T(8,128)}, f32[2,2,128,128]{3,2,1,0:T(8,128)S(1)}, u32[]{:S(2)}, u32[]{:S(2)}) %collective-permute-start.24) | collective-permute-done | bytes 262176 | tf_op jit(solution)/shard_map/ppermute | solution.py:540
  86.4 16.5 %collective-permute-done.25.refs_11_ = f32[2,2,128,128]{3,2,1,0:T(8,128)} collective-permute-done((f32[2,2,128,128]{3,2,1,0:T(8,128)}, f32[2,2,128,128]{3,2,1,0:T(8,128)}, u32[]{:S(2)}, u32[]{:S(2)}) %collective-permute-start.25) | collective-permute-done | bytes 262176 | tf_op jit(solution)/shard_map/ppermute | solution.py:540
  108.8 6.2 %collective-permute-done.27.refs_13_ = f32[2,2,128,128]{3,2,1,0:T(8,128)S(1)} collective-permute-done((f32[2,2,128,128]{3,2,1,0:T(8,128)}, f32[2,2,128,128]{3,2,1,0:T(8,128)S(1)}, u32[]{:S(2)}, u32[]{:S(2)}) %collective-permute-start.27) | collective-permute-done | bytes 262176 | tf_op jit(solution)/shard_map/ppermute | solution.py:540
  115.0 32.9 %collective-permute-done.28.refs_14_ = f32[2,2,128,128]{3,2,1,0:T(8,128)S(1)} collective-permute-done((f32[2,2,128,128]{3,2,1,0:T(8,128)}, f32[2,2,128,128]{3,2,1,0:T(8,128)S(1)}, u32[]{:S(2)}, u32[]{:S(2)}) %collective-permute-start.28) | collective-permute-done | bytes 262176 | tf_op jit(solution)/shard_map/ppermute | solution.py:540
  149.9 4.1 collective-permute-done.29.refs_15_
  160.8 3.9 collective-permute-done.11.refs_12_
  164.6 6.6 %collective-permute-done.12.refs_13_ = f32[2,2,128,128]{3,2,1,0:T(8,128)S(1)} collective-permute-done((f32[2,2,128,128]{3,2,1,0:T(8,128)S(1)}, f32[2,2,128,128]{3,2,1,0:T(8,128)S(1)}, u32[]{:S(2)}, u32[]{:S(2)}) %collective-permute-start.12) | collective-permute-done | bytes 262176 | tf_op jit(solution)/shard_map/ppermute | solution.py:540
  171.2 4.6 collective-permute-done.13.refs_14_
  175.9 7.4 %collective-permute-done.14.refs_15_ = f32[2,2,128,128]{3,2,1,0:T(8,128)S(1)} collective-permute-done((f32[2,2,128,128]{3,2,1,0:T(8,128)S(1)}, f32[2,2,128,128]{3,2,1,0:T(8,128)S(1)}, u32[]{:S(2)}, u32[]{:S(2)}) %collective-permute-start.14) | collective-permute-done | bytes 262176 | tf_op jit(solution)/shard_map/ppermute | solution.py:540
  183.4 4.7 collective-permute-start.7
  189.1 2.6 collective-permute-start.9
  193.1 32.0 %shard_map.177 = (f32[2,1,128,4096]{3,2,1,0:T(8,128)}, f32[2,8,128]{2,1,0:T(8,128)}, f32[2,1,256,128]{3,2,1,0:T(8,128)}, f32[2,1,256,128]{3,2,1,0:T(8,128)}, f32...) custom-call(f32[2,2,128,128]{3,2,1,0:T(8,128)} %get-tuple-element.91, ...), custom_call_target="tpu_custom_call" | custom-call | flops 20000000000 | bytes 30000000 | tf_op jit(solution)/shard_map/pallas_call | solution.py:409
  229.3 3.3 collective-permute-start.64
  232.6 32.1 %shard_map.178 = (f32[2,1,128,4096]{3,2,1,0:T(8,128)}, f32[2,8,128]{2,1,0:T(8,128)}, f32[2,1,256,128]{3,2,1,0:T(8,128)}, f32[2,1,256,128]{3,2,1,0:T(8,128)}, f32...) custom-call(f32[2,2,128,128]{3,2,1,0:T(8,128)} %get-tuple-element.75, ...), custom_call_target="tpu_custom_call" | custom-call | flops 20000000000 | bytes 30000000 | tf_op jit(solution)/shard_map/pallas_call | solution.py:409
  270.3 9.9 %collective-permute-done.67 = f32[2,8,128]{2,1,0:T(8,128)S(1)} collective-permute-done((f32[2,8,128]{2,1,0:T(8,128)S(1)}, f32[2,8,128]{2,1,0:T(8,128)S(1)}, u32[]{:S(2)}, u32[]{:S(2)}) %collective-permute-start.67) | collective-permute-done | bytes 8224 | tf_op jit(solution)/shard_map/ppermute | solution.py:546
  280.3 3.9 collective-permute-start.62
  284.2 4.3 collective-permute-done.62.edge_other
  291.0 3.3 collective-permute-done.69
  297.2 2.9 collective-permute-start.48
  300.1 2.8 collective-permute-start.49
  306.0 19.4 %shard_map.179 = (f32[2,128,4096]{2,1,0:T(8,128)}, f32[2,2,8,4096]{3,2,1,0:T(8,128)}) custom-call(f32[256,4096]{1,0:T(8,128)} %bitcast.17, f32[136,4096]{1,0:T(8,128)} %collective-permute-done.60.other, f32[8,4096]{1,0:T(8,128)} %copy-done.72, f32[8,4096]{1,0:T(8,128)} %copy-done.73, f32[2,128,4096]{2,1,0:T(8,128)} %dual.1, f32[3,2,4096]{2,1,0:T(2,128)} %copy-done.74, ...), custom_call_target="tpu_custom_call" | custom-call | flops 10000000000 | bytes 30000000 | tf_op jit(solution)/shard_map/pallas_call | solution.py:409
  325.4 2.4 collective-permute-start.53
  327.8 2.4 collective-permute-start.54
  333.2 14.4 %shard_map.180 = (f32[128,4096]{1,0:T(8,128)}, f32[128,4096]{1,0:T(8,128)}) custom-call(f32[2,128,4096]{2,1,0:T(8,128)} %get-tuple-element.74.wave, f32[2,2,8,4096]{3,2,1,0:T(8,128)} %get-tuple-element.141.outside), custom_call_target="tpu_custom_call" | custom-call | flops 10000000000 | bytes 30000000 | tf_op jit(solution)/shard_map/pallas_call | solution.py:409
  347.6 15.0 %collective-permute-done.53.refs_9_ = f32[2,1,256,128]{3,2,1,0:T(8,128)S(1)} collective-permute-done((f32[2,1,256,128]{3,2,1,0:T(8,128)S(1)}, f32[2,1,256,128]{3,2,1,0:T(8,128)S(1)}, u32[]{:S(2)}, u32[]{:S(2)}) %collective-permute-start.53) | collective-permute-done | bytes 262176 | tf_op jit(solution)/shard_map/ppermute | solution.py:540
  363.7 10.1 %collective-permute-done.54.refs_10_ = f32[2,1,256,128]{3,2,1,0:T(8,128)S(1)} collective-permute-done((f32[2,1,256,128]{3,2,1,0:T(8,128)S(1)}, f32[2,1,256,128]{3,2,1,0:T(8,128)S(1)}, u32[]{:S(2)}, u32[]{:S(2)}) %collective-permute-start.54) | collective-permute-done | bytes 262176 | tf_op jit(solution)/shard_map/ppermute | solution.py:540
  375.3 4.1 collective-permute-done.55.refs_11_
  379.9 11.6 %collective-permute-done.56.refs_12_ = f32[2,1,256,128]{3,2,1,0:T(8,128)S(1)} collective-permute-done((f32[2,1,256,128]{3,2,1,0:T(8,128)S(1)}, f32[2,1,256,128]{3,2,1,0:T(8,128)S(1)}, u32[]{:S(2)}, u32[]{:S(2)}) %collective-permute-start.56) | collective-permute-done | bytes 262176 | tf_op jit(solution)/shard_map/ppermute | solution.py:540
  392.8 4.5 collective-permute-done.57.refs_13_
  401.1 2.8 collective-permute-done.58.refs_14_
  404.5 5.0 collective-permute-done.59.refs_15_
  411.7 4.2 broadcast_multiply_fusion
  417.0 2.6 collective-permute-start.36
  419.6 5.0 collective-permute-done.34.refs_5_
  424.6 10.3 %collective-permute-done.35.refs_6_ = f32[2,1,256,128]{3,2,1,0:T(8,128)S(1)} collective-permute-done((f32[2,1,256,128]{3,2,1,0:T(8,128)S(1)}, f32[2,1,256,128]{3,2,1,0:T(8,128)S(1)}, u32[]{:S(2)}, u32[]{:S(2)}) %collective-permute-start.35) | collective-permute-done | bytes 262176 | tf_op jit(solution)/shard_map/ppermute | solution.py:540
  434.9 3.4 collective-permute-start.39
  438.3 3.9 pad_maximum_fusion
  447.0 21.0 %collective-permute-start.42 = (f32[2,1,256,128]{3,2,1,0:T(8,128)S(1)}, f32[2,1,256,128]{3,2,1,0:T(8,128)}, u32[]{:S(2)}, u32[]{:S(2)}) collective-permute-start(f32[2,1,256,128]{3,2,1,0:T(8,128)S(1)} %copy-done.3), channel_id=1, source_target_pairs={{0,26},{2,24},{4,30},{6,28},{8,18},{10,16},{12,22},{14,20},{16,10}... | collective-permute-start | bytes 786440 | tf_op jit(solution)/shard_map/ppermute | solution.py:540
  469.2 14.4 %collective-permute-start.44 = (f32[2,1,256,128]{3,2,1,0:T(8,128)S(1)}, f32[2,1,256,128]{3,2,1,0:T(8,128)}, u32[]{:S(2)}, u32[]{:S(2)}) collective-permute-start(f32[2,1,256,128]{3,2,1,0:T(8,128)S(1)} %copy-done.1), channel_id=1, source_target_pairs={{0,30},{2,28},{4,26},{6,24},{8,22},{10,20},{12,18},{14,16},{16,14}... | collective-permute-start | bytes 786440 | tf_op jit(solution)/shard_map/ppermute | solution.py:540
  483.7 12.1 %shard_map.181.refs_16_ = f32[256,4096]{1,0:T(8,128)} custom-call(f32[2,1,256,128]{3,2,1,0:T(8,128)} %get-tuple-element.124.refs_0_, f32[2,1,256,128]{3,2,1,0:T(8,128)} %copy-done.9, f32[2,1,256,128]{3,2,1,0:T(8,128)} %copy-done.11, f32[2,1,256,128]{3,2,1,0:T(8,128)} %copy-done.13, f32[2,1,256,128]{3,2,1,0:T(8,128)} %copy-done.26, ...), custom_call_target="tpu_custom_call" | custom-call | flops 10000000000 | bytes 30000000 | tf_op jit(solution)/shard_map/pallas_call | solution.py:409
  495.8 12.1 %collective-permute-done.42.refs_13_ = f32[2,1,256,128]{3,2,1,0:T(8,128)} collective-permute-done((f32[2,1,256,128]{3,2,1,0:T(8,128)S(1)}, f32[2,1,256,128]{3,2,1,0:T(8,128)}, u32[]{:S(2)}, u32[]{:S(2)}) %collective-permute-start.42) | collective-permute-done | bytes 262176 | tf_op jit(solution)/shard_map/ppermute | solution.py:540
  509.1 7.5 %collective-permute-done.44.refs_15_ = f32[2,1,256,128]{3,2,1,0:T(8,128)} collective-permute-done((f32[2,1,256,128]{3,2,1,0:T(8,128)S(1)}, f32[2,1,256,128]{3,2,1,0:T(8,128)}, u32[]{:S(2)}, u32[]{:S(2)}) %collective-permute-start.44) | collective-permute-done | bytes 262176 | tf_op jit(solution)/shard_map/ppermute | solution.py:540
  516.6 11.8 %shard_map.182 = f32[256,4096]{1,0:T(8,128)} custom-call(f32[2,1,256,128]{3,2,1,0:T(8,128)} %get-tuple-element.108.refs_0_, f32[2,1,256,128]{3,2,1,0:T(8,128)} %collective-permute-done.30.refs_1_, f32[2,1,256,128]{3,2,1,0:T(8,128)} %collective-permute-done.31.refs_2_, f32[2,1,256,128]{3,2,1,0:T(8,128)} %copy-done.63, f32[2,1,256,128]{3,2,1,0:T(8,128)} %copy-done.65, ...), custom_call_target="tpu_custom_call" | custom-call | flops 10000000000 | bytes 30000000 | tf_op jit(solution)/shard_map/pallas_call | solution.py:409
  (267 shorter events, 71.1 us)
Async XLA Ops:
  35.2 45.2 %collective-permute-start.23 = (f32[2,2,128,128]{3,2,1,0:T(8,128)}, f32[2,2,128,128]{3,2,1,0:T(8,128)S(1)}, u32[]{:S(2)}, u32[]{:S(2)}) collective-permute-start(f32[2,2,128,128]{3,2,1,0:T(8,128)} %get-tuple-element.100), channel_id=1, source_target_pairs={{0,18},{2,16},{4,22},{6,20},{8,26},{10,24},{12,30},{14,28},{16,2},... | collective-permute-start | bytes 786440 | tf_op jit(solution)/shard_map/ppermute | solution.py:540
  35.6 50.4 %collective-permute-start.24 = (f32[2,2,128,128]{3,2,1,0:T(8,128)}, f32[2,2,128,128]{3,2,1,0:T(8,128)S(1)}, u32[]{:S(2)}, u32[]{:S(2)}) collective-permute-start(f32[2,2,128,128]{3,2,1,0:T(8,128)} %get-tuple-element.101), channel_id=1, source_target_pairs={{0,20},{2,22},{4,16},{6,18},{8,28},{10,30},{12,24},{14,26},{16,4},... | collective-permute-start | bytes 786440 | tf_op jit(solution)/shard_map/ppermute | solution.py:540
  38.0 64.9 %collective-permute-start.25 = (f32[2,2,128,128]{3,2,1,0:T(8,128)}, f32[2,2,128,128]{3,2,1,0:T(8,128)}, u32[]{:S(2)}, u32[]{:S(2)}) collective-permute-start(f32[2,2,128,128]{3,2,1,0:T(8,128)} %get-tuple-element.102), channel_id=1, source_target_pairs={{0,22},{2,20},{4,18},{6,16},{8,30},{10,28},{12,26},{14,24},{16,6},... | collective-permute-start | bytes 786440 | tf_op jit(solution)/shard_map/ppermute | solution.py:540
  49.4 59.1 %collective-permute-start.26 = (f32[2,2,128,128]{3,2,1,0:T(8,128)}, f32[2,2,128,128]{3,2,1,0:T(8,128)S(1)}, u32[]{:S(2)}, u32[]{:S(2)}) collective-permute-start(f32[2,2,128,128]{3,2,1,0:T(8,128)} %get-tuple-element.103), channel_id=1, source_target_pairs={{0,24},{2,26},{4,28},{6,30},{8,16},{10,18},{12,20},{14,22},{16,8},... | collective-permute-start | bytes 786440 | tf_op jit(solution)/shard_map/ppermute | solution.py:540
  50.5 64.5 %collective-permute-start.27 = (f32[2,2,128,128]{3,2,1,0:T(8,128)}, f32[2,2,128,128]{3,2,1,0:T(8,128)S(1)}, u32[]{:S(2)}, u32[]{:S(2)}) collective-permute-start(f32[2,2,128,128]{3,2,1,0:T(8,128)} %get-tuple-element.104), channel_id=1, source_target_pairs={{0,26},{2,24},{4,30},{6,28},{8,18},{10,16},{12,22},{14,20},{16,10}... | collective-permute-start | bytes 786440 | tf_op jit(solution)/shard_map/ppermute | solution.py:540
  80.4 67.5 %collective-permute-start.28 = (f32[2,2,128,128]{3,2,1,0:T(8,128)}, f32[2,2,128,128]{3,2,1,0:T(8,128)S(1)}, u32[]{:S(2)}, u32[]{:S(2)}) collective-permute-start(f32[2,2,128,128]{3,2,1,0:T(8,128)} %get-tuple-element.105), channel_id=1, source_target_pairs={{0,28},{2,30},{4,24},{6,26},{8,20},{10,22},{12,16},{14,18},{16,12}... | collective-permute-start | bytes 786440 | tf_op jit(solution)/shard_map/ppermute | solution.py:540
  86.0 68.0 %collective-permute-start.29 = (f32[2,2,128,128]{3,2,1,0:T(8,128)}, f32[2,2,128,128]{3,2,1,0:T(8,128)S(1)}, u32[]{:S(2)}, u32[]{:S(2)}) collective-permute-start(f32[2,2,128,128]{3,2,1,0:T(8,128)} %get-tuple-element.106), channel_id=1, source_target_pairs={{0,30},{2,28},{4,26},{6,24},{8,22},{10,20},{12,18},{14,16},{16,14}... | collective-permute-start | bytes 786440 | tf_op jit(solution)/shard_map/ppermute | solution.py:540
  102.9 52.9 %collective-permute-start = (f32[2,2,128,128]{3,2,1,0:T(8,128)}, f32[2,2,128,128]{3,2,1,0:T(8,128)S(1)}, u32[]{:S(2)}, u32[]{:S(2)}) collective-permute-start(f32[2,2,128,128]{3,2,1,0:T(8,128)} %get-tuple-element.76), channel_id=1, source_target_pairs={{0,2},{2,0},{4,6},{6,4},{8,10},{10,8},{12,14},{14,12},{16,18},{18,... | collective-permute-start | bytes 786440 | tf_op jit(solution)/shard_map/ppermute | solution.py:540
  108.5 49.1 %collective-permute-start.1 = (f32[2,2,128,128]{3,2,1,0:T(8,128)S(1)}, f32[2,2,128,128]{3,2,1,0:T(8,128)S(1)}, u32[]{:S(2)}, u32[]{:S(2)}) collective-permute-start(f32[2,2,128,128]{3,2,1,0:T(8,128)S(1)} %copy-done.58), channel_id=1, source_target_pairs={{0,4},{2,6},{4,0},{6,2},{8,12},{10,14},{12,8},{14,10},{16,20},{18,... | collective-permute-start | bytes 786440 | tf_op jit(solution)/shard_map/ppermute | solution.py:540
  115.0 44.6 %collective-permute-start.10 = (f32[2,2,128,128]{3,2,1,0:T(8,128)S(1)}, f32[2,2,128,128]{3,2,1,0:T(8,128)S(1)}, u32[]{:S(2)}, u32[]{:S(2)}) collective-permute-start(f32[2,2,128,128]{3,2,1,0:T(8,128)S(1)} %copy-done.55), channel_id=1, source_target_pairs={{0,22},{2,20},{4,18},{6,16},{8,30},{10,28},{12,26},{14,24},{16,6},... | collective-permute-start | bytes 786440 | tf_op jit(solution)/shard_map/ppermute | solution.py:540
  157.6 25.7 %collective-permute-start.14 = (f32[2,2,128,128]{3,2,1,0:T(8,128)S(1)}, f32[2,2,128,128]{3,2,1,0:T(8,128)S(1)}, u32[]{:S(2)}, u32[]{:S(2)}) collective-permute-start(f32[2,2,128,128]{3,2,1,0:T(8,128)S(1)} %copy-done.43), channel_id=1, source_target_pairs={{0,30},{2,28},{4,26},{6,24},{8,22},{10,20},{12,18},{14,16},{16,14}... | collective-permute-start | bytes 786440 | tf_op jit(solution)/shard_map/ppermute | solution.py:540
  159.6 23.7 %collective-permute-start.2 = (f32[2,2,128,128]{3,2,1,0:T(8,128)S(1)}, f32[2,2,128,128]{3,2,1,0:T(8,128)S(1)}, u32[]{:S(2)}, u32[]{:S(2)}) collective-permute-start(f32[2,2,128,128]{3,2,1,0:T(8,128)S(1)} %copy-done.40), channel_id=1, source_target_pairs={{0,6},{2,4},{4,2},{6,0},{8,14},{10,12},{12,10},{14,8},{16,22},{18,... | collective-permute-start | bytes 786440 | tf_op jit(solution)/shard_map/ppermute | solution.py:540
  164.6 23.4 %collective-permute-start.3 = (f32[2,2,128,128]{3,2,1,0:T(8,128)S(1)}, f32[2,2,128,128]{3,2,1,0:T(8,128)S(1)}, u32[]{:S(2)}, u32[]{:S(2)}) collective-permute-start(f32[2,2,128,128]{3,2,1,0:T(8,128)S(1)} %copy-done.37), channel_id=1, source_target_pairs={{0,8},{2,10},{4,12},{6,14},{8,0},{10,2},{12,4},{14,6},{16,24},{18,... | collective-permute-start | bytes 786440 | tf_op jit(solution)/shard_map/ppermute | solution.py:540
  183.3 41.8 %collective-permute-start.6 = (f32[2,2,128,128]{3,2,1,0:T(8,128)}, f32[2,2,128,128]{3,2,1,0:T(8,128)}, u32[]{:S(2)}, u32[]{:S(2)}) collective-permute-start(f32[2,2,128,128]{3,2,1,0:T(8,128)} %get-tuple-element.82), channel_id=1, source_target_pairs={{0,14},{2,12},{4,10},{6,8},{8,6},{10,4},{12,2},{14,0},{16,30},{18,... | collective-permute-start | bytes 786440 | tf_op jit(solution)/shard_map/ppermute | solution.py:540
  183.4 43.7 %collective-permute-start.7 = (f32[2,2,128,128]{3,2,1,0:T(8,128)}, f32[2,2,128,128]{3,2,1,0:T(8,128)}, u32[]{:S(2)}, u32[]{:S(2)}) collective-permute-start(f32[2,2,128,128]{3,2,1,0:T(8,128)} %get-tuple-element.83), channel_id=1, source_target_pairs={{0,16},{2,18},{4,20},{6,22},{8,24},{10,26},{12,28},{14,30},{16,0},... | collective-permute-start | bytes 786440 | tf_op jit(solution)/shard_map/ppermute | solution.py:540
  188.1 41.2 %collective-permute-start.8 = (f32[2,2,128,128]{3,2,1,0:T(8,128)S(1)}, f32[2,2,128,128]{3,2,1,0:T(8,128)}, u32[]{:S(2)}, u32[]{:S(2)}) collective-permute-start(f32[2,2,128,128]{3,2,1,0:T(8,128)S(1)} %copy-done.20), channel_id=1, source_target_pairs={{0,18},{2,16},{4,22},{6,20},{8,26},{10,24},{12,30},{14,28},{16,2},... | collective-permute-start | bytes 786440 | tf_op jit(solution)/shard_map/ppermute | solution.py:540
  189.1 43.5 %collective-permute-start.9 = (f32[2,2,128,128]{3,2,1,0:T(8,128)S(1)}, f32[2,2,128,128]{3,2,1,0:T(8,128)}, u32[]{:S(2)}, u32[]{:S(2)}) collective-permute-start(f32[2,2,128,128]{3,2,1,0:T(8,128)S(1)} %copy-done.17), channel_id=1, source_target_pairs={{0,20},{2,22},{4,16},{6,18},{8,28},{10,30},{12,24},{14,26},{16,4},... | collective-permute-start | bytes 786440 | tf_op jit(solution)/shard_map/ppermute | solution.py:540
  191.7 114.1 %collective-permute-start.60 = (f32[136,4096]{1,0:T(8,128)S(1)}, f32[136,4096]{1,0:T(8,128)}, u32[]{:S(2)}, u32[]{:S(2)}) collective-permute-start(f32[136,4096]{1,0:T(8,128)S(1)} %dynamic-slice_bitcast_fusion), channel_id=1, source_target_pairs={{0,1},{1,0},{2,3},{3,2},{4,5},{5,4},{6,7},{7,6},{8,9},{9,8},{10,11... | collective-permute-start | bytes 6684680 | tf_op jit(solution)/shard_map/ppermute | solution.py:519
  225.1 44.6 %collective-permute-start.61 = (f32[8,4096]{1,0:T(8,128)S(1)}, f32[8,4096]{1,0:T(8,128)S(1)}, u32[]{:S(2)}, u32[]{:S(2)}) collective-permute-start(f32[8,4096]{1,0:T(8,128)S(1)} %get-tuple-element.152), channel_id=1, source_target_pairs={{0,2},{2,4},{4,6},{6,8},{8,10},{10,12},{12,14},{14,16},{16,18},{18... | collective-permute-start | bytes 393224 | tf_op jit(solution)/shard_map/ppermute | solution.py:564
  227.1 39.8 %collective-permute-start.63 = (f32[3,2,4096]{2,1,0:T(2,128)S(1)}, f32[3,2,4096]{2,1,0:T(2,128)S(1)}, u32[]{:S(2)}, u32[]{:S(2)}) collective-permute-start(f32[3,2,4096]{2,1,0:T(2,128)S(1)} %pad_maximum_fusion.1), channel_id=1, source_target_pairs={{0,1},{1,2},{2,3},{3,4},{4,5},{5,6},{6,7},{7,8},{8,9},{9,10},{10,1... | collective-permute-start | bytes 294920 | tf_op jit(solution)/shard_map/ppermute | solution.py:574
  229.3 37.7 %collective-permute-start.64 = (f32[3,2,4096]{2,1,0:T(2,128)S(1)}, f32[3,2,4096]{2,1,0:T(2,128)S(1)}, u32[]{:S(2)}, u32[]{:S(2)}) collective-permute-start(f32[3,2,4096]{2,1,0:T(2,128)S(1)} %pad_maximum_fusion.2), channel_id=1, source_target_pairs={{1,0},{2,1},{3,2},{4,3},{5,4},{6,5},{7,6},{8,7},{9,8},{10,9},{11,1... | collective-permute-start | bytes 294920 | tf_op jit(solution)/shard_map/ppermute | solution.py:574
  266.9 33.2 %collective-permute-start.45 = (f32[2,1,256,128]{3,2,1,0:T(8,128)}, f32[2,1,256,128]{3,2,1,0:T(8,128)S(1)}, u32[]{:S(2)}, u32[]{:S(2)}) collective-permute-start(f32[2,1,256,128]{3,2,1,0:T(8,128)} %get-tuple-element.125), channel_id=1, source_target_pairs={{0,2},{2,0},{4,6},{6,4},{8,10},{10,8},{12,14},{14,12},{16,18},{18,... | collective-permute-start | bytes 786440 | tf_op jit(solution)/shard_map/ppermute | solution.py:540
  267.0 35.9 %collective-permute-start.46 = (f32[2,1,256,128]{3,2,1,0:T(8,128)}, f32[2,1,256,128]{3,2,1,0:T(8,128)S(1)}, u32[]{:S(2)}, u32[]{:S(2)}) collective-permute-start(f32[2,1,256,128]{3,2,1,0:T(8,128)} %get-tuple-element.126), channel_id=1, source_target_pairs={{0,4},{2,6},{4,0},{6,2},{8,12},{10,14},{12,8},{14,10},{16,20},{18,... | collective-permute-start | bytes 786440 | tf_op jit(solution)/shard_map/ppermute | solution.py:540
  267.9 36.7 %collective-permute-start.47 = (f32[2,1,256,128]{3,2,1,0:T(8,128)}, f32[2,1,256,128]{3,2,1,0:T(8,128)S(1)}, u32[]{:S(2)}, u32[]{:S(2)}) collective-permute-start(f32[2,1,256,128]{3,2,1,0:T(8,128)} %get-tuple-element.127), channel_id=1, source_target_pairs={{0,6},{2,4},{4,2},{6,0},{8,14},{10,12},{12,10},{14,8},{16,22},{18,... | collective-permute-start | bytes 786440 | tf_op jit(solution)/shard_map/ppermute | solution.py:540
  297.2 28.2 %collective-permute-start.48 = (f32[2,1,256,128]{3,2,1,0:T(8,128)}, f32[2,1,256,128]{3,2,1,0:T(8,128)S(1)}, u32[]{:S(2)}, u32[]{:S(2)}) collective-permute-start(f32[2,1,256,128]{3,2,1,0:T(8,128)} %get-tuple-element.128), channel_id=1, source_target_pairs={{0,8},{2,10},{4,12},{6,14},{8,0},{10,2},{12,4},{14,6},{16,24},{18,... | collective-permute-start | bytes 786440 | tf_op jit(solution)/shard_map/ppermute | solution.py:540
  300.1 27.7 %collective-permute-start.49 = (f32[2,1,256,128]{3,2,1,0:T(8,128)}, f32[2,1,256,128]{3,2,1,0:T(8,128)}, u32[]{:S(2)}, u32[]{:S(2)}) collective-permute-start(f32[2,1,256,128]{3,2,1,0:T(8,128)} %get-tuple-element.129), channel_id=1, source_target_pairs={{0,10},{2,8},{4,14},{6,12},{8,2},{10,0},{12,6},{14,4},{16,26},{18,... | collective-permute-start | bytes 786440 | tf_op jit(solution)/shard_map/ppermute | solution.py:540
  302.9 27.3 %collective-permute-start.50 = (f32[2,1,256,128]{3,2,1,0:T(8,128)}, f32[2,1,256,128]{3,2,1,0:T(8,128)}, u32[]{:S(2)}, u32[]{:S(2)}) collective-permute-start(f32[2,1,256,128]{3,2,1,0:T(8,128)} %get-tuple-element.130), channel_id=1, source_target_pairs={{0,12},{2,14},{4,8},{6,10},{8,4},{10,6},{12,0},{14,2},{16,28},{18,... | collective-permute-start | bytes 786440 | tf_op jit(solution)/shard_map/ppermute | solution.py:540
  304.7 26.9 %collective-permute-start.51 = (f32[2,1,256,128]{3,2,1,0:T(8,128)}, f32[2,1,256,128]{3,2,1,0:T(8,128)}, u32[]{:S(2)}, u32[]{:S(2)}) collective-permute-start(f32[2,1,256,128]{3,2,1,0:T(8,128)} %get-tuple-element.131), channel_id=1, source_target_pairs={{0,14},{2,12},{4,10},{6,8},{8,6},{10,4},{12,2},{14,0},{16,30},{18,... | collective-permute-start | bytes 786440 | tf_op jit(solution)/shard_map/ppermute | solution.py:540
  305.9 26.0 %collective-permute-start.52 = (f32[2,1,256,128]{3,2,1,0:T(8,128)}, f32[2,1,256,128]{3,2,1,0:T(8,128)S(1)}, u32[]{:S(2)}, u32[]{:S(2)}) collective-permute-start(f32[2,1,256,128]{3,2,1,0:T(8,128)} %get-tuple-element.132), channel_id=1, source_target_pairs={{0,16},{2,18},{4,20},{6,22},{8,24},{10,26},{12,28},{14,30},{16,0},... | collective-permute-start | bytes 786440 | tf_op jit(solution)/shard_map/ppermute | solution.py:540
  325.4 37.2 %collective-permute-start.53 = (f32[2,1,256,128]{3,2,1,0:T(8,128)S(1)}, f32[2,1,256,128]{3,2,1,0:T(8,128)S(1)}, u32[]{:S(2)}, u32[]{:S(2)}) collective-permute-start(f32[2,1,256,128]{3,2,1,0:T(8,128)S(1)} %copy-done.30), channel_id=1, source_target_pairs={{0,18},{2,16},{4,22},{6,20},{8,26},{10,24},{12,30},{14,28},{16,2},... | collective-permute-start | bytes 786440 | tf_op jit(solution)/shard_map/ppermute | solution.py:540
  327.8 46.1 %collective-permute-start.54 = (f32[2,1,256,128]{3,2,1,0:T(8,128)S(1)}, f32[2,1,256,128]{3,2,1,0:T(8,128)S(1)}, u32[]{:S(2)}, u32[]{:S(2)}) collective-permute-start(f32[2,1,256,128]{3,2,1,0:T(8,128)S(1)} %copy-done.28), channel_id=1, source_target_pairs={{0,20},{2,22},{4,16},{6,18},{8,28},{10,30},{12,24},{14,26},{16,4},... | collective-permute-start | bytes 786440 | tf_op jit(solution)/shard_map/ppermute | solution.py:540
  330.2 49.2 %collective-permute-start.55 = (f32[2,1,256,128]{3,2,1,0:T(8,128)S(1)}, f32[2,1,256,128]{3,2,1,0:T(8,128)S(1)}, u32[]{:S(2)}, u32[]{:S(2)}) collective-permute-start(f32[2,1,256,128]{3,2,1,0:T(8,128)S(1)} %copy-done.27), channel_id=1, source_target_pairs={{0,22},{2,20},{4,18},{6,16},{8,30},{10,28},{12,26},{14,24},{16,6},... | collective-permute-start | bytes 786440 | tf_op jit(solution)/shard_map/ppermute | solution.py:540
  331.6 60.0 %collective-permute-start.56 = (f32[2,1,256,128]{3,2,1,0:T(8,128)S(1)}, f32[2,1,256,128]{3,2,1,0:T(8,128)S(1)}, u32[]{:S(2)}, u32[]{:S(2)}) collective-permute-start(f32[2,1,256,128]{3,2,1,0:T(8,128)S(1)} %copy-done.25), channel_id=1, source_target_pairs={{0,24},{2,26},{4,28},{6,30},{8,16},{10,18},{12,20},{14,22},{16,8},... | collective-permute-start | bytes 786440 | tf_op jit(solution)/shard_map/ppermute | solution.py:540
  331.9 65.5 %collective-permute-start.57 = (f32[2,1,256,128]{3,2,1,0:T(8,128)S(1)}, f32[2,1,256,128]{3,2,1,0:T(8,128)}, u32[]{:S(2)}, u32[]{:S(2)}) collective-permute-start(f32[2,1,256,128]{3,2,1,0:T(8,128)S(1)} %copy-done.24), channel_id=1, source_target_pairs={{0,26},{2,24},{4,30},{6,28},{8,18},{10,16},{12,22},{14,20},{16,10}... | collective-permute-start | bytes 786440 | tf_op jit(solution)/shard_map/ppermute | solution.py:540
  362.6 41.3 %collective-permute-start.58 = (f32[2,1,256,128]{3,2,1,0:T(8,128)S(1)}, f32[2,1,256,128]{3,2,1,0:T(8,128)}, u32[]{:S(2)}, u32[]{:S(2)}) collective-permute-start(f32[2,1,256,128]{3,2,1,0:T(8,128)S(1)} %copy-done.15), channel_id=1, source_target_pairs={{0,28},{2,30},{4,24},{6,26},{8,20},{10,22},{12,16},{14,18},{16,12}... | collective-permute-start | bytes 786440 | tf_op jit(solution)/shard_map/ppermute | solution.py:540
  373.8 35.7 %collective-permute-start.59 = (f32[2,1,256,128]{3,2,1,0:T(8,128)S(1)}, f32[2,1,256,128]{3,2,1,0:T(8,128)}, u32[]{:S(2)}, u32[]{:S(2)}) collective-permute-start(f32[2,1,256,128]{3,2,1,0:T(8,128)S(1)} %copy-done.12), channel_id=1, source_target_pairs={{0,30},{2,28},{4,26},{6,24},{8,22},{10,20},{12,18},{14,16},{16,14}... | collective-permute-start | bytes 786440 | tf_op jit(solution)/shard_map/ppermute | solution.py:540
  379.4 30.1 %collective-permute-start.30 = (f32[2,1,256,128]{3,2,1,0:T(8,128)}, f32[2,1,256,128]{3,2,1,0:T(8,128)}, u32[]{:S(2)}, u32[]{:S(2)}) collective-permute-start(f32[2,1,256,128]{3,2,1,0:T(8,128)} %get-tuple-element.109), channel_id=1, source_target_pairs={{0,2},{2,0},{4,6},{6,4},{8,10},{10,8},{12,14},{14,12},{16,18},{18,... | collective-permute-start | bytes 786440 | tf_op jit(solution)/shard_map/ppermute | solution.py:540
  397.3 71.9 %collective-permute-start.65 = (f32[128,4096]{1,0:T(8,128)}, f32[128,4096]{1,0:T(8,128)S(1)}, u32[]{:S(2)}, u32[]{:S(2)}) collective-permute-start(f32[128,4096]{1,0:T(8,128)} %get-tuple-element.143), channel_id=1, source_target_pairs={{0,1},{1,0},{2,3},{3,2},{4,5},{5,4},{6,7},{7,6},{8,9},{9,8},{10,11... | collective-permute-start | bytes 6291464 | tf_op jit(solution)/shard_map/ppermute | solution.py:519
  411.6 23.3 %collective-permute-start.35 = (f32[2,1,256,128]{3,2,1,0:T(8,128)S(1)}, f32[2,1,256,128]{3,2,1,0:T(8,128)S(1)}, u32[]{:S(2)}, u32[]{:S(2)}) collective-permute-start(f32[2,1,256,128]{3,2,1,0:T(8,128)S(1)} %copy-done.14), channel_id=1, source_target_pairs={{0,12},{2,14},{4,8},{6,10},{8,4},{10,6},{12,0},{14,2},{16,28},{18,... | collective-permute-start | bytes 786440 | tf_op jit(solution)/shard_map/ppermute | solution.py:540
  417.0 25.3 %collective-permute-start.36 = (f32[2,1,256,128]{3,2,1,0:T(8,128)S(1)}, f32[2,1,256,128]{3,2,1,0:T(8,128)S(1)}, u32[]{:S(2)}, u32[]{:S(2)}) collective-permute-start(f32[2,1,256,128]{3,2,1,0:T(8,128)S(1)} %copy-done.10), channel_id=1, source_target_pairs={{0,14},{2,12},{4,10},{6,8},{8,6},{10,4},{12,2},{14,0},{16,30},{18,... | collective-permute-start | bytes 786440 | tf_op jit(solution)/shard_map/ppermute | solution.py:540
  419.6 25.0 %collective-permute-start.37 = (f32[2,1,256,128]{3,2,1,0:T(8,128)S(1)}, f32[2,1,256,128]{3,2,1,0:T(8,128)S(1)}, u32[]{:S(2)}, u32[]{:S(2)}) collective-permute-start(f32[2,1,256,128]{3,2,1,0:T(8,128)S(1)} %copy-done.8), channel_id=1, source_target_pairs={{0,16},{2,18},{4,20},{6,22},{8,24},{10,26},{12,28},{14,30},{16,0},... | collective-permute-start | bytes 786440 | tf_op jit(solution)/shard_map/ppermute | solution.py:540
  424.6 22.4 %collective-permute-start.38 = (f32[2,1,256,128]{3,2,1,0:T(8,128)S(1)}, f32[2,1,256,128]{3,2,1,0:T(8,128)S(1)}, u32[]{:S(2)}, u32[]{:S(2)}) collective-permute-start(f32[2,1,256,128]{3,2,1,0:T(8,128)S(1)} %copy-done.7), channel_id=1, source_target_pairs={{0,18},{2,16},{4,22},{6,20},{8,26},{10,24},{12,30},{14,28},{16,2},... | collective-permute-start | bytes 786440 | tf_op jit(solution)/shard_map/ppermute | solution.py:540
  434.9 33.1 %collective-permute-start.39 = (f32[2,1,256,128]{3,2,1,0:T(8,128)S(1)}, f32[2,1,256,128]{3,2,1,0:T(8,128)}, u32[]{:S(2)}, u32[]{:S(2)}) collective-permute-start(f32[2,1,256,128]{3,2,1,0:T(8,128)S(1)} %copy-done.6), channel_id=1, source_target_pairs={{0,20},{2,22},{4,16},{6,18},{8,28},{10,30},{12,24},{14,26},{16,4},... | collective-permute-start | bytes 786440 | tf_op jit(solution)/shard_map/ppermute | solution.py:540
  442.3 53.5 %collective-permute-start.40 = (f32[2,1,256,128]{3,2,1,0:T(8,128)S(1)}, f32[2,1,256,128]{3,2,1,0:T(8,128)}, u32[]{:S(2)}, u32[]{:S(2)}) collective-permute-start(f32[2,1,256,128]{3,2,1,0:T(8,128)S(1)} %copy-done.5), channel_id=1, source_target_pairs={{0,22},{2,20},{4,18},{6,16},{8,30},{10,28},{12,26},{14,24},{16,6},... | collective-permute-start | bytes 786440 | tf_op jit(solution)/shard_map/ppermute | solution.py:540
  444.5 51.3 %collective-permute-start.41 = (f32[2,1,256,128]{3,2,1,0:T(8,128)S(1)}, f32[2,1,256,128]{3,2,1,0:T(8,128)}, u32[]{:S(2)}, u32[]{:S(2)}) collective-permute-start(f32[2,1,256,128]{3,2,1,0:T(8,128)S(1)} %copy-done.4), channel_id=1, source_target_pairs={{0,24},{2,26},{4,28},{6,30},{8,16},{10,18},{12,20},{14,22},{16,8},... | collective-permute-start | bytes 786440 | tf_op jit(solution)/shard_map/ppermute | solution.py:540
  447.0 60.9 %collective-permute-start.42 = (f32[2,1,256,128]{3,2,1,0:T(8,128)S(1)}, f32[2,1,256,128]{3,2,1,0:T(8,128)}, u32[]{:S(2)}, u32[]{:S(2)}) collective-permute-start(f32[2,1,256,128]{3,2,1,0:T(8,128)S(1)} %copy-done.3), channel_id=1, source_target_pairs={{0,26},{2,24},{4,30},{6,28},{8,18},{10,16},{12,22},{14,20},{16,10}... | collective-permute-start | bytes 786440 | tf_op jit(solution)/shard_map/ppermute | solution.py:540
  468.0 41.1 %collective-permute-start.43 = (f32[2,1,256,128]{3,2,1,0:T(8,128)S(1)}, f32[2,1,256,128]{3,2,1,0:T(8,128)}, u32[]{:S(2)}, u32[]{:S(2)}) collective-permute-start(f32[2,1,256,128]{3,2,1,0:T(8,128)S(1)} %copy-done.2), channel_id=1, source_target_pairs={{0,28},{2,30},{4,24},{6,26},{8,20},{10,22},{12,16},{14,18},{16,12}... | collective-permute-start | bytes 786440 | tf_op jit(solution)/shard_map/ppermute | solution.py:540
  469.2 47.4 %collective-permute-start.44 = (f32[2,1,256,128]{3,2,1,0:T(8,128)S(1)}, f32[2,1,256,128]{3,2,1,0:T(8,128)}, u32[]{:S(2)}, u32[]{:S(2)}) collective-permute-start(f32[2,1,256,128]{3,2,1,0:T(8,128)S(1)} %copy-done.1), channel_id=1, source_target_pairs={{0,30},{2,28},{4,26},{6,24},{8,22},{10,20},{12,18},{14,16},{16,14}... | collective-permute-start | bytes 786440 | tf_op jit(solution)/shard_map/ppermute | solution.py:540
  (99 other events, 3804.2 us)
